TPU v7x, 256 devices: a whole 4x4x8 slice. The times are simulated.
256 devices in a mesh: ctx: 32 (over y, z), tp: 8 (over x, core).
Axes of the slice: x: 4, y: 4, z: 8, core: 2. Of those that a mesh axis runs over, the one named last changes fastest.
Arguments:
- queries: bfloat16 [8192, 8192], P('ctx', 'tp'), may hold values from -24 to 24
- keys: bfloat16 [8192, 1024], P('ctx', 'tp'), may hold values from -24 to 24
- values: bfloat16 [8192, 1024], P('ctx', 'tp'), may hold values from -6 to 6
- vertical: int32 [64, 8], P('tp'), may hold values from 0 to 127
- slash: int32 [64, 8], P('tp'), may hold values from 1 to 63
- block_position: int32 [128], replicated, may hold values from 0 to 127, as said below
- ssm_input: bfloat16 [8192, 16384], P('ctx', 'tp'), may hold values from -6 to 6
- gate: bfloat16 [8192, 16384], P('ctx', 'tp'), may hold values from -20 to 20
- state_in: bfloat16 [8192, 16], P('ctx'), may hold values from -6 to 6
- state_out: bfloat16 [8192, 16], P('ctx'), may hold values from -6 to 6
- step_size: float32 [8192, 256], P('ctx', 'tp'), may hold values from 0 to 10, as said below
- decay_log: float32 [256], P('tp'), may hold values from -3.2 to -2.5
- skip_gain: float32 [256], P('tp'), may hold values from 0.5 to 2
- norm_gain: float32 [16384], P('tp'), may hold values from 0.1 to 1.9
Outputs:
- attention_out: bfloat16 [8192, 8192], P('ctx', 'tp')
- recurrent_mixer_result: bfloat16 [8192, 16384], P('ctx', 'tp')
Inputs may be any that keep to these rules, and one draw needn't show every extreme that they name: `vertical`: block indices of the sequence; a head may name a block twice. `block_position`: a permutation of the sequence's blocks; the m-th block stored on each index of ctx lies in the m-th group of as many consecutive blocks as ctx has devices. `step_size`: positive.
All inputs are finite; a program needn't handle non-finite values.
Results may differ from a plain program's by a relative error of at most 0.0054.
Values may be sent and summed in bfloat16 or wider, within the bound.
A program may use at most 128 MiB of HBM per device.

v0:
```python
import math

import jax
import jax.numpy as jnp
from jax import lax
from jax.sharding import PartitionSpec as P

HEAD_DIM = 128
SSM_HEAD_DIM = 64
D_STATE = 16
BLOCK = 64
INNER = 16384


NEG_FILL = -1e30


def passed_along(value, axis, steps):
    count = lax.axis_size(axis)
    pairs = [(source, (source + steps) % count) for source in range(count)]
    return lax.ppermute(value, axis, pairs)


def shifted(array, axis, by):
    size = lax.axis_size(axis)
    pairs = [(i, i + by) for i in range(size) if 0 <= i + by < size]
    return lax.ppermute(array, axis, pairs)


def positions_of_tokens(block_pos):
    offsets = jnp.arange(BLOCK, dtype=jnp.int32)
    return (block_pos[:, None] * BLOCK + offsets[None, :]).reshape(-1)


def allowed_blocks(query_pos, key_pos, vertical_local, slash_local):
    in_vertical = jnp.any(key_pos[None, None, :, None] == vertical_local[:, :, None, :], axis=-1)
    offset = query_pos[:, None] - key_pos[None, :]
    on_slash = jnp.any(offset[None, None, :, :, None] == slash_local[:, :, None, None, :], axis=-1)
    return in_vertical[:, :, None, :] | on_slash | (offset == 0)[None, None, :, :]


def flash_update(running, scores, allowed, value_rows):
    top_score, denom_sum, weighted_sum = running
    masked = jnp.where(allowed, scores, NEG_FILL)
    new_top = jnp.maximum(top_score, jnp.max(masked, axis=-1))
    expo = jnp.where(allowed, jnp.exp(masked - new_top[..., None]), 0.0)
    factor = jnp.exp(top_score - new_top)
    denom_sum = denom_sum * factor + jnp.sum(expo, axis=-1)
    contrib = jnp.einsum(
        "kgts,skd->kgtd", expo.astype(jnp.bfloat16), value_rows, preferred_element_type=jnp.float32
    )
    return (new_top, denom_sum, weighted_sum * factor[..., None] + contrib)


def attend_visiting(queries, keys, values, vertical, slash, block_position):
    row_count = queries.shape[0]
    q_heads = queries.shape[1] // HEAD_DIM
    kv_heads = keys.shape[1] // HEAD_DIM
    group_size = q_heads // kv_heads
    blocks_here = row_count // BLOCK
    cycle_size = lax.axis_size("ctx")
    my_index = lax.axis_index("ctx")
    score_scale = 1.0 / math.sqrt(HEAD_DIM)
    query_rows = queries.reshape(row_count, kv_heads, group_size, HEAD_DIM)
    vertical_local = vertical.reshape(kv_heads, group_size, vertical.shape[1])
    slash_local = slash.reshape(kv_heads, group_size, slash.shape[1])
    query_pos = lax.dynamic_slice_in_dim(block_position, my_index * blocks_here, blocks_here)
    query_tok = positions_of_tokens(query_pos)

    def visit_keys(running, key_values, source):
        key_pos = lax.dynamic_slice_in_dim(block_position, source * blocks_here, blocks_here)
        key_tok = positions_of_tokens(key_pos)
        block_ok = allowed_blocks(query_pos, key_pos, vertical_local, slash_local)
        causal = (key_tok[None, :] <= query_tok[:, None])[None, None]
        allowed = jnp.repeat(jnp.repeat(block_ok, BLOCK, axis=2), BLOCK, axis=3) & causal
        key_rows = key_values[0].reshape(row_count, kv_heads, HEAD_DIM)
        value_rows = key_values[1].reshape(row_count, kv_heads, HEAD_DIM)
        scores = (
            jnp.einsum("tkgd,skd->kgts", query_rows, key_rows, preferred_element_type=jnp.float32)
            * score_scale
        )
        return flash_update(running, scores, allowed, value_rows)

    initial = (
        jnp.full((kv_heads, group_size, row_count), NEG_FILL, jnp.float32),
        jnp.zeros((kv_heads, group_size, row_count), jnp.float32),
        jnp.zeros((kv_heads, group_size, row_count, HEAD_DIM), jnp.float32),
    )

    def cycle_turn(turn_index, carry):
        running, key_values = carry
        source = (my_index - turn_index) % cycle_size
        running = visit_keys(running, key_values, source)
        key_values = passed_along(key_values, "ctx", 1)
        return (running, key_values)

    running, key_values = lax.fori_loop(
        0, cycle_size - 1, cycle_turn, (initial, jnp.stack((keys, values)))
    )
    running = visit_keys(running, key_values, (my_index - cycle_size + 1) % cycle_size)
    _, denom_sum, weighted_sum = running
    result = weighted_sum / denom_sum[..., None]
    return (
        jnp.transpose(result, (2, 0, 1, 3))
        .reshape(row_count, q_heads * HEAD_DIM)
        .astype(jnp.bfloat16)
    )


def mamba_mix(ssm_input, gate, state_in, state_out, step_size, decay_log, skip_gain, norm_gain):
    careful = lax.Precision.HIGH
    row_count = ssm_input.shape[0]
    head_count = step_size.shape[1]
    inner_width = ssm_input.shape[1]
    inputs = ssm_input.astype(jnp.float32).reshape(row_count, head_count, SSM_HEAD_DIM)
    in_map = state_in.astype(jnp.float32)
    out_map = state_out.astype(jnp.float32)
    log_steps = -jnp.exp(decay_log)[None, :] * step_size
    cumulative = jnp.cumsum(log_steps, axis=0)
    grouped_per_head = cumulative.T
    lower = jnp.arange(row_count)[:, None] >= jnp.arange(row_count)[None, :]
    decay = jnp.where(
        lower[None],
        jnp.exp(jnp.minimum(grouped_per_head[:, :, None] - grouped_per_head[:, None, :], 0.0)),
        0.0,
    )
    inner = jnp.dot(state_out, state_in.T, preferred_element_type=jnp.float32)
    weighted = inputs * step_size[:, :, None]
    within = jnp.einsum("hts,shp->thp", decay * inner[None], weighted, precision=careful)
    tail = jnp.exp(cumulative[-1][None, :] - cumulative)
    local_state = jnp.einsum(
        "sn,shp->nhp", in_map, weighted * tail[:, :, None], precision=careful
    ).reshape(D_STATE, inner_width)
    carry_decay = jnp.repeat(jnp.exp(cumulative[-1]), SSM_HEAD_DIM)[None, :]

    def hand_over(turn_index, incoming):
        return shifted(carry_decay * incoming + local_state, "ctx", 1)

    incoming = lax.fori_loop(0, lax.axis_size("ctx") - 1, hand_over, jnp.zeros_like(local_state))
    from_past = jnp.dot(
        out_map, incoming, precision=careful, preferred_element_type=jnp.float32
    ).reshape(row_count, head_count, SSM_HEAD_DIM)
    from_past = from_past * jnp.exp(cumulative)[:, :, None]
    mixed = (within + from_past + skip_gain[None, :, None] * inputs).reshape(row_count, inner_width)
    gate_full = gate.astype(jnp.float32)
    gated = mixed * gate_full * jax.nn.sigmoid(gate_full)
    squares = lax.psum(jnp.sum(gated * gated, axis=1), "tp")
    scaled = gated * lax.rsqrt(squares / INNER + 1e-05)[:, None] * norm_gain[None, :]
    return scaled.astype(jnp.bfloat16)


def local(
    queries,
    keys,
    values,
    vertical,
    slash,
    block_position,
    ssm_input,
    gate,
    state_in,
    state_out,
    step_size,
    decay_log,
    skip_gain,
    norm_gain,
):
    attention_out = attend_visiting(queries, keys, values, vertical, slash, block_position)
    recurrent_mixer_result = mamba_mix(
        ssm_input, gate, state_in, state_out, step_size, decay_log, skip_gain, norm_gain
    )
    return (attention_out, recurrent_mixer_result)


def solution(mesh):
    return jax.shard_map(
        local,
        mesh=mesh,
        in_specs=(
            P("ctx", "tp"),
            P("ctx", "tp"),
            P("ctx", "tp"),
            P("tp", None),
            P("tp", None),
            P(),
            P("ctx", "tp"),
            P("ctx", "tp"),
            P("ctx", None),
            P("ctx", None),
            P("ctx", "tp"),
            P("tp"),
            P("tp"),
            P("tp"),
        ),
        out_specs=(P("ctx", "tp"), P("ctx", "tp")),
        check_vma=False,
    )
```

profile of v0, /device:TPU:9, one launch (start us, length us, event | category | flops | bytes accessed | tf_op | source)
XLA Modules:
  0.0 582.7 jit_solution(7373096415645136859)
XLA Ops:
  12.2 204.9 %while.34 = (s32[]{:T(128)}, f32[1,8,256]{2,1,0:T(8,128)S(1)}, f32[1,8,256]{2,1,0:T(8,128)S(1)}, f32[1,8,256,128]{3,2,1,0:T(8,128)S(1)}, bf16[2,256,128]{2,1,0:T...) while((s32[]{:T(128)}, f32[1,8,256]{2,1,0:T(8,128)S(1)}, ...), condition=%wide.region_5.6_spmd.clone, body=%wide.region_0.5_spmd.clone.sunk | while | flops 275070112 | bytes 10201092 | solution.py:97
  18.0 3.0 collective-permute-done.1
  49.3 2.4 collective-permute-done.1
  55.8 3.3 collective-permute-done.1
  63.3 2.4 collective-permute-done.1
  93.9 2.7 collective-permute-done.1
  100.8 2.9 collective-permute-done.1
  131.9 2.1 collective-permute-done.1
  138.3 3.5 collective-permute-done.1
  146.0 2.7 collective-permute-done.1
  176.9 2.6 collective-permute-done.1
  183.7 4.7 collective-permute-done.1
  192.5 3.0 collective-permute-done.1
  199.7 3.5 collective-permute-done.1
  207.4 3.1 collective-permute-done.1
  214.7 2.4 collective-permute-done.1
  223.5 268.1 %while.33 = (s32[]{:T(128)}, f32[16,2048]{1,0:T(8,128)S(1)}, f32[16,2048]{1,0:T(8,128)S(1)}, f32[32]{0:T(128)S(1)}, s32[]{:T(128)}) while((s32[]{:T(128)}, f32[16,2048]{1,0:T(8,128)S(1)}, f32[16,2048]{1,0:T(8,128)S(1)}, f32[32]{0:T(128)S(1)}, s32[]{:T(128)}) %tuple.98), condition=%wide.region_13.14_spmd.clone, body=%wide.region_12.13_spmd.clone.sunk | while | flops 65538 | bytes 950501 | solution.py:139
  223.6 1.9 collective-permute-start
  225.6 6.6 %collective-permute-done = f32[16,2048]{1,0:T(8,128)S(1)} collective-permute-done((f32[16,2048]{1,0:T(8,128)S(1)}, f32[16,2048]{1,0:T(8,128)S(1)}, u32[]{:S(2)}, u32[]{:S(2)}) %collective-permute-start) | collective-permute-done | bytes 131104 | tf_op jit(solution)/shard_map/while/body/eval_jaxpr/ppermute | solution.py:27
  232.4 1.9 collective-permute-start
  234.3 7.3 %collective-permute-done = f32[16,2048]{1,0:T(8,128)S(1)} collective-permute-done((f32[16,2048]{1,0:T(8,128)S(1)}, f32[16,2048]{1,0:T(8,128)S(1)}, u32[]{:S(2)}, u32[]{:S(2)}) %collective-permute-start) | collective-permute-done | bytes 131104 | tf_op jit(solution)/shard_map/while/body/eval_jaxpr/ppermute | solution.py:27
  241.8 1.9 collective-permute-start
  243.7 7.9 %collective-permute-done = f32[16,2048]{1,0:T(8,128)S(1)} collective-permute-done((f32[16,2048]{1,0:T(8,128)S(1)}, f32[16,2048]{1,0:T(8,128)S(1)}, u32[]{:S(2)}, u32[]{:S(2)}) %collective-permute-start) | collective-permute-done | bytes 131104 | tf_op jit(solution)/shard_map/while/body/eval_jaxpr/ppermute | solution.py:27
  251.8 1.9 collective-permute-start
  253.7 7.6 %collective-permute-done = f32[16,2048]{1,0:T(8,128)S(1)} collective-permute-done((f32[16,2048]{1,0:T(8,128)S(1)}, f32[16,2048]{1,0:T(8,128)S(1)}, u32[]{:S(2)}, u32[]{:S(2)}) %collective-permute-start) | collective-permute-done | bytes 131104 | tf_op jit(solution)/shard_map/while/body/eval_jaxpr/ppermute | solution.py:27
  261.5 1.9 collective-permute-start
  263.5 7.4 %collective-permute-done = f32[16,2048]{1,0:T(8,128)S(1)} collective-permute-done((f32[16,2048]{1,0:T(8,128)S(1)}, f32[16,2048]{1,0:T(8,128)S(1)}, u32[]{:S(2)}, u32[]{:S(2)}) %collective-permute-start) | collective-permute-done | bytes 131104 | tf_op jit(solution)/shard_map/while/body/eval_jaxpr/ppermute | solution.py:27
  272.9 7.4 %collective-permute-done = f32[16,2048]{1,0:T(8,128)S(1)} collective-permute-done((f32[16,2048]{1,0:T(8,128)S(1)}, f32[16,2048]{1,0:T(8,128)S(1)}, u32[]{:S(2)}, u32[]{:S(2)}) %collective-permute-start) | collective-permute-done | bytes 131104 | tf_op jit(solution)/shard_map/while/body/eval_jaxpr/ppermute | solution.py:27
  282.5 7.8 %collective-permute-done = f32[16,2048]{1,0:T(8,128)S(1)} collective-permute-done((f32[16,2048]{1,0:T(8,128)S(1)}, f32[16,2048]{1,0:T(8,128)S(1)}, u32[]{:S(2)}, u32[]{:S(2)}) %collective-permute-start) | collective-permute-done | bytes 131104 | tf_op jit(solution)/shard_map/while/body/eval_jaxpr/ppermute | solution.py:27
  290.4 1.9 collective-permute-start
  292.4 7.3 %collective-permute-done = f32[16,2048]{1,0:T(8,128)S(1)} collective-permute-done((f32[16,2048]{1,0:T(8,128)S(1)}, f32[16,2048]{1,0:T(8,128)S(1)}, u32[]{:S(2)}, u32[]{:S(2)}) %collective-permute-start) | collective-permute-done | bytes 131104 | tf_op jit(solution)/shard_map/while/body/eval_jaxpr/ppermute | solution.py:27
  299.9 1.9 collective-permute-start
  301.8 7.7 %collective-permute-done = f32[16,2048]{1,0:T(8,128)S(1)} collective-permute-done((f32[16,2048]{1,0:T(8,128)S(1)}, f32[16,2048]{1,0:T(8,128)S(1)}, u32[]{:S(2)}, u32[]{:S(2)}) %collective-permute-start) | collective-permute-done | bytes 131104 | tf_op jit(solution)/shard_map/while/body/eval_jaxpr/ppermute | solution.py:27
  309.7 1.9 collective-permute-start
  311.6 5.9 %collective-permute-done = f32[16,2048]{1,0:T(8,128)S(1)} collective-permute-done((f32[16,2048]{1,0:T(8,128)S(1)}, f32[16,2048]{1,0:T(8,128)S(1)}, u32[]{:S(2)}, u32[]{:S(2)}) %collective-permute-start) | collective-permute-done | bytes 131104 | tf_op jit(solution)/shard_map/while/body/eval_jaxpr/ppermute | solution.py:27
  319.6 5.9 %collective-permute-done = f32[16,2048]{1,0:T(8,128)S(1)} collective-permute-done((f32[16,2048]{1,0:T(8,128)S(1)}, f32[16,2048]{1,0:T(8,128)S(1)}, u32[]{:S(2)}, u32[]{:S(2)}) %collective-permute-start) | collective-permute-done | bytes 131104 | tf_op jit(solution)/shard_map/while/body/eval_jaxpr/ppermute | solution.py:27
  327.6 7.1 %collective-permute-done = f32[16,2048]{1,0:T(8,128)S(1)} collective-permute-done((f32[16,2048]{1,0:T(8,128)S(1)}, f32[16,2048]{1,0:T(8,128)S(1)}, u32[]{:S(2)}, u32[]{:S(2)}) %collective-permute-start) | collective-permute-done | bytes 131104 | tf_op jit(solution)/shard_map/while/body/eval_jaxpr/ppermute | solution.py:27
  336.8 6.2 %collective-permute-done = f32[16,2048]{1,0:T(8,128)S(1)} collective-permute-done((f32[16,2048]{1,0:T(8,128)S(1)}, f32[16,2048]{1,0:T(8,128)S(1)}, u32[]{:S(2)}, u32[]{:S(2)}) %collective-permute-start) | collective-permute-done | bytes 131104 | tf_op jit(solution)/shard_map/while/body/eval_jaxpr/ppermute | solution.py:27
  345.1 5.9 %collective-permute-done = f32[16,2048]{1,0:T(8,128)S(1)} collective-permute-done((f32[16,2048]{1,0:T(8,128)S(1)}, f32[16,2048]{1,0:T(8,128)S(1)}, u32[]{:S(2)}, u32[]{:S(2)}) %collective-permute-start) | collective-permute-done | bytes 131104 | tf_op jit(solution)/shard_map/while/body/eval_jaxpr/ppermute | solution.py:27
  353.1 5.9 %collective-permute-done = f32[16,2048]{1,0:T(8,128)S(1)} collective-permute-done((f32[16,2048]{1,0:T(8,128)S(1)}, f32[16,2048]{1,0:T(8,128)S(1)}, u32[]{:S(2)}, u32[]{:S(2)}) %collective-permute-start) | collective-permute-done | bytes 131104 | tf_op jit(solution)/shard_map/while/body/eval_jaxpr/ppermute | solution.py:27
  361.1 5.9 %collective-permute-done = f32[16,2048]{1,0:T(8,128)S(1)} collective-permute-done((f32[16,2048]{1,0:T(8,128)S(1)}, f32[16,2048]{1,0:T(8,128)S(1)}, u32[]{:S(2)}, u32[]{:S(2)}) %collective-permute-start) | collective-permute-done | bytes 131104 | tf_op jit(solution)/shard_map/while/body/eval_jaxpr/ppermute | solution.py:27
  369.1 5.9 %collective-permute-done = f32[16,2048]{1,0:T(8,128)S(1)} collective-permute-done((f32[16,2048]{1,0:T(8,128)S(1)}, f32[16,2048]{1,0:T(8,128)S(1)}, u32[]{:S(2)}, u32[]{:S(2)}) %collective-permute-start) | collective-permute-done | bytes 131104 | tf_op jit(solution)/shard_map/while/body/eval_jaxpr/ppermute | solution.py:27
  375.2 1.9 collective-permute-start
  377.1 5.9 %collective-permute-done = f32[16,2048]{1,0:T(8,128)S(1)} collective-permute-done((f32[16,2048]{1,0:T(8,128)S(1)}, f32[16,2048]{1,0:T(8,128)S(1)}, u32[]{:S(2)}, u32[]{:S(2)}) %collective-permute-start) | collective-permute-done | bytes 131104 | tf_op jit(solution)/shard_map/while/body/eval_jaxpr/ppermute | solution.py:27
  385.1 6.1 %collective-permute-done = f32[16,2048]{1,0:T(8,128)S(1)} collective-permute-done((f32[16,2048]{1,0:T(8,128)S(1)}, f32[16,2048]{1,0:T(8,128)S(1)}, u32[]{:S(2)}, u32[]{:S(2)}) %collective-permute-start) | collective-permute-done | bytes 131104 | tf_op jit(solution)/shard_map/while/body/eval_jaxpr/ppermute | solution.py:27
  393.3 7.5 %collective-permute-done = f32[16,2048]{1,0:T(8,128)S(1)} collective-permute-done((f32[16,2048]{1,0:T(8,128)S(1)}, f32[16,2048]{1,0:T(8,128)S(1)}, u32[]{:S(2)}, u32[]{:S(2)}) %collective-permute-start) | collective-permute-done | bytes 131104 | tf_op jit(solution)/shard_map/while/body/eval_jaxpr/ppermute | solution.py:27
  401.0 1.9 collective-permute-start
  402.9 6.8 %collective-permute-done = f32[16,2048]{1,0:T(8,128)S(1)} collective-permute-done((f32[16,2048]{1,0:T(8,128)S(1)}, f32[16,2048]{1,0:T(8,128)S(1)}, u32[]{:S(2)}, u32[]{:S(2)}) %collective-permute-start) | collective-permute-done | bytes 131104 | tf_op jit(solution)/shard_map/while/body/eval_jaxpr/ppermute | solution.py:27
  411.8 5.9 %collective-permute-done = f32[16,2048]{1,0:T(8,128)S(1)} collective-permute-done((f32[16,2048]{1,0:T(8,128)S(1)}, f32[16,2048]{1,0:T(8,128)S(1)}, u32[]{:S(2)}, u32[]{:S(2)}) %collective-permute-start) | collective-permute-done | bytes 131104 | tf_op jit(solution)/shard_map/while/body/eval_jaxpr/ppermute | solution.py:27
  419.8 5.9 %collective-permute-done = f32[16,2048]{1,0:T(8,128)S(1)} collective-permute-done((f32[16,2048]{1,0:T(8,128)S(1)}, f32[16,2048]{1,0:T(8,128)S(1)}, u32[]{:S(2)}, u32[]{:S(2)}) %collective-permute-start) | collective-permute-done | bytes 131104 | tf_op jit(solution)/shard_map/while/body/eval_jaxpr/ppermute | solution.py:27
  427.8 5.9 %collective-permute-done = f32[16,2048]{1,0:T(8,128)S(1)} collective-permute-done((f32[16,2048]{1,0:T(8,128)S(1)}, f32[16,2048]{1,0:T(8,128)S(1)}, u32[]{:S(2)}, u32[]{:S(2)}) %collective-permute-start) | collective-permute-done | bytes 131104 | tf_op jit(solution)/shard_map/while/body/eval_jaxpr/ppermute | solution.py:27
  435.8 5.9 %collective-permute-done = f32[16,2048]{1,0:T(8,128)S(1)} collective-permute-done((f32[16,2048]{1,0:T(8,128)S(1)}, f32[16,2048]{1,0:T(8,128)S(1)}, u32[]{:S(2)}, u32[]{:S(2)}) %collective-permute-start) | collective-permute-done | bytes 131104 | tf_op jit(solution)/shard_map/while/body/eval_jaxpr/ppermute | solution.py:27
  441.8 1.9 collective-permute-start
  443.8 5.9 %collective-permute-done = f32[16,2048]{1,0:T(8,128)S(1)} collective-permute-done((f32[16,2048]{1,0:T(8,128)S(1)}, f32[16,2048]{1,0:T(8,128)S(1)}, u32[]{:S(2)}, u32[]{:S(2)}) %collective-permute-start) | collective-permute-done | bytes 131104 | tf_op jit(solution)/shard_map/while/body/eval_jaxpr/ppermute | solution.py:27
  451.7 5.9 %collective-permute-done = f32[16,2048]{1,0:T(8,128)S(1)} collective-permute-done((f32[16,2048]{1,0:T(8,128)S(1)}, f32[16,2048]{1,0:T(8,128)S(1)}, u32[]{:S(2)}, u32[]{:S(2)}) %collective-permute-start) | collective-permute-done | bytes 131104 | tf_op jit(solution)/shard_map/while/body/eval_jaxpr/ppermute | solution.py:27
  457.8 1.9 collective-permute-start
  459.7 6.7 %collective-permute-done = f32[16,2048]{1,0:T(8,128)S(1)} collective-permute-done((f32[16,2048]{1,0:T(8,128)S(1)}, f32[16,2048]{1,0:T(8,128)S(1)}, u32[]{:S(2)}, u32[]{:S(2)}) %collective-permute-start) | collective-permute-done | bytes 131104 | tf_op jit(solution)/shard_map/while/body/eval_jaxpr/ppermute | solution.py:27
  466.6 1.9 collective-permute-start
  468.6 7.0 %collective-permute-done = f32[16,2048]{1,0:T(8,128)S(1)} collective-permute-done((f32[16,2048]{1,0:T(8,128)S(1)}, f32[16,2048]{1,0:T(8,128)S(1)}, u32[]{:S(2)}, u32[]{:S(2)}) %collective-permute-start) | collective-permute-done | bytes 131104 | tf_op jit(solution)/shard_map/while/body/eval_jaxpr/ppermute | solution.py:27
  477.7 5.9 %collective-permute-done = f32[16,2048]{1,0:T(8,128)S(1)} collective-permute-done((f32[16,2048]{1,0:T(8,128)S(1)}, f32[16,2048]{1,0:T(8,128)S(1)}, u32[]{:S(2)}, u32[]{:S(2)}) %collective-permute-start) | collective-permute-done | bytes 131104 | tf_op jit(solution)/shard_map/while/body/eval_jaxpr/ppermute | solution.py:27
  485.7 5.9 %collective-permute-done = f32[16,2048]{1,0:T(8,128)S(1)} collective-permute-done((f32[16,2048]{1,0:T(8,128)S(1)}, f32[16,2048]{1,0:T(8,128)S(1)}, u32[]{:S(2)}, u32[]{:S(2)}) %collective-permute-start) | collective-permute-done | bytes 131104 | tf_op jit(solution)/shard_map/while/body/eval_jaxpr/ppermute | solution.py:27
  492.3 6.8 %fusion.31 = f32[256,32,64]{0,2,1:T(8,128)} fusion(f32[256,32,64]{0,2,1:T(8,128)S(1)} %bitcast.207, f32[256,32,64]{0,2,1:T(8,128)S(1)} %bitcast.209, f32[256,256]{1,0:T(8,128)S(1)} %fusion.64, f32[32,256]{1,0:T(8,128)S(1)} %copy-done.9, pred[256,256]{1,0:T(8,128)(4,1)S(1)} %iota_compare_fusion, f32[32]{0:T(128)S(1)} %copy-done.14, ...), kind=kOutput, calls=%fused_computation.52 | convolution fusion | flops 816316416 | bytes 6717568 | tf_op jit(solution)/shard_map/hts,shp->thp/dot_general | solution.py:129
  499.1 2.0 copy.74
  501.9 79.1 %psum.7 = f32[256]{0:T(256)S(1)} all-reduce(f32[256]{0:T(256)S(1)} %multiply_reduce_fusion), channel_id=1, replica_groups=mesh['ctx'=32,'tp'=8] {'tp'}, use_global_device_ids=true, to_apply=%region_15.16 | all-reduce | flops 256 | bytes 2048 | tf_op jit(solution)/shard_map/psum | solution.py:147
  (887 shorter events, 218.0 us)
Async XLA Ops:
  12.3 8.8 %collective-permute-start.1 = (bf16[2,256,128]{2,1,0:T(8,128)(2,1)S(1)}, bf16[2,256,128]{2,1,0:T(8,128)(2,1)S(1)}, u32[]{:S(2)}, u32[]{:S(2)}) collective-permute-start(bf16[2,256,128]{2,1,0:T(8,128)(2,1)S(1)} %copy.106), channel_id=1, source_target_pairs={{0,8},{8,16},{16,24},{24,32},{32,40},{40,48},{48,56},{56,64},{64,7... | collective-permute-start | bytes 393224 | tf_op jit(solution)/shard_map/while/body/eval_jaxpr/ppermute | solution.py:21
  21.0 6.0 %collective-permute-start.1 = (bf16[2,256,128]{2,1,0:T(8,128)(2,1)S(1)}, bf16[2,256,128]{2,1,0:T(8,128)(2,1)S(1)}, u32[]{:S(2)}, u32[]{:S(2)}) collective-permute-start(bf16[2,256,128]{2,1,0:T(8,128)(2,1)S(1)} %copy.106), channel_id=1, source_target_pairs={{0,8},{8,16},{16,24},{24,32},{32,40},{40,48},{48,56},{56,64},{64,7... | collective-permute-start | bytes 393224 | tf_op jit(solution)/shard_map/while/body/eval_jaxpr/ppermute | solution.py:21
  27.1 6.0 %collective-permute-start.1 = (bf16[2,256,128]{2,1,0:T(8,128)(2,1)S(1)}, bf16[2,256,128]{2,1,0:T(8,128)(2,1)S(1)}, u32[]{:S(2)}, u32[]{:S(2)}) collective-permute-start(bf16[2,256,128]{2,1,0:T(8,128)(2,1)S(1)} %copy.106), channel_id=1, source_target_pairs={{0,8},{8,16},{16,24},{24,32},{32,40},{40,48},{48,56},{56,64},{64,7... | collective-permute-start | bytes 393224 | tf_op jit(solution)/shard_map/while/body/eval_jaxpr/ppermute | solution.py:21
  33.1 6.0 %collective-permute-start.1 = (bf16[2,256,128]{2,1,0:T(8,128)(2,1)S(1)}, bf16[2,256,128]{2,1,0:T(8,128)(2,1)S(1)}, u32[]{:S(2)}, u32[]{:S(2)}) collective-permute-start(bf16[2,256,128]{2,1,0:T(8,128)(2,1)S(1)} %copy.106), channel_id=1, source_target_pairs={{0,8},{8,16},{16,24},{24,32},{32,40},{40,48},{48,56},{56,64},{64,7... | collective-permute-start | bytes 393224 | tf_op jit(solution)/shard_map/while/body/eval_jaxpr/ppermute | solution.py:21
  39.1 6.0 %collective-permute-start.1 = (bf16[2,256,128]{2,1,0:T(8,128)(2,1)S(1)}, bf16[2,256,128]{2,1,0:T(8,128)(2,1)S(1)}, u32[]{:S(2)}, u32[]{:S(2)}) collective-permute-start(bf16[2,256,128]{2,1,0:T(8,128)(2,1)S(1)} %copy.106), channel_id=1, source_target_pairs={{0,8},{8,16},{16,24},{24,32},{32,40},{40,48},{48,56},{56,64},{64,7... | collective-permute-start | bytes 393224 | tf_op jit(solution)/shard_map/while/body/eval_jaxpr/ppermute | solution.py:21
  45.1 6.5 %collective-permute-start.1 = (bf16[2,256,128]{2,1,0:T(8,128)(2,1)S(1)}, bf16[2,256,128]{2,1,0:T(8,128)(2,1)S(1)}, u32[]{:S(2)}, u32[]{:S(2)}) collective-permute-start(bf16[2,256,128]{2,1,0:T(8,128)(2,1)S(1)} %copy.106), channel_id=1, source_target_pairs={{0,8},{8,16},{16,24},{24,32},{32,40},{40,48},{48,56},{56,64},{64,7... | collective-permute-start | bytes 393224 | tf_op jit(solution)/shard_map/while/body/eval_jaxpr/ppermute | solution.py:21
  51.7 7.4 %collective-permute-start.1 = (bf16[2,256,128]{2,1,0:T(8,128)(2,1)S(1)}, bf16[2,256,128]{2,1,0:T(8,128)(2,1)S(1)}, u32[]{:S(2)}, u32[]{:S(2)}) collective-permute-start(bf16[2,256,128]{2,1,0:T(8,128)(2,1)S(1)} %copy.106), channel_id=1, source_target_pairs={{0,8},{8,16},{16,24},{24,32},{32,40},{40,48},{48,56},{56,64},{64,7... | collective-permute-start | bytes 393224 | tf_op jit(solution)/shard_map/while/body/eval_jaxpr/ppermute | solution.py:21
  59.1 6.5 %collective-permute-start.1 = (bf16[2,256,128]{2,1,0:T(8,128)(2,1)S(1)}, bf16[2,256,128]{2,1,0:T(8,128)(2,1)S(1)}, u32[]{:S(2)}, u32[]{:S(2)}) collective-permute-start(bf16[2,256,128]{2,1,0:T(8,128)(2,1)S(1)} %copy.106), channel_id=1, source_target_pairs={{0,8},{8,16},{16,24},{24,32},{32,40},{40,48},{48,56},{56,64},{64,7... | collective-permute-start | bytes 393224 | tf_op jit(solution)/shard_map/while/body/eval_jaxpr/ppermute | solution.py:21
  65.7 6.0 %collective-permute-start.1 = (bf16[2,256,128]{2,1,0:T(8,128)(2,1)S(1)}, bf16[2,256,128]{2,1,0:T(8,128)(2,1)S(1)}, u32[]{:S(2)}, u32[]{:S(2)}) collective-permute-start(bf16[2,256,128]{2,1,0:T(8,128)(2,1)S(1)} %copy.106), channel_id=1, source_target_pairs={{0,8},{8,16},{16,24},{24,32},{32,40},{40,48},{48,56},{56,64},{64,7... | collective-permute-start | bytes 393224 | tf_op jit(solution)/shard_map/while/body/eval_jaxpr/ppermute | solution.py:21
  71.7 6.0 %collective-permute-start.1 = (bf16[2,256,128]{2,1,0:T(8,128)(2,1)S(1)}, bf16[2,256,128]{2,1,0:T(8,128)(2,1)S(1)}, u32[]{:S(2)}, u32[]{:S(2)}) collective-permute-start(bf16[2,256,128]{2,1,0:T(8,128)(2,1)S(1)} %copy.106), channel_id=1, source_target_pairs={{0,8},{8,16},{16,24},{24,32},{32,40},{40,48},{48,56},{56,64},{64,7... | collective-permute-start | bytes 393224 | tf_op jit(solution)/shard_map/while/body/eval_jaxpr/ppermute | solution.py:21
  77.7 6.0 %collective-permute-start.1 = (bf16[2,256,128]{2,1,0:T(8,128)(2,1)S(1)}, bf16[2,256,128]{2,1,0:T(8,128)(2,1)S(1)}, u32[]{:S(2)}, u32[]{:S(2)}) collective-permute-start(bf16[2,256,128]{2,1,0:T(8,128)(2,1)S(1)} %copy.106), channel_id=1, source_target_pairs={{0,8},{8,16},{16,24},{24,32},{32,40},{40,48},{48,56},{56,64},{64,7... | collective-permute-start | bytes 393224 | tf_op jit(solution)/shard_map/while/body/eval_jaxpr/ppermute | solution.py:21
  83.7 6.0 %collective-permute-start.1 = (bf16[2,256,128]{2,1,0:T(8,128)(2,1)S(1)}, bf16[2,256,128]{2,1,0:T(8,128)(2,1)S(1)}, u32[]{:S(2)}, u32[]{:S(2)}) collective-permute-start(bf16[2,256,128]{2,1,0:T(8,128)(2,1)S(1)} %copy.106), channel_id=1, source_target_pairs={{0,8},{8,16},{16,24},{24,32},{32,40},{40,48},{48,56},{56,64},{64,7... | collective-permute-start | bytes 393224 | tf_op jit(solution)/shard_map/while/body/eval_jaxpr/ppermute | solution.py:21
  89.7 6.9 %collective-permute-start.1 = (bf16[2,256,128]{2,1,0:T(8,128)(2,1)S(1)}, bf16[2,256,128]{2,1,0:T(8,128)(2,1)S(1)}, u32[]{:S(2)}, u32[]{:S(2)}) collective-permute-start(bf16[2,256,128]{2,1,0:T(8,128)(2,1)S(1)} %copy.106), channel_id=1, source_target_pairs={{0,8},{8,16},{16,24},{24,32},{32,40},{40,48},{48,56},{56,64},{64,7... | collective-permute-start | bytes 393224 | tf_op jit(solution)/shard_map/while/body/eval_jaxpr/ppermute | solution.py:21
  96.6 7.1 %collective-permute-start.1 = (bf16[2,256,128]{2,1,0:T(8,128)(2,1)S(1)}, bf16[2,256,128]{2,1,0:T(8,128)(2,1)S(1)}, u32[]{:S(2)}, u32[]{:S(2)}) collective-permute-start(bf16[2,256,128]{2,1,0:T(8,128)(2,1)S(1)} %copy.106), channel_id=1, source_target_pairs={{0,8},{8,16},{16,24},{24,32},{32,40},{40,48},{48,56},{56,64},{64,7... | collective-permute-start | bytes 393224 | tf_op jit(solution)/shard_map/while/body/eval_jaxpr/ppermute | solution.py:21
  103.7 6.0 %collective-permute-start.1 = (bf16[2,256,128]{2,1,0:T(8,128)(2,1)S(1)}, bf16[2,256,128]{2,1,0:T(8,128)(2,1)S(1)}, u32[]{:S(2)}, u32[]{:S(2)}) collective-permute-start(bf16[2,256,128]{2,1,0:T(8,128)(2,1)S(1)} %copy.106), channel_id=1, source_target_pairs={{0,8},{8,16},{16,24},{24,32},{32,40},{40,48},{48,56},{56,64},{64,7... | collective-permute-start | bytes 393224 | tf_op jit(solution)/shard_map/while/body/eval_jaxpr/ppermute | solution.py:21
  109.7 6.0 %collective-permute-start.1 = (bf16[2,256,128]{2,1,0:T(8,128)(2,1)S(1)}, bf16[2,256,128]{2,1,0:T(8,128)(2,1)S(1)}, u32[]{:S(2)}, u32[]{:S(2)}) collective-permute-start(bf16[2,256,128]{2,1,0:T(8,128)(2,1)S(1)} %copy.106), channel_id=1, source_target_pairs={{0,8},{8,16},{16,24},{24,32},{32,40},{40,48},{48,56},{56,64},{64,7... | collective-permute-start | bytes 393224 | tf_op jit(solution)/shard_map/while/body/eval_jaxpr/ppermute | solution.py:21
  115.8 6.0 %collective-permute-start.1 = (bf16[2,256,128]{2,1,0:T(8,128)(2,1)S(1)}, bf16[2,256,128]{2,1,0:T(8,128)(2,1)S(1)}, u32[]{:S(2)}, u32[]{:S(2)}) collective-permute-start(bf16[2,256,128]{2,1,0:T(8,128)(2,1)S(1)} %copy.106), channel_id=1, source_target_pairs={{0,8},{8,16},{16,24},{24,32},{32,40},{40,48},{48,56},{56,64},{64,7... | collective-permute-start | bytes 393224 | tf_op jit(solution)/shard_map/while/body/eval_jaxpr/ppermute | solution.py:21
  121.8 6.0 %collective-permute-start.1 = (bf16[2,256,128]{2,1,0:T(8,128)(2,1)S(1)}, bf16[2,256,128]{2,1,0:T(8,128)(2,1)S(1)}, u32[]{:S(2)}, u32[]{:S(2)}) collective-permute-start(bf16[2,256,128]{2,1,0:T(8,128)(2,1)S(1)} %copy.106), channel_id=1, source_target_pairs={{0,8},{8,16},{16,24},{24,32},{32,40},{40,48},{48,56},{56,64},{64,7... | collective-permute-start | bytes 393224 | tf_op jit(solution)/shard_map/while/body/eval_jaxpr/ppermute | solution.py:21
  127.8 6.3 %collective-permute-start.1 = (bf16[2,256,128]{2,1,0:T(8,128)(2,1)S(1)}, bf16[2,256,128]{2,1,0:T(8,128)(2,1)S(1)}, u32[]{:S(2)}, u32[]{:S(2)}) collective-permute-start(bf16[2,256,128]{2,1,0:T(8,128)(2,1)S(1)} %copy.106), channel_id=1, source_target_pairs={{0,8},{8,16},{16,24},{24,32},{32,40},{40,48},{48,56},{56,64},{64,7... | collective-permute-start | bytes 393224 | tf_op jit(solution)/shard_map/while/body/eval_jaxpr/ppermute | solution.py:21
  134.1 7.7 %collective-permute-start.1 = (bf16[2,256,128]{2,1,0:T(8,128)(2,1)S(1)}, bf16[2,256,128]{2,1,0:T(8,128)(2,1)S(1)}, u32[]{:S(2)}, u32[]{:S(2)}) collective-permute-start(bf16[2,256,128]{2,1,0:T(8,128)(2,1)S(1)} %copy.106), channel_id=1, source_target_pairs={{0,8},{8,16},{16,24},{24,32},{32,40},{40,48},{48,56},{56,64},{64,7... | collective-permute-start | bytes 393224 | tf_op jit(solution)/shard_map/while/body/eval_jaxpr/ppermute | solution.py:21
  141.8 6.8 %collective-permute-start.1 = (bf16[2,256,128]{2,1,0:T(8,128)(2,1)S(1)}, bf16[2,256,128]{2,1,0:T(8,128)(2,1)S(1)}, u32[]{:S(2)}, u32[]{:S(2)}) collective-permute-start(bf16[2,256,128]{2,1,0:T(8,128)(2,1)S(1)} %copy.106), channel_id=1, source_target_pairs={{0,8},{8,16},{16,24},{24,32},{32,40},{40,48},{48,56},{56,64},{64,7... | collective-permute-start | bytes 393224 | tf_op jit(solution)/shard_map/while/body/eval_jaxpr/ppermute | solution.py:21
  148.6 6.0 %collective-permute-start.1 = (bf16[2,256,128]{2,1,0:T(8,128)(2,1)S(1)}, bf16[2,256,128]{2,1,0:T(8,128)(2,1)S(1)}, u32[]{:S(2)}, u32[]{:S(2)}) collective-permute-start(bf16[2,256,128]{2,1,0:T(8,128)(2,1)S(1)} %copy.106), channel_id=1, source_target_pairs={{0,8},{8,16},{16,24},{24,32},{32,40},{40,48},{48,56},{56,64},{64,7... | collective-permute-start | bytes 393224 | tf_op jit(solution)/shard_map/while/body/eval_jaxpr/ppermute | solution.py:21
  154.7 6.0 %collective-permute-start.1 = (bf16[2,256,128]{2,1,0:T(8,128)(2,1)S(1)}, bf16[2,256,128]{2,1,0:T(8,128)(2,1)S(1)}, u32[]{:S(2)}, u32[]{:S(2)}) collective-permute-start(bf16[2,256,128]{2,1,0:T(8,128)(2,1)S(1)} %copy.106), channel_id=1, source_target_pairs={{0,8},{8,16},{16,24},{24,32},{32,40},{40,48},{48,56},{56,64},{64,7... | collective-permute-start | bytes 393224 | tf_op jit(solution)/shard_map/while/body/eval_jaxpr/ppermute | solution.py:21
  160.7 6.0 %collective-permute-start.1 = (bf16[2,256,128]{2,1,0:T(8,128)(2,1)S(1)}, bf16[2,256,128]{2,1,0:T(8,128)(2,1)S(1)}, u32[]{:S(2)}, u32[]{:S(2)}) collective-permute-start(bf16[2,256,128]{2,1,0:T(8,128)(2,1)S(1)} %copy.106), channel_id=1, source_target_pairs={{0,8},{8,16},{16,24},{24,32},{32,40},{40,48},{48,56},{56,64},{64,7... | collective-permute-start | bytes 393224 | tf_op jit(solution)/shard_map/while/body/eval_jaxpr/ppermute | solution.py:21
  166.7 6.0 %collective-permute-start.1 = (bf16[2,256,128]{2,1,0:T(8,128)(2,1)S(1)}, bf16[2,256,128]{2,1,0:T(8,128)(2,1)S(1)}, u32[]{:S(2)}, u32[]{:S(2)}) collective-permute-start(bf16[2,256,128]{2,1,0:T(8,128)(2,1)S(1)} %copy.106), channel_id=1, source_target_pairs={{0,8},{8,16},{16,24},{24,32},{32,40},{40,48},{48,56},{56,64},{64,7... | collective-permute-start | bytes 393224 | tf_op jit(solution)/shard_map/while/body/eval_jaxpr/ppermute | solution.py:21
  172.7 6.8 %collective-permute-start.1 = (bf16[2,256,128]{2,1,0:T(8,128)(2,1)S(1)}, bf16[2,256,128]{2,1,0:T(8,128)(2,1)S(1)}, u32[]{:S(2)}, u32[]{:S(2)}) collective-permute-start(bf16[2,256,128]{2,1,0:T(8,128)(2,1)S(1)} %copy.106), channel_id=1, source_target_pairs={{0,8},{8,16},{16,24},{24,32},{32,40},{40,48},{48,56},{56,64},{64,7... | collective-permute-start | bytes 393224 | tf_op jit(solution)/shard_map/while/body/eval_jaxpr/ppermute | solution.py:21
  179.5 8.9 %collective-permute-start.1 = (bf16[2,256,128]{2,1,0:T(8,128)(2,1)S(1)}, bf16[2,256,128]{2,1,0:T(8,128)(2,1)S(1)}, u32[]{:S(2)}, u32[]{:S(2)}) collective-permute-start(bf16[2,256,128]{2,1,0:T(8,128)(2,1)S(1)} %copy.106), channel_id=1, source_target_pairs={{0,8},{8,16},{16,24},{24,32},{32,40},{40,48},{48,56},{56,64},{64,7... | collective-permute-start | bytes 393224 | tf_op jit(solution)/shard_map/while/body/eval_jaxpr/ppermute | solution.py:21
  188.4 7.1 %collective-permute-start.1 = (bf16[2,256,128]{2,1,0:T(8,128)(2,1)S(1)}, bf16[2,256,128]{2,1,0:T(8,128)(2,1)S(1)}, u32[]{:S(2)}, u32[]{:S(2)}) collective-permute-start(bf16[2,256,128]{2,1,0:T(8,128)(2,1)S(1)} %copy.106), channel_id=1, source_target_pairs={{0,8},{8,16},{16,24},{24,32},{32,40},{40,48},{48,56},{56,64},{64,7... | collective-permute-start | bytes 393224 | tf_op jit(solution)/shard_map/while/body/eval_jaxpr/ppermute | solution.py:21
  195.5 7.7 %collective-permute-start.1 = (bf16[2,256,128]{2,1,0:T(8,128)(2,1)S(1)}, bf16[2,256,128]{2,1,0:T(8,128)(2,1)S(1)}, u32[]{:S(2)}, u32[]{:S(2)}) collective-permute-start(bf16[2,256,128]{2,1,0:T(8,128)(2,1)S(1)} %copy.106), channel_id=1, source_target_pairs={{0,8},{8,16},{16,24},{24,32},{32,40},{40,48},{48,56},{56,64},{64,7... | collective-permute-start | bytes 393224 | tf_op jit(solution)/shard_map/while/body/eval_jaxpr/ppermute | solution.py:21
  203.2 7.2 %collective-permute-start.1 = (bf16[2,256,128]{2,1,0:T(8,128)(2,1)S(1)}, bf16[2,256,128]{2,1,0:T(8,128)(2,1)S(1)}, u32[]{:S(2)}, u32[]{:S(2)}) collective-permute-start(bf16[2,256,128]{2,1,0:T(8,128)(2,1)S(1)} %copy.106), channel_id=1, source_target_pairs={{0,8},{8,16},{16,24},{24,32},{32,40},{40,48},{48,56},{56,64},{64,7... | collective-permute-start | bytes 393224 | tf_op jit(solution)/shard_map/while/body/eval_jaxpr/ppermute | solution.py:21
  210.5 6.6 %collective-permute-start.1 = (bf16[2,256,128]{2,1,0:T(8,128)(2,1)S(1)}, bf16[2,256,128]{2,1,0:T(8,128)(2,1)S(1)}, u32[]{:S(2)}, u32[]{:S(2)}) collective-permute-start(bf16[2,256,128]{2,1,0:T(8,128)(2,1)S(1)} %copy.106), channel_id=1, source_target_pairs={{0,8},{8,16},{16,24},{24,32},{32,40},{40,48},{48,56},{56,64},{64,7... | collective-permute-start | bytes 393224 | tf_op jit(solution)/shard_map/while/body/eval_jaxpr/ppermute | solution.py:21
  223.4 268.9 %copy-start.9 = (f32[32,256]{1,0:T(8,128)S(1)}, f32[32,256]{1,0:T(8,128)}, u32[]{:S(2)}) copy-start(f32[32,256]{1,0:T(8,128)} %get-tuple-element.464) | copy-start | bytes 98308
  223.4 268.9 %copy-start.10 = (f32[256,32]{0,1:T(8,128)S(1)}, f32[256,32]{0,1:T(8,128)}, u32[]{:S(2)}) copy-start(f32[256,32]{0,1:T(8,128)} %get-tuple-element.462) | copy-start | bytes 98308
  223.6 8.5 %collective-permute-start = (f32[16,2048]{1,0:T(8,128)S(1)}, f32[16,2048]{1,0:T(8,128)S(1)}, u32[]{:S(2)}, u32[]{:S(2)}) collective-permute-start(f32[16,2048]{1,0:T(8,128)S(1)} %multiply_add_fusion.2), channel_id=1, source_target_pairs={{0,8},{8,16},{16,24},{24,32},{32,40},{40,48},{48,56},{56,64},{64,7... | collective-permute-start | bytes 393224 | tf_op jit(solution)/shard_map/while/body/eval_jaxpr/ppermute | solution.py:27
  232.4 9.3 %collective-permute-start = (f32[16,2048]{1,0:T(8,128)S(1)}, f32[16,2048]{1,0:T(8,128)S(1)}, u32[]{:S(2)}, u32[]{:S(2)}) collective-permute-start(f32[16,2048]{1,0:T(8,128)S(1)} %multiply_add_fusion.2), channel_id=1, source_target_pairs={{0,8},{8,16},{16,24},{24,32},{32,40},{40,48},{48,56},{56,64},{64,7... | collective-permute-start | bytes 393224 | tf_op jit(solution)/shard_map/while/body/eval_jaxpr/ppermute | solution.py:27
  241.8 9.8 %collective-permute-start = (f32[16,2048]{1,0:T(8,128)S(1)}, f32[16,2048]{1,0:T(8,128)S(1)}, u32[]{:S(2)}, u32[]{:S(2)}) collective-permute-start(f32[16,2048]{1,0:T(8,128)S(1)} %multiply_add_fusion.2), channel_id=1, source_target_pairs={{0,8},{8,16},{16,24},{24,32},{32,40},{40,48},{48,56},{56,64},{64,7... | collective-permute-start | bytes 393224 | tf_op jit(solution)/shard_map/while/body/eval_jaxpr/ppermute | solution.py:27
  251.8 9.6 %collective-permute-start = (f32[16,2048]{1,0:T(8,128)S(1)}, f32[16,2048]{1,0:T(8,128)S(1)}, u32[]{:S(2)}, u32[]{:S(2)}) collective-permute-start(f32[16,2048]{1,0:T(8,128)S(1)} %multiply_add_fusion.2), channel_id=1, source_target_pairs={{0,8},{8,16},{16,24},{24,32},{32,40},{40,48},{48,56},{56,64},{64,7... | collective-permute-start | bytes 393224 | tf_op jit(solution)/shard_map/while/body/eval_jaxpr/ppermute | solution.py:27
  261.5 9.3 %collective-permute-start = (f32[16,2048]{1,0:T(8,128)S(1)}, f32[16,2048]{1,0:T(8,128)S(1)}, u32[]{:S(2)}, u32[]{:S(2)}) collective-permute-start(f32[16,2048]{1,0:T(8,128)S(1)} %multiply_add_fusion.2), channel_id=1, source_target_pairs={{0,8},{8,16},{16,24},{24,32},{32,40},{40,48},{48,56},{56,64},{64,7... | collective-permute-start | bytes 393224 | tf_op jit(solution)/shard_map/while/body/eval_jaxpr/ppermute | solution.py:27
  271.0 9.3 %collective-permute-start = (f32[16,2048]{1,0:T(8,128)S(1)}, f32[16,2048]{1,0:T(8,128)S(1)}, u32[]{:S(2)}, u32[]{:S(2)}) collective-permute-start(f32[16,2048]{1,0:T(8,128)S(1)} %multiply_add_fusion.2), channel_id=1, source_target_pairs={{0,8},{8,16},{16,24},{24,32},{32,40},{40,48},{48,56},{56,64},{64,7... | collective-permute-start | bytes 393224 | tf_op jit(solution)/shard_map/while/body/eval_jaxpr/ppermute | solution.py:27
  280.5 9.7 %collective-permute-start = (f32[16,2048]{1,0:T(8,128)S(1)}, f32[16,2048]{1,0:T(8,128)S(1)}, u32[]{:S(2)}, u32[]{:S(2)}) collective-permute-start(f32[16,2048]{1,0:T(8,128)S(1)} %multiply_add_fusion.2), channel_id=1, source_target_pairs={{0,8},{8,16},{16,24},{24,32},{32,40},{40,48},{48,56},{56,64},{64,7... | collective-permute-start | bytes 393224 | tf_op jit(solution)/shard_map/while/body/eval_jaxpr/ppermute | solution.py:27
  290.4 9.3 %collective-permute-start = (f32[16,2048]{1,0:T(8,128)S(1)}, f32[16,2048]{1,0:T(8,128)S(1)}, u32[]{:S(2)}, u32[]{:S(2)}) collective-permute-start(f32[16,2048]{1,0:T(8,128)S(1)} %multiply_add_fusion.2), channel_id=1, source_target_pairs={{0,8},{8,16},{16,24},{24,32},{32,40},{40,48},{48,56},{56,64},{64,7... | collective-permute-start | bytes 393224 | tf_op jit(solution)/shard_map/while/body/eval_jaxpr/ppermute | solution.py:27
  299.9 9.6 %collective-permute-start = (f32[16,2048]{1,0:T(8,128)S(1)}, f32[16,2048]{1,0:T(8,128)S(1)}, u32[]{:S(2)}, u32[]{:S(2)}) collective-permute-start(f32[16,2048]{1,0:T(8,128)S(1)} %multiply_add_fusion.2), channel_id=1, source_target_pairs={{0,8},{8,16},{16,24},{24,32},{32,40},{40,48},{48,56},{56,64},{64,7... | collective-permute-start | bytes 393224 | tf_op jit(solution)/shard_map/while/body/eval_jaxpr/ppermute | solution.py:27
  309.7 7.8 %collective-permute-start = (f32[16,2048]{1,0:T(8,128)S(1)}, f32[16,2048]{1,0:T(8,128)S(1)}, u32[]{:S(2)}, u32[]{:S(2)}) collective-permute-start(f32[16,2048]{1,0:T(8,128)S(1)} %multiply_add_fusion.2), channel_id=1, source_target_pairs={{0,8},{8,16},{16,24},{24,32},{32,40},{40,48},{48,56},{56,64},{64,7... | collective-permute-start | bytes 393224 | tf_op jit(solution)/shard_map/while/body/eval_jaxpr/ppermute | solution.py:27
  317.7 7.8 %collective-permute-start = (f32[16,2048]{1,0:T(8,128)S(1)}, f32[16,2048]{1,0:T(8,128)S(1)}, u32[]{:S(2)}, u32[]{:S(2)}) collective-permute-start(f32[16,2048]{1,0:T(8,128)S(1)} %multiply_add_fusion.2), channel_id=1, source_target_pairs={{0,8},{8,16},{16,24},{24,32},{32,40},{40,48},{48,56},{56,64},{64,7... | collective-permute-start | bytes 393224 | tf_op jit(solution)/shard_map/while/body/eval_jaxpr/ppermute | solution.py:27
  325.7 9.0 %collective-permute-start = (f32[16,2048]{1,0:T(8,128)S(1)}, f32[16,2048]{1,0:T(8,128)S(1)}, u32[]{:S(2)}, u32[]{:S(2)}) collective-permute-start(f32[16,2048]{1,0:T(8,128)S(1)} %multiply_add_fusion.2), channel_id=1, source_target_pairs={{0,8},{8,16},{16,24},{24,32},{32,40},{40,48},{48,56},{56,64},{64,7... | collective-permute-start | bytes 393224 | tf_op jit(solution)/shard_map/while/body/eval_jaxpr/ppermute | solution.py:27
  334.9 8.1 %collective-permute-start = (f32[16,2048]{1,0:T(8,128)S(1)}, f32[16,2048]{1,0:T(8,128)S(1)}, u32[]{:S(2)}, u32[]{:S(2)}) collective-permute-start(f32[16,2048]{1,0:T(8,128)S(1)} %multiply_add_fusion.2), channel_id=1, source_target_pairs={{0,8},{8,16},{16,24},{24,32},{32,40},{40,48},{48,56},{56,64},{64,7... | collective-permute-start | bytes 393224 | tf_op jit(solution)/shard_map/while/body/eval_jaxpr/ppermute | solution.py:27
  343.2 7.8 %collective-permute-start = (f32[16,2048]{1,0:T(8,128)S(1)}, f32[16,2048]{1,0:T(8,128)S(1)}, u32[]{:S(2)}, u32[]{:S(2)}) collective-permute-start(f32[16,2048]{1,0:T(8,128)S(1)} %multiply_add_fusion.2), channel_id=1, source_target_pairs={{0,8},{8,16},{16,24},{24,32},{32,40},{40,48},{48,56},{56,64},{64,7... | collective-permute-start | bytes 393224 | tf_op jit(solution)/shard_map/while/body/eval_jaxpr/ppermute | solution.py:27
  351.2 7.8 %collective-permute-start = (f32[16,2048]{1,0:T(8,128)S(1)}, f32[16,2048]{1,0:T(8,128)S(1)}, u32[]{:S(2)}, u32[]{:S(2)}) collective-permute-start(f32[16,2048]{1,0:T(8,128)S(1)} %multiply_add_fusion.2), channel_id=1, source_target_pairs={{0,8},{8,16},{16,24},{24,32},{32,40},{40,48},{48,56},{56,64},{64,7... | collective-permute-start | bytes 393224 | tf_op jit(solution)/shard_map/while/body/eval_jaxpr/ppermute | solution.py:27
  359.2 7.8 %collective-permute-start = (f32[16,2048]{1,0:T(8,128)S(1)}, f32[16,2048]{1,0:T(8,128)S(1)}, u32[]{:S(2)}, u32[]{:S(2)}) collective-permute-start(f32[16,2048]{1,0:T(8,128)S(1)} %multiply_add_fusion.2), channel_id=1, source_target_pairs={{0,8},{8,16},{16,24},{24,32},{32,40},{40,48},{48,56},{56,64},{64,7... | collective-permute-start | bytes 393224 | tf_op jit(solution)/shard_map/while/body/eval_jaxpr/ppermute | solution.py:27
  367.2 7.8 %collective-permute-start = (f32[16,2048]{1,0:T(8,128)S(1)}, f32[16,2048]{1,0:T(8,128)S(1)}, u32[]{:S(2)}, u32[]{:S(2)}) collective-permute-start(f32[16,2048]{1,0:T(8,128)S(1)} %multiply_add_fusion.2), channel_id=1, source_target_pairs={{0,8},{8,16},{16,24},{24,32},{32,40},{40,48},{48,56},{56,64},{64,7... | collective-permute-start | bytes 393224 | tf_op jit(solution)/shard_map/while/body/eval_jaxpr/ppermute | solution.py:27
  375.2 7.8 %collective-permute-start = (f32[16,2048]{1,0:T(8,128)S(1)}, f32[16,2048]{1,0:T(8,128)S(1)}, u32[]{:S(2)}, u32[]{:S(2)}) collective-permute-start(f32[16,2048]{1,0:T(8,128)S(1)} %multiply_add_fusion.2), channel_id=1, source_target_pairs={{0,8},{8,16},{16,24},{24,32},{32,40},{40,48},{48,56},{56,64},{64,7... | collective-permute-start | bytes 393224 | tf_op jit(solution)/shard_map/while/body/eval_jaxpr/ppermute | solution.py:27
  383.2 8.1 %collective-permute-start = (f32[16,2048]{1,0:T(8,128)S(1)}, f32[16,2048]{1,0:T(8,128)S(1)}, u32[]{:S(2)}, u32[]{:S(2)}) collective-permute-start(f32[16,2048]{1,0:T(8,128)S(1)} %multiply_add_fusion.2), channel_id=1, source_target_pairs={{0,8},{8,16},{16,24},{24,32},{32,40},{40,48},{48,56},{56,64},{64,7... | collective-permute-start | bytes 393224 | tf_op jit(solution)/shard_map/while/body/eval_jaxpr/ppermute | solution.py:27
  391.4 9.4 %collective-permute-start = (f32[16,2048]{1,0:T(8,128)S(1)}, f32[16,2048]{1,0:T(8,128)S(1)}, u32[]{:S(2)}, u32[]{:S(2)}) collective-permute-start(f32[16,2048]{1,0:T(8,128)S(1)} %multiply_add_fusion.2), channel_id=1, source_target_pairs={{0,8},{8,16},{16,24},{24,32},{32,40},{40,48},{48,56},{56,64},{64,7... | collective-permute-start | bytes 393224 | tf_op jit(solution)/shard_map/while/body/eval_jaxpr/ppermute | solution.py:27
  401.0 8.7 %collective-permute-start = (f32[16,2048]{1,0:T(8,128)S(1)}, f32[16,2048]{1,0:T(8,128)S(1)}, u32[]{:S(2)}, u32[]{:S(2)}) collective-permute-start(f32[16,2048]{1,0:T(8,128)S(1)} %multiply_add_fusion.2), channel_id=1, source_target_pairs={{0,8},{8,16},{16,24},{24,32},{32,40},{40,48},{48,56},{56,64},{64,7... | collective-permute-start | bytes 393224 | tf_op jit(solution)/shard_map/while/body/eval_jaxpr/ppermute | solution.py:27
  409.9 7.8 %collective-permute-start = (f32[16,2048]{1,0:T(8,128)S(1)}, f32[16,2048]{1,0:T(8,128)S(1)}, u32[]{:S(2)}, u32[]{:S(2)}) collective-permute-start(f32[16,2048]{1,0:T(8,128)S(1)} %multiply_add_fusion.2), channel_id=1, source_target_pairs={{0,8},{8,16},{16,24},{24,32},{32,40},{40,48},{48,56},{56,64},{64,7... | collective-permute-start | bytes 393224 | tf_op jit(solution)/shard_map/while/body/eval_jaxpr/ppermute | solution.py:27
  417.8 7.8 %collective-permute-start = (f32[16,2048]{1,0:T(8,128)S(1)}, f32[16,2048]{1,0:T(8,128)S(1)}, u32[]{:S(2)}, u32[]{:S(2)}) collective-permute-start(f32[16,2048]{1,0:T(8,128)S(1)} %multiply_add_fusion.2), channel_id=1, source_target_pairs={{0,8},{8,16},{16,24},{24,32},{32,40},{40,48},{48,56},{56,64},{64,7... | collective-permute-start | bytes 393224 | tf_op jit(solution)/shard_map/while/body/eval_jaxpr/ppermute | solution.py:27
  425.8 7.8 %collective-permute-start = (f32[16,2048]{1,0:T(8,128)S(1)}, f32[16,2048]{1,0:T(8,128)S(1)}, u32[]{:S(2)}, u32[]{:S(2)}) collective-permute-start(f32[16,2048]{1,0:T(8,128)S(1)} %multiply_add_fusion.2), channel_id=1, source_target_pairs={{0,8},{8,16},{16,24},{24,32},{32,40},{40,48},{48,56},{56,64},{64,7... | collective-permute-start | bytes 393224 | tf_op jit(solution)/shard_map/while/body/eval_jaxpr/ppermute | solution.py:27
  433.8 7.8 %collective-permute-start = (f32[16,2048]{1,0:T(8,128)S(1)}, f32[16,2048]{1,0:T(8,128)S(1)}, u32[]{:S(2)}, u32[]{:S(2)}) collective-permute-start(f32[16,2048]{1,0:T(8,128)S(1)} %multiply_add_fusion.2), channel_id=1, source_target_pairs={{0,8},{8,16},{16,24},{24,32},{32,40},{40,48},{48,56},{56,64},{64,7... | collective-permute-start | bytes 393224 | tf_op jit(solution)/shard_map/while/body/eval_jaxpr/ppermute | solution.py:27
  441.8 7.8 %collective-permute-start = (f32[16,2048]{1,0:T(8,128)S(1)}, f32[16,2048]{1,0:T(8,128)S(1)}, u32[]{:S(2)}, u32[]{:S(2)}) collective-permute-start(f32[16,2048]{1,0:T(8,128)S(1)} %multiply_add_fusion.2), channel_id=1, source_target_pairs={{0,8},{8,16},{16,24},{24,32},{32,40},{40,48},{48,56},{56,64},{64,7... | collective-permute-start | bytes 393224 | tf_op jit(solution)/shard_map/while/body/eval_jaxpr/ppermute | solution.py:27
  449.8 7.8 %collective-permute-start = (f32[16,2048]{1,0:T(8,128)S(1)}, f32[16,2048]{1,0:T(8,128)S(1)}, u32[]{:S(2)}, u32[]{:S(2)}) collective-permute-start(f32[16,2048]{1,0:T(8,128)S(1)} %multiply_add_fusion.2), channel_id=1, source_target_pairs={{0,8},{8,16},{16,24},{24,32},{32,40},{40,48},{48,56},{56,64},{64,7... | collective-permute-start | bytes 393224 | tf_op jit(solution)/shard_map/while/body/eval_jaxpr/ppermute | solution.py:27
  457.8 8.7 %collective-permute-start = (f32[16,2048]{1,0:T(8,128)S(1)}, f32[16,2048]{1,0:T(8,128)S(1)}, u32[]{:S(2)}, u32[]{:S(2)}) collective-permute-start(f32[16,2048]{1,0:T(8,128)S(1)} %multiply_add_fusion.2), channel_id=1, source_target_pairs={{0,8},{8,16},{16,24},{24,32},{32,40},{40,48},{48,56},{56,64},{64,7... | collective-permute-start | bytes 393224 | tf_op jit(solution)/shard_map/while/body/eval_jaxpr/ppermute | solution.py:27
  466.6 8.9 %collective-permute-start = (f32[16,2048]{1,0:T(8,128)S(1)}, f32[16,2048]{1,0:T(8,128)S(1)}, u32[]{:S(2)}, u32[]{:S(2)}) collective-permute-start(f32[16,2048]{1,0:T(8,128)S(1)} %multiply_add_fusion.2), channel_id=1, source_target_pairs={{0,8},{8,16},{16,24},{24,32},{32,40},{40,48},{48,56},{56,64},{64,7... | collective-permute-start | bytes 393224 | tf_op jit(solution)/shard_map/while/body/eval_jaxpr/ppermute | solution.py:27
  475.7 7.8 %collective-permute-start = (f32[16,2048]{1,0:T(8,128)S(1)}, f32[16,2048]{1,0:T(8,128)S(1)}, u32[]{:S(2)}, u32[]{:S(2)}) collective-permute-start(f32[16,2048]{1,0:T(8,128)S(1)} %multiply_add_fusion.2), channel_id=1, source_target_pairs={{0,8},{8,16},{16,24},{24,32},{32,40},{40,48},{48,56},{56,64},{64,7... | collective-permute-start | bytes 393224 | tf_op jit(solution)/shard_map/while/body/eval_jaxpr/ppermute | solution.py:27
  483.7 7.8 %collective-permute-start = (f32[16,2048]{1,0:T(8,128)S(1)}, f32[16,2048]{1,0:T(8,128)S(1)}, u32[]{:S(2)}, u32[]{:S(2)}) collective-permute-start(f32[16,2048]{1,0:T(8,128)S(1)} %multiply_add_fusion.2), channel_id=1, source_target_pairs={{0,8},{8,16},{16,24},{24,32},{32,40},{40,48},{48,56},{56,64},{64,7... | collective-permute-start | bytes 393224 | tf_op jit(solution)/shard_map/while/body/eval_jaxpr/ppermute | solution.py:27
  (13 other events, 402.8 us)
where the time goes:
time: 584 us; the launch traced here: 583 us
  waiting for transfers between devices  277 us (47%)
  blocking collectives  79.1 us (14%)
  other arithmetic  71.6 us (12%)
  starting transfers between devices  63.8 us (11%)
  matrix products  58 us (10%)
  local copies, waits for them, and re-layouts  28.8 us (5%)
    ppermute x31, waiting for transfers between devices, shifted(): return lax.ppermute(array, axis, pairs)  203 us
    psum x1, blocking collectives, mamba_mix(): squares = lax.psum(jnp.sum(gated * gated, axis=1), 'tp')  79.1 us
    ppermute x31, waiting for transfers between devices, passed_along(): return lax.ppermute(value, axis, pairs)  73.8 us
    ppermute x31, starting transfers between devices, shifted(): return lax.ppermute(array, axis, pairs)  59.5 us
    dot_general x32, matrix products, flash_update(): jnp.einsum('kgts,skd->kgtd', expo.astype(jnp.bfloat16), value_rows, prefe...  30.9 us
    convert_element_type x31, other arithmetic, flash_update(): expo.astype(jnp.bfloat16)  22.4 us
    dot_general x32, matrix products, visit_keys(): jnp.einsum('tkgd,skd->kgts', query_rows, key_rows, preferred_element_type...  17.8 us
    reduce_or x32, other arithmetic, allowed_blocks(): jnp.any(offset[None, None, :, :, None] == slash_local[:, :, None, None, :...  14.6 us
  transfers between devices with their start and end apart: 62, of which 62 were waited for; matrix products, arithmetic and copies ran while one was open for 21% of the time, Pallas kernels for 0%

commit v1 on v0

v1 whole, which is shorter than its diff:
```python
import math

import jax
import jax.numpy as jnp
from jax import lax
from jax.experimental import pallas as pl
from jax.experimental.pallas import tpu as pltpu
from jax.sharding import PartitionSpec as P

HEAD_DIM = 128
SSM_HEAD_DIM = 64
D_STATE = 16
BLOCK = 64
INNER = 16384
NEG_FILL = -1e30


def shifted(array, axis, by):
    size = lax.axis_size(axis)
    pairs = [(i, i + by) for i in range(size) if 0 <= i + by < size]
    return lax.ppermute(array, axis, pairs)


def key_block_table(vertical, slash, block_position, blocks_here):
    my_index = lax.axis_index("ctx")
    total_blocks = block_position.shape[0]
    query_seq = lax.dynamic_slice_in_dim(block_position, my_index * blocks_here, blocks_here)
    storage_of = jnp.zeros((total_blocks,), jnp.int32).at[block_position].set(
        jnp.arange(total_blocks, dtype=jnp.int32)
    )
    heads = vertical.shape[0]
    br = query_seq[None, :, None]
    cand_v = jnp.broadcast_to(vertical[:, None, :], (heads, blocks_here, vertical.shape[1]))
    cand_s = br - slash[:, None, :]
    cand = jnp.concatenate([cand_v, cand_s], axis=-1)
    ok = jnp.concatenate([cand_v < br, cand_s >= 0], axis=-1)
    count = cand.shape[-1]
    earlier = jnp.arange(count)[None, :] < jnp.arange(count)[:, None]
    dup = jnp.any(
        (cand[..., :, None] == cand[..., None, :]) & ok[..., None, :] & earlier[None, None], axis=-1
    )
    ok = ok & ~dup
    diag = jnp.broadcast_to(query_seq[None, :, None], (heads, blocks_here, 1))
    cand = jnp.concatenate([diag, cand, jnp.zeros_like(diag)], axis=-1)
    ok = jnp.concatenate([jnp.ones_like(diag, bool), ok, jnp.zeros_like(diag, bool)], axis=-1)
    index = storage_of[jnp.clip(cand, 0, total_blocks - 1)]
    slots = cand.shape[-1]
    valid_cols = jnp.repeat(ok.astype(jnp.float32), BLOCK, axis=-1).reshape(heads * blocks_here, 1, slots * BLOCK)
    return index.reshape(-1).astype(jnp.int32), valid_cols, slots


def sparse_attention_kernel(slots, blocks_here, q_ref, kv_ref, idx_ref, valid_ref, o_ref, kbuf, vbuf):
    score_scale = 1.0 / math.sqrt(HEAD_DIM)
    width = slots * BLOCK
    units = valid_ref.shape[0]

    def unit(i, carry):
        head = i // blocks_here
        qblock = i % blocks_here
        for j in range(slots):
            src = pl.multiple_of(idx_ref[i * slots + j] * BLOCK, BLOCK)
            kbuf[pl.ds(j * BLOCK, BLOCK), :] = kv_ref[0, pl.ds(src, BLOCK), :]
            vbuf[pl.ds(j * BLOCK, BLOCK), :] = kv_ref[1, pl.ds(src, BLOCK), :]
        rows = pl.ds(pl.multiple_of(qblock * BLOCK, BLOCK), BLOCK)
        cols = pl.ds(pl.multiple_of(head * HEAD_DIM, HEAD_DIM), HEAD_DIM)
        q = q_ref[rows, cols]
        scores = lax.dot_general(
            q, kbuf[...], (((1,), (1,)), ((), ())), preferred_element_type=jnp.float32
        ) * score_scale
        r = lax.broadcasted_iota(jnp.int32, (BLOCK, width), 0)
        c = lax.broadcasted_iota(jnp.int32, (BLOCK, width), 1)
        allowed = ((c >= BLOCK) | (c <= r)) & (valid_ref[i] > 0.5)
        masked = jnp.where(allowed, scores, NEG_FILL)
        top = jnp.max(masked, axis=1, keepdims=True)
        expo = jnp.where(allowed, jnp.exp(masked - top), 0.0)
        denom = jnp.sum(expo, axis=1, keepdims=True)
        out = jnp.dot(expo.astype(jnp.bfloat16), vbuf[...], preferred_element_type=jnp.float32)
        o_ref[rows, cols] = (out / denom).astype(o_ref.dtype)
        return carry

    lax.fori_loop(0, units, unit, 0)


def attend_sparse(queries, keys, values, vertical, slash, block_position):
    row_count = queries.shape[0]
    blocks_here = row_count // BLOCK
    kv_all = lax.all_gather(jnp.stack((keys, values)), "ctx", axis=1, tiled=True)
    index, valid_cols, slots = key_block_table(vertical, slash, block_position, blocks_here)
    units = valid_cols.shape[0]
    flops = units * 4 * BLOCK * slots * BLOCK * HEAD_DIM
    return pl.pallas_call(
        lambda *refs: sparse_attention_kernel(slots, blocks_here, *refs),
        out_shape=jax.ShapeDtypeStruct(queries.shape, queries.dtype),
        in_specs=[
            pl.BlockSpec(memory_space=pltpu.VMEM),
            pl.BlockSpec(memory_space=pltpu.VMEM),
            pl.BlockSpec(memory_space=pltpu.SMEM),
            pl.BlockSpec(memory_space=pltpu.VMEM),
        ],
        out_specs=pl.BlockSpec(memory_space=pltpu.VMEM),
        scratch_shapes=[
            pltpu.VMEM((slots * BLOCK, HEAD_DIM), jnp.bfloat16),
            pltpu.VMEM((slots * BLOCK, HEAD_DIM), jnp.bfloat16),
        ],
        cost_estimate=pl.CostEstimate(
            flops=flops,
            transcendentals=units * BLOCK * slots * BLOCK,
            bytes_accessed=2 * queries.size * 2 + kv_all.size * 2,
        ),
    )(queries, kv_all, index, valid_cols)


def mamba_mix(ssm_input, gate, state_in, state_out, step_size, decay_log, skip_gain, norm_gain):
    careful = lax.Precision.HIGH
    row_count = ssm_input.shape[0]
    head_count = step_size.shape[1]
    inner_width = ssm_input.shape[1]
    inputs = ssm_input.astype(jnp.float32).reshape(row_count, head_count, SSM_HEAD_DIM)
    in_map = state_in.astype(jnp.float32)
    out_map = state_out.astype(jnp.float32)
    log_steps = -jnp.exp(decay_log)[None, :] * step_size
    cumulative = jnp.cumsum(log_steps, axis=0)
    grouped_per_head = cumulative.T
    lower = jnp.arange(row_count)[:, None] >= jnp.arange(row_count)[None, :]
    decay = jnp.where(
        lower[None],
        jnp.exp(jnp.minimum(grouped_per_head[:, :, None] - grouped_per_head[:, None, :], 0.0)),
        0.0,
    )
    inner = jnp.dot(state_out, state_in.T, preferred_element_type=jnp.float32)
    weighted = inputs * step_size[:, :, None]
    within = jnp.einsum("hts,shp->thp", decay * inner[None], weighted, precision=careful)
    tail = jnp.exp(cumulative[-1][None, :] - cumulative)
    local_state = jnp.einsum(
        "sn,shp->nhp", in_map, weighted * tail[:, :, None], precision=careful
    ).reshape(D_STATE, inner_width)
    carry_decay = jnp.repeat(jnp.exp(cumulative[-1]), SSM_HEAD_DIM)[None, :]

    packed = shifted(jnp.concatenate([carry_decay, local_state], axis=0), "ctx", 1)
    size = lax.axis_size("ctx")
    step = 1
    while step < size:
        got = shifted(packed, "ctx", step)
        factor = packed[0:1]
        packed = jnp.concatenate([factor * got[0:1], factor * got[1:] + packed[1:]], axis=0)
        step *= 2
    incoming = packed[1:]

    from_past = jnp.dot(
        out_map, incoming, precision=careful, preferred_element_type=jnp.float32
    ).reshape(row_count, head_count, SSM_HEAD_DIM)
    from_past = from_past * jnp.exp(cumulative)[:, :, None]
    mixed = (within + from_past + skip_gain[None, :, None] * inputs).reshape(row_count, inner_width)
    gate_full = gate.astype(jnp.float32)
    gated = mixed * gate_full * jax.nn.sigmoid(gate_full)
    squares = lax.psum(jnp.sum(gated * gated, axis=1), "tp")
    scaled = gated * lax.rsqrt(squares / INNER + 1e-05)[:, None] * norm_gain[None, :]
    return scaled.astype(jnp.bfloat16)


def local(
    queries,
    keys,
    values,
    vertical,
    slash,
    block_position,
    ssm_input,
    gate,
    state_in,
    state_out,
    step_size,
    decay_log,
    skip_gain,
    norm_gain,
):
    attention_out = attend_sparse(queries, keys, values, vertical, slash, block_position)
    recurrent_mixer_result = mamba_mix(
        ssm_input, gate, state_in, state_out, step_size, decay_log, skip_gain, norm_gain
    )
    return (attention_out, recurrent_mixer_result)


def solution(mesh):
    return jax.shard_map(
        local,
        mesh=mesh,
        in_specs=(
            P("ctx", "tp"),
            P("ctx", "tp"),
            P("ctx", "tp"),
            P("tp", None),
            P("tp", None),
            P(),
            P("ctx", "tp"),
            P("ctx", "tp"),
            P("ctx", None),
            P("ctx", None),
            P("ctx", "tp"),
            P("tp"),
            P("tp"),
            P("tp"),
        ),
        out_specs=(P("ctx", "tp"), P("ctx", "tp")),
        check_vma=False,
    )
```

time: 584 us -> 139 us (0.24)
  the two profiles are of different devices: /device:TPU:9 before, /device:TPU:1 now
where the time goes in v1:
time: 139 us; the launch traced here: 138 us
  starting transfers between devices  35.7 us (26%)
  waiting for transfers between devices  21.7 us (16%)
  Pallas kernels  21.1 us (15%)
  between operations  14.4 us (10%)
  blocking collectives  14.2 us (10%)
  local copies, waits for them, and re-layouts  13 us (9%)
  other arithmetic  9.07 us (7%)
  matrix products  8.57 us (6%)
    ppermute x6, starting transfers between devices, shifted(): return lax.ppermute(array, axis, pairs)  35.7 us
    ppermute x6, waiting for transfers between devices, shifted(): return lax.ppermute(array, axis, pairs)  21.6 us
    pallas_call x1, Pallas kernels, attend_sparse(): pl.pallas_call(lambda *refs: sparse_attention_kernel(slots, blocks_here,...  21.1 us
    psum x1, blocking collectives, mamba_mix(): squares = lax.psum(jnp.sum(gated * gated, axis=1), 'tp')  14.2 us
    dot_general x1, matrix products, mamba_mix(): jnp.einsum('hts,shp->thp', decay * inner[None], weighted, precision=careful)  6.66 us
    gather x1, local copies, waits for them, and re-layouts, key_block_table(): index = storage_of[jnp.clip(cand, 0, total_blocks - 1)]  5.48 us
  transfers between devices with their start and end apart: 7, of which 5 were waited for; matrix products, arithmetic and copies ran while one was open for 18% of the time, Pallas kernels for 0%

profile of v1, /device:TPU:1, one launch (start us, length us, event | category | flops | bytes accessed | tf_op | source)
XLA Modules:
  0.0 137.7 jit_solution(16430895531946577096)
XLA Ops:
  7.2 0.0 copy-start
  7.2 0.0 copy-start.3
  7.2 0.0 copy-start.7
  7.2 0.0 all-gather.2.cloned.1.call-start
  7.2 0.7 exponential_negate_fusion
  7.9 0.8 copy_bitcast_fusion.1
  8.7 0.6 reduce-window.6
  9.3 0.2 slice_reduce_fusion
  9.5 0.1 fusion.37
  9.6 0.2 slice_reduce_fusion.1
  9.8 0.1 bitcast_exponential_fusion
  9.9 1.5 %copy.36 = f32[256,2048]{0,1:T(8,128)S(1)} copy(bf16[256,2048]{1,0:T(8,128)(2,1)} %param.20) | data formatting | bytes 3145728 | tf_op jit(solution)/shard_map/reshape | solution.py:118
  11.4 0.0 copy-start.4
  11.4 0.0 copy-start.5
  11.4 0.0 copy-done.3
  11.4 0.0 copy-start.11
  11.5 0.0 copy-start.8
  11.5 0.9 fusion.20
  12.4 0.1 copy.39
  12.5 0.1 reshape.140
  12.6 0.1 broadcast_in_dim.37
  12.7 0.1 broadcast_in_dim_reshape.3
  12.8 4.4 %collective-permute-start = (f32[17,2048]{1,0:T(8,128)S(1)}, f32[17,2048]{1,0:T(8,128)S(1)}, u32[]{:S(2)}, u32[]{:S(2)}) collective-permute-start(f32[17,2048]{1,0:T(8,128)S(1)} %pad_maximum_fusion), channel_id=1, source_target_pairs={{0,8},{8,16},{16,24},{24,32},{32,40},{40,48},{48,56},{56,64},{64,7... | collective-permute-start | bytes 417800 | tf_op jit(solution)/shard_map/ppermute | solution.py:21
  17.2 0.7 pad_maximum_fusion.5
  17.9 0.0 all-gather.2.cloned.1.call-update
  18.0 0.2 fusion.38
  18.2 0.1 dynamic_slice.3
  18.3 0.1 broadcast_subtract_fusion
  18.3 6.7 %fusion = f32[32,64,256]{2,1,0:T(8,128)} fusion(f32[256,256]{1,0:T(8,128)S(1)} %fusion.38, f32[32,256]{1,0:T(8,128)S(1)} %get-tuple-element.7, pred[256,256]{1,0:T(8,128)(4,1)S(1)} %iota_compare_fusion, f32[256,32,64]{0,2,1:T(8,128)S(1)} %bitcast.54, f32[256,32]{0,1:T(8,128)S(1)} %copy-done.3), kind=kOutput, calls=%fused_computation.2 | convolution fusion | flops 814219264 | bytes 4587520 | tf_op jit(solution)/shard_map/hts,shp->thp/dot_general | solution.py:132
  25.0 0.1 broadcast_compare_fusion
  25.1 0.1 pad_add_fusion.1
  25.2 0.1 pad_add_fusion
  25.3 0.0 collective-permute-done
  25.3 3.5 %collective-permute-start.1 = (f32[17,2048]{1,0:T(8,128)S(1)}, f32[17,2048]{1,0:T(8,128)S(1)}, u32[]{:S(2)}, u32[]{:S(2)}) collective-permute-start(f32[17,2048]{1,0:T(8,128)S(1)} %collective-permute-done), channel_id=1, source_target_pairs={{0,8},{8,16},{16,24},{24,32},{32,40},{40,48},{48,56},{56,64},{64,7... | collective-permute-start | bytes 417800 | tf_op jit(solution)/shard_map/ppermute | solution.py:21
  28.9 0.1 pad.12.clone
  28.9 0.1 pad.20.clone
  29.0 0.8 and_reduce_fusion
  29.8 2.3 %collective-permute-done.1 = f32[17,2048]{1,0:T(8,128)S(1)} collective-permute-done((f32[17,2048]{1,0:T(8,128)S(1)}, f32[17,2048]{1,0:T(8,128)S(1)}, u32[]{:S(2)}, u32[]{:S(2)}) %collective-permute-start.1) | collective-permute-done | bytes 139296 | tf_op jit(solution)/shard_map/ppermute | solution.py:21
  32.1 6.1 %collective-permute-start.2 = (f32[17,2048]{1,0:T(8,128)S(1)}, f32[17,2048]{1,0:T(8,128)S(1)}, u32[]{:S(2)}, u32[]{:S(2)}) collective-permute-start(f32[17,2048]{1,0:T(8,128)S(1)} %pad_maximum_fusion.1), channel_id=1, source_target_pairs={{0,16},{8,24},{16,32},{24,40},{32,48},{40,56},{48,64},{56,72},{64,... | collective-permute-start | bytes 417800 | tf_op jit(solution)/shard_map/ppermute | solution.py:21
  38.2 0.1 not_and_fusion
  38.3 7.7 %collective-permute-done.2 = f32[17,2048]{1,0:T(8,128)S(1)} collective-permute-done((f32[17,2048]{1,0:T(8,128)S(1)}, f32[17,2048]{1,0:T(8,128)S(1)}, u32[]{:S(2)}, u32[]{:S(2)}) %collective-permute-start.2) | collective-permute-done | bytes 139296 | tf_op jit(solution)/shard_map/ppermute | solution.py:21
  46.1 11.6 %collective-permute-start.3 = (f32[17,2048]{1,0:T(8,128)S(1)}, f32[17,2048]{1,0:T(8,128)S(1)}, u32[]{:S(2)}, u32[]{:S(2)}) collective-permute-start(f32[17,2048]{1,0:T(8,128)S(1)} %pad_maximum_fusion.2), channel_id=1, source_target_pairs={{0,32},{8,40},{16,48},{24,56},{32,64},{40,72},{48,80},{56,88},{64,... | collective-permute-start | bytes 417800 | tf_op jit(solution)/shard_map/ppermute | solution.py:21
  57.7 0.1 add_convert_fusion
  57.8 8.9 %collective-permute-done.3 = f32[17,2048]{1,0:T(8,128)S(1)} collective-permute-done((f32[17,2048]{1,0:T(8,128)S(1)}, f32[17,2048]{1,0:T(8,128)S(1)}, u32[]{:S(2)}, u32[]{:S(2)}) %collective-permute-start.3) | collective-permute-done | bytes 139296 | tf_op jit(solution)/shard_map/ppermute | solution.py:21
  66.8 4.3 %collective-permute-start.4 = (f32[17,2048]{1,0:T(8,128)S(1)}, f32[17,2048]{1,0:T(8,128)S(1)}, u32[]{:S(2)}, u32[]{:S(2)}) collective-permute-start(f32[17,2048]{1,0:T(8,128)S(1)} %pad_maximum_fusion.3), channel_id=1, source_target_pairs={{0,64},{8,72},{16,80},{24,88},{32,96},{40,104},{48,112},{56,120},{... | collective-permute-start | bytes 417800 | tf_op jit(solution)/shard_map/ppermute | solution.py:21
  71.0 0.1 broadcast_in_dim.25
  71.1 0.1 compare_select_fusion
  71.2 2.6 %collective-permute-done.4 = f32[17,2048]{1,0:T(8,128)S(1)} collective-permute-done((f32[17,2048]{1,0:T(8,128)S(1)}, f32[17,2048]{1,0:T(8,128)S(1)}, u32[]{:S(2)}, u32[]{:S(2)}) %collective-permute-start.4) | collective-permute-done | bytes 139296 | tf_op jit(solution)/shard_map/ppermute | solution.py:21
  73.9 5.8 %collective-permute-start.5 = (f32[17,2048]{1,0:T(8,128)S(1)}, f32[17,2048]{1,0:T(8,128)S(1)}, u32[]{:S(2)}, u32[]{:S(2)}) collective-permute-start(f32[17,2048]{1,0:T(8,128)S(1)} %pad_maximum_fusion.4), channel_id=1, source_target_pairs={{0,128},{8,136},{16,144},{24,152},{32,160},{40,168},{48,176},{56,1... | collective-permute-start | bytes 417800 | tf_op jit(solution)/shard_map/ppermute | solution.py:21
  79.8 0.2 broadcast_in_dim.31
  79.9 0.9 reshape_reshape.4.refs_3_
  80.8 0.1 reshape.147
  80.9 1.0 scatter_custom_fusion
  81.9 5.5 %gather_fusion = s32[576]{0:T(1024)} fusion(s32[128]{0:T(128)S(1)} %scatter_custom_fusion, s32[1024]{0:T(1024)S(1)} %pad_clamp_fusion), kind=kCustom, calls=%fused_computation | custom fusion | bytes 6912 | tf_op jit(solution)/shard_map/gather | solution.py:46
  87.4 0.1 collective-permute-done.5
  87.4 0.8 fusion.27
  88.2 0.8 copy-done.2
  89.0 2.1 %fusion.15 = f32[256,32,64]{0,2,1:T(8,128)} fusion(f32[32,64,256]{2,1,0:T(8,128)S(1)} %copy-done.2, f32[256,32,64]{0,2,1:T(8,128)S(1)} %bitcast.55, f32[256,32,64]{0,2,1:T(8,128)S(1)} %bitcast.56, f32[32]{0:T(128)S(1)} %copy-done.10, f32[256,32]{0,1:T(8,128)S(1)} %get-tuple-element.4), kind=kLoop, calls=%fused_computation.20 | loop fusion | flops 2097152 | bytes 8421504 | tf_op jit(solution)/shard_map/add | solution.py:153
  91.0 2.1 %copy.40 = f32[256,2048]{1,0:T(8,128)S(1)} copy(f32[256,2048]{0,1:T(8,128)} %bitcast.57) | data formatting | bytes 4194304 | tf_op jit(solution)/shard_map/reshape | solution.py:153
  93.1 0.0 copy-start.9
  93.1 0.7 multiply_reduce_fusion
  93.8 14.2 %psum.7 = f32[256]{0:T(256)S(1)} all-reduce(f32[256]{0:T(256)S(1)} %multiply_reduce_fusion), channel_id=1, replica_groups=mesh['ctx'=32,'tp'=8] {'tp'}, use_global_device_ids=true, to_apply=%region_5.6 | all-reduce | flops 256 | bytes 2048 | tf_op jit(solution)/shard_map/psum | solution.py:156
  108.1 1.7 %multiply_convert_fusion = bf16[256,2048]{1,0:T(8,128)(2,1)} fusion(f32[2048]{0:T(1024)S(1)} %copy-done.9, f32[256]{0:T(256)S(1)} %add_rsqrt_fusion, f32[256,2048]{1,0:T(8,128)S(1)} %copy.40, bf16[256,2048]{1,0:T(8,128)(2,1)S(1)} %copy-done.1), kind=kLoop, calls=%fused_computation.21 | loop fusion | flops 4718592 | bytes 4203520 | tf_op jit(solution)/shard_map/convert_element_type | solution.py:158
  109.8 21.1 %shard_map.149 = bf16[256,1024]{1,0:T(8,128)(2,1)} custom-call(bf16[256,1024]{1,0:T(8,128)(2,1)} %refs_0_.1, bf16[2,8192,128]{2,1,0:T(8,128)(2,1)} %all-gather.2.cloned.1.call-done.refs_1_, s32[576]{0:T(1024)} %gather_fusion, f32[32,1,1152]{2,1,0:T(1,128)} %reshape_reshape.4.refs_3_), custom_call_target="tpu_custom_call" | custom-call | flops 1207959552 | bytes 5242880 | tf_op jit(solution)/shard_map/pallas_call | solution.py:91
  (40 shorter events, 0.4 us)
Async XLA Ops:
  7.2 10.8 %copy-start = (bf16[256,16]{0,1:T(8,128)(2,1)S(1)}, bf16[256,16]{0,1:T(8,128)(2,1)}, u32[]{:S(2)}) copy-start(bf16[256,16]{0,1:T(8,128)(2,1)} %param.23) | copy-start | bytes 24580
  7.2 4.2 %copy-start.3 = (f32[256,32]{0,1:T(8,128)S(1)}, f32[256,32]{0,1:T(8,128)}, u32[]{:S(2)}) copy-start(f32[256,32]{0,1:T(8,128)} %param.24) | copy-start | bytes 98308
  7.2 4.2 %copy-start.7 = (bf16[256,16]{0,1:T(8,128)(2,1)S(1)}, bf16[256,16]{0,1:T(8,128)(2,1)}, u32[]{:S(2)}) copy-start(bf16[256,16]{0,1:T(8,128)(2,1)} %param.22) | copy-start | bytes 24580
  7.2 102.6 %all-gather.2.cloned.1.call-start = ((), (), s32[]{:S(2)}) async-start(), calls=%async_computation | async-start | bytes 4325376 | tf_op jit(solution)/shard_map/all_gather | solution.py:87
  11.4 5.8 %copy-start.4 = (bf16[256,128]{1,0:T(8,128)(2,1)S(1)}, bf16[256,128]{1,0:T(8,128)(2,1)}, u32[]{:S(2)}) copy-start(bf16[256,128]{1,0:T(8,128)(2,1)} %param.16) | copy-start | bytes 196612
  11.4 5.8 %copy-start.5 = (bf16[256,128]{1,0:T(8,128)(2,1)S(1)}, bf16[256,128]{1,0:T(8,128)(2,1)}, u32[]{:S(2)}) copy-start(bf16[256,128]{1,0:T(8,128)(2,1)} %param.15) | copy-start | bytes 196612
  11.4 6.7 %copy-start.11 = (s32[128]{0:T(128)S(1)}, s32[128]{0:T(128)}, u32[]{:S(2)}) copy-start(s32[128]{0:T(128)} %param.19) | copy-start | bytes 1540
  11.5 6.8 %copy-start.8 = (s32[8,8]{1,0:T(8,128)S(1)}, s32[8,8]{1,0:T(8,128)}, u32[]{:S(2)}) copy-start(s32[8,8]{1,0:T(8,128)} %param.18) | copy-start | bytes 772
  12.8 12.5 %collective-permute-start = (f32[17,2048]{1,0:T(8,128)S(1)}, f32[17,2048]{1,0:T(8,128)S(1)}, u32[]{:S(2)}, u32[]{:S(2)}) collective-permute-start(f32[17,2048]{1,0:T(8,128)S(1)} %pad_maximum_fusion), channel_id=1, source_target_pairs={{0,8},{8,16},{16,24},{24,32},{32,40},{40,48},{48,56},{56,64},{64,7... | collective-permute-start | bytes 417800 | tf_op jit(solution)/shard_map/ppermute | solution.py:21
  18.3 6.7 %copy-start.6 = (s32[8,8]{1,0:T(8,128)S(1)}, s32[8,8]{1,0:T(8,128)}, u32[]{:S(2)}) copy-start(s32[8,8]{1,0:T(8,128)} %param.17) | copy-start | bytes 772
  25.3 6.8 %collective-permute-start.1 = (f32[17,2048]{1,0:T(8,128)S(1)}, f32[17,2048]{1,0:T(8,128)S(1)}, u32[]{:S(2)}, u32[]{:S(2)}) collective-permute-start(f32[17,2048]{1,0:T(8,128)S(1)} %collective-permute-done), channel_id=1, source_target_pairs={{0,8},{8,16},{16,24},{24,32},{32,40},{40,48},{48,56},{56,64},{64,7... | collective-permute-start | bytes 417800 | tf_op jit(solution)/shard_map/ppermute | solution.py:21
  32.1 13.9 %collective-permute-start.2 = (f32[17,2048]{1,0:T(8,128)S(1)}, f32[17,2048]{1,0:T(8,128)S(1)}, u32[]{:S(2)}, u32[]{:S(2)}) collective-permute-start(f32[17,2048]{1,0:T(8,128)S(1)} %pad_maximum_fusion.1), channel_id=1, source_target_pairs={{0,16},{8,24},{16,32},{24,40},{32,48},{40,56},{48,64},{56,72},{64,... | collective-permute-start | bytes 417800 | tf_op jit(solution)/shard_map/ppermute | solution.py:21
  46.1 20.6 %collective-permute-start.3 = (f32[17,2048]{1,0:T(8,128)S(1)}, f32[17,2048]{1,0:T(8,128)S(1)}, u32[]{:S(2)}, u32[]{:S(2)}) collective-permute-start(f32[17,2048]{1,0:T(8,128)S(1)} %pad_maximum_fusion.2), channel_id=1, source_target_pairs={{0,32},{8,40},{16,48},{24,56},{32,64},{40,72},{48,80},{56,88},{64,... | collective-permute-start | bytes 417800 | tf_op jit(solution)/shard_map/ppermute | solution.py:21
  66.8 7.1 %collective-permute-start.4 = (f32[17,2048]{1,0:T(8,128)S(1)}, f32[17,2048]{1,0:T(8,128)S(1)}, u32[]{:S(2)}, u32[]{:S(2)}) collective-permute-start(f32[17,2048]{1,0:T(8,128)S(1)} %pad_maximum_fusion.3), channel_id=1, source_target_pairs={{0,64},{8,72},{16,80},{24,88},{32,96},{40,104},{48,112},{56,120},{... | collective-permute-start | bytes 417800 | tf_op jit(solution)/shard_map/ppermute | solution.py:21
  73.9 13.5 %collective-permute-start.5 = (f32[17,2048]{1,0:T(8,128)S(1)}, f32[17,2048]{1,0:T(8,128)S(1)}, u32[]{:S(2)}, u32[]{:S(2)}) collective-permute-start(f32[17,2048]{1,0:T(8,128)S(1)} %pad_maximum_fusion.4), channel_id=1, source_target_pairs={{0,128},{8,136},{16,144},{24,152},{32,160},{40,168},{48,176},{56,1... | collective-permute-start | bytes 417800 | tf_op jit(solution)/shard_map/ppermute | solution.py:21
  87.4 1.6 %copy-start.2 = (f32[32,64,256]{2,1,0:T(8,128)S(1)}, f32[32,64,256]{2,1,0:T(8,128)}, u32[]{:S(2)}) copy-start(f32[32,64,256]{2,1,0:T(8,128)} %fusion) | copy-start | bytes 6291460
  87.4 1.6 %copy-start.10 = (f32[32]{0:T(128)S(1)}, f32[32]{0:T(128)}, u32[]{:S(2)}) copy-start(f32[32]{0:T(128)} %param.26) | copy-start | bytes 388
  91.0 2.1 %copy-start.1 = (bf16[256,2048]{1,0:T(8,128)(2,1)S(1)}, bf16[256,2048]{1,0:T(8,128)(2,1)}, u32[]{:S(2)}) copy-start(bf16[256,2048]{1,0:T(8,128)(2,1)} %param.21) | copy-start | bytes 3145732
  93.1 15.0 %copy-start.9 = (f32[2048]{0:T(1024)S(1)}, f32[2048]{0:T(1024)}, u32[]{:S(2)}) copy-start(f32[2048]{0:T(1024)} %param.27) | copy-start | bytes 24580
Sparse Core Ops, SparseCore 0:
  18.0 89.8 all-gather.1

commit v2 on v1

--- a/solution.py
+++ b/solution.py
@@ -45,14 +45,14 @@
     ok = jnp.concatenate([jnp.ones_like(diag, bool), ok, jnp.zeros_like(diag, bool)], axis=-1)
     index = storage_of[jnp.clip(cand, 0, total_blocks - 1)]
     slots = cand.shape[-1]
-    valid_cols = jnp.repeat(ok.astype(jnp.float32), BLOCK, axis=-1).reshape(heads * blocks_here, 1, slots * BLOCK)
-    return index.reshape(-1).astype(jnp.int32), valid_cols, slots
-
-
-def sparse_attention_kernel(slots, blocks_here, q_ref, kv_ref, idx_ref, valid_ref, o_ref, kbuf, vbuf):
+    col_bias = jnp.where(ok, 0.0, NEG_FILL).astype(jnp.float32)
+    col_bias = jnp.repeat(col_bias, BLOCK, axis=-1).reshape(heads * blocks_here, 1, slots * BLOCK)
+    return index.reshape(-1).astype(jnp.int32), col_bias, slots
+
+
+def sparse_attention_kernel(slots, blocks_here, q_ref, kv_ref, idx_ref, bias_ref, causal_ref, o_ref, kbuf, vbuf):
     score_scale = 1.0 / math.sqrt(HEAD_DIM)
-    width = slots * BLOCK
-    units = valid_ref.shape[0]
+    units = bias_ref.shape[0]
 
     def unit(i, carry):
         head = i // blocks_here
@@ -67,26 +67,26 @@
         scores = lax.dot_general(
             q, kbuf[...], (((1,), (1,)), ((), ())), preferred_element_type=jnp.float32
         ) * score_scale
-        r = lax.broadcasted_iota(jnp.int32, (BLOCK, width), 0)
-        c = lax.broadcasted_iota(jnp.int32, (BLOCK, width), 1)
-        allowed = ((c >= BLOCK) | (c <= r)) & (valid_ref[i] > 0.5)
-        masked = jnp.where(allowed, scores, NEG_FILL)
+        masked = scores + causal_ref[...] + bias_ref[i]
         top = jnp.max(masked, axis=1, keepdims=True)
-        expo = jnp.where(allowed, jnp.exp(masked - top), 0.0)
+        expo = jnp.exp(masked - top)
         denom = jnp.sum(expo, axis=1, keepdims=True)
         out = jnp.dot(expo.astype(jnp.bfloat16), vbuf[...], preferred_element_type=jnp.float32)
         o_ref[rows, cols] = (out / denom).astype(o_ref.dtype)
         return carry
 
-    lax.fori_loop(0, units, unit, 0)
+    lax.fori_loop(0, units, unit, 0, unroll=4)
 
 
 def attend_sparse(queries, keys, values, vertical, slash, block_position):
     row_count = queries.shape[0]
     blocks_here = row_count // BLOCK
     kv_all = lax.all_gather(jnp.stack((keys, values)), "ctx", axis=1, tiled=True)
-    index, valid_cols, slots = key_block_table(vertical, slash, block_position, blocks_here)
-    units = valid_cols.shape[0]
+    index, col_bias, slots = key_block_table(vertical, slash, block_position, blocks_here)
+    units = col_bias.shape[0]
+    r = lax.broadcasted_iota(jnp.int32, (BLOCK, slots * BLOCK), 0)
+    c = lax.broadcasted_iota(jnp.int32, (BLOCK, slots * BLOCK), 1)
+    causal_bias = jnp.where((c < BLOCK) & (c > r), NEG_FILL, 0.0).astype(jnp.float32)
     flops = units * 4 * BLOCK * slots * BLOCK * HEAD_DIM
     return pl.pallas_call(
         lambda *refs: sparse_attention_kernel(slots, blocks_here, *refs),
@@ -95,6 +95,7 @@
             pl.BlockSpec(memory_space=pltpu.VMEM),
             pl.BlockSpec(memory_space=pltpu.VMEM),
             pl.BlockSpec(memory_space=pltpu.SMEM),
+            pl.BlockSpec(memory_space=pltpu.VMEM),
             pl.BlockSpec(memory_space=pltpu.VMEM),
         ],
         out_specs=pl.BlockSpec(memory_space=pltpu.VMEM),
@@ -107,7 +108,7 @@
             transcendentals=units * BLOCK * slots * BLOCK,
             bytes_accessed=2 * queries.size * 2 + kv_all.size * 2,
         ),
-    )(queries, kv_all, index, valid_cols)
+    )(queries, kv_all, index, col_bias, causal_bias)
 
 
 def mamba_mix(ssm_input, gate, state_in, state_out, step_size, decay_log, skip_gain, norm_gain):

time: 139 us -> 140 us (level)
  Pallas kernels: 21.1 us -> 16.9 us
  waiting for transfers between devices: 21.7 us -> 24 us
  blocking collectives: 14.2 us -> 16.1 us
    pallas_call x1, Pallas kernels: 21.1 us -> 16.9 us  [attend_sparse(): pl.pallas_call(lambda *refs: sparse_attention_kernel(slots, blocks_here,...]
    ppermute x6, waiting for transfers between devices: 21.6 us -> 23.9 us  [shifted(): return lax.ppermute(array, axis, pairs)]
    psum x1, blocking collectives: 14.2 us -> 16.1 us  [mamba_mix(): squares = lax.psum(jnp.sum(gated * gated, axis=1), 'tp')]
  transfers between devices with their start and end apart: 7 -> 7, of which waited for: 5 -> 4; matrix products, arithmetic and copies ran while one was open for 18% -> 18% of each run, Pallas kernels for 0% -> 0%
where the time goes in v2:
time: 140 us; the launch traced here: 139 us
  starting transfers between devices  36.6 us (26%)
  waiting for transfers between devices  24 us (17%)
  Pallas kernels  16.9 us (12%)
  blocking collectives  16.1 us (12%)
  between operations  14.4 us (10%)
  local copies, waits for them, and re-layouts  13.1 us (9%)
  other arithmetic  9.83 us (7%)
  matrix products  8.57 us (6%)
    ppermute x6, starting transfers between devices, shifted(): return lax.ppermute(array, axis, pairs)  36.5 us
    ppermute x6, waiting for transfers between devices, shifted(): return lax.ppermute(array, axis, pairs)  23.9 us
    pallas_call x1, Pallas kernels, attend_sparse(): pl.pallas_call(lambda *refs: sparse_attention_kernel(slots, blocks_here,...  16.9 us
    psum x1, blocking collectives, mamba_mix(): squares = lax.psum(jnp.sum(gated * gated, axis=1), 'tp')  16.1 us
    dot_general x1, matrix products, mamba_mix(): jnp.einsum('hts,shp->thp', decay * inner[None], weighted, precision=careful)  6.66 us
    gather x1, local copies, waits for them, and re-layouts, key_block_table(): index = storage_of[jnp.clip(cand, 0, total_blocks - 1)]  5.47 us
  transfers between devices with their start and end apart: 7, of which 4 were waited for; matrix products, arithmetic and copies ran while one was open for 18% of the time, Pallas kernels for 0%

profile of v2, /device:TPU:1, one launch (start us, length us, event | category | flops | bytes accessed | tf_op | source)
XLA Modules:
  0.0 139.4 jit_solution(6421334869151126382)
XLA Ops:
  7.2 0.0 copy-start
  7.2 0.0 copy-start.3
  7.2 0.0 copy-start.7
  7.2 0.0 all-gather.2.cloned.1.call-start
  7.2 0.7 exponential_negate_fusion
  7.9 0.8 copy_bitcast_fusion.1
  8.7 0.6 reduce-window.6
  9.3 0.2 slice_reduce_fusion
  9.5 0.1 fusion.39
  9.6 0.2 slice_reduce_fusion.1
  9.8 0.1 bitcast_exponential_fusion
  9.9 1.5 %copy.36 = f32[256,2048]{0,1:T(8,128)S(1)} copy(bf16[256,2048]{1,0:T(8,128)(2,1)} %param.20) | data formatting | bytes 3145728 | tf_op jit(solution)/shard_map/reshape | solution.py:119
  11.4 0.0 copy-start.4
  11.4 0.0 copy-start.5
  11.4 0.0 copy-start.11
  11.5 0.0 copy-start.8
  11.5 0.9 fusion.20
  12.4 0.1 copy.39
  12.5 0.1 reshape.140
  12.6 0.1 broadcast_in_dim.93
  12.7 0.1 broadcast_in_dim_reshape.3
  12.8 4.4 %collective-permute-start = (f32[17,2048]{1,0:T(8,128)S(1)}, f32[17,2048]{1,0:T(8,128)S(1)}, u32[]{:S(2)}, u32[]{:S(2)}) collective-permute-start(f32[17,2048]{1,0:T(8,128)S(1)} %pad_maximum_fusion), channel_id=1, source_target_pairs={{0,8},{8,16},{16,24},{24,32},{32,40},{40,48},{48,56},{56,64},{64,7... | collective-permute-start | bytes 417800 | tf_op jit(solution)/shard_map/ppermute | solution.py:21
  17.2 0.7 pad_maximum_fusion.5
  17.9 0.0 all-gather.2.cloned.1.call-update
  18.0 0.2 fusion.40
  18.2 0.8 fusion.27.refs_4_
  18.9 0.1 dynamic_slice.3
  19.0 0.1 broadcast_subtract_fusion
  19.1 6.7 %fusion = f32[32,64,256]{2,1,0:T(8,128)} fusion(f32[256,256]{1,0:T(8,128)S(1)} %fusion.40, f32[32,256]{1,0:T(8,128)S(1)} %get-tuple-element.7, pred[256,256]{1,0:T(8,128)(4,1)S(1)} %iota_compare_fusion.1, f32[256,32,64]{0,2,1:T(8,128)S(1)} %bitcast.54, f32[256,32]{0,1:T(8,128)S(1)} %copy-done.3), kind=kOutput, calls=%fused_computation.2 | convolution fusion | flops 814219264 | bytes 4587520 | tf_op jit(solution)/shard_map/hts,shp->thp/dot_general | solution.py:133
  25.8 0.1 broadcast_compare_fusion
  25.9 0.1 pad_add_fusion.1
  25.9 0.1 pad_add_fusion
  26.0 0.0 collective-permute-done
  26.0 3.5 %collective-permute-start.1 = (f32[17,2048]{1,0:T(8,128)S(1)}, f32[17,2048]{1,0:T(8,128)S(1)}, u32[]{:S(2)}, u32[]{:S(2)}) collective-permute-start(f32[17,2048]{1,0:T(8,128)S(1)} %collective-permute-done), channel_id=1, source_target_pairs={{0,8},{8,16},{16,24},{24,32},{32,40},{40,48},{48,56},{56,64},{64,7... | collective-permute-start | bytes 417800 | tf_op jit(solution)/shard_map/ppermute | solution.py:21
  29.6 0.1 pad.12.clone
  29.7 0.1 pad.20.clone
  29.8 0.8 and_reduce_fusion
  30.5 2.3 %collective-permute-done.1 = f32[17,2048]{1,0:T(8,128)S(1)} collective-permute-done((f32[17,2048]{1,0:T(8,128)S(1)}, f32[17,2048]{1,0:T(8,128)S(1)}, u32[]{:S(2)}, u32[]{:S(2)}) %collective-permute-start.1) | collective-permute-done | bytes 139296 | tf_op jit(solution)/shard_map/ppermute | solution.py:21
  32.9 6.9 %collective-permute-start.2 = (f32[17,2048]{1,0:T(8,128)S(1)}, f32[17,2048]{1,0:T(8,128)S(1)}, u32[]{:S(2)}, u32[]{:S(2)}) collective-permute-start(f32[17,2048]{1,0:T(8,128)S(1)} %pad_maximum_fusion.1), channel_id=1, source_target_pairs={{0,16},{8,24},{16,32},{24,40},{32,48},{40,56},{48,64},{56,72},{64,... | collective-permute-start | bytes 417800 | tf_op jit(solution)/shard_map/ppermute | solution.py:21
  39.7 0.1 not_and_fusion
  39.8 9.5 %collective-permute-done.2 = f32[17,2048]{1,0:T(8,128)S(1)} collective-permute-done((f32[17,2048]{1,0:T(8,128)S(1)}, f32[17,2048]{1,0:T(8,128)S(1)}, u32[]{:S(2)}, u32[]{:S(2)}) %collective-permute-start.2) | collective-permute-done | bytes 139296 | tf_op jit(solution)/shard_map/ppermute | solution.py:21
  49.4 9.3 %collective-permute-start.3 = (f32[17,2048]{1,0:T(8,128)S(1)}, f32[17,2048]{1,0:T(8,128)S(1)}, u32[]{:S(2)}, u32[]{:S(2)}) collective-permute-start(f32[17,2048]{1,0:T(8,128)S(1)} %pad_maximum_fusion.2), channel_id=1, source_target_pairs={{0,32},{8,40},{16,48},{24,56},{32,64},{40,72},{48,80},{56,88},{64,... | collective-permute-start | bytes 417800 | tf_op jit(solution)/shard_map/ppermute | solution.py:21
  58.7 0.1 add_select_fusion
  58.8 8.2 %collective-permute-done.3 = f32[17,2048]{1,0:T(8,128)S(1)} collective-permute-done((f32[17,2048]{1,0:T(8,128)S(1)}, f32[17,2048]{1,0:T(8,128)S(1)}, u32[]{:S(2)}, u32[]{:S(2)}) %collective-permute-start.3) | collective-permute-done | bytes 139296 | tf_op jit(solution)/shard_map/ppermute | solution.py:21
  67.1 6.7 %collective-permute-start.4 = (f32[17,2048]{1,0:T(8,128)S(1)}, f32[17,2048]{1,0:T(8,128)S(1)}, u32[]{:S(2)}, u32[]{:S(2)}) collective-permute-start(f32[17,2048]{1,0:T(8,128)S(1)} %pad_maximum_fusion.3), channel_id=1, source_target_pairs={{0,64},{8,72},{16,80},{24,88},{32,96},{40,104},{48,112},{56,120},{... | collective-permute-start | bytes 417800 | tf_op jit(solution)/shard_map/ppermute | solution.py:21
  73.8 0.1 broadcast_in_dim.45
  73.9 0.1 compare_select_fusion
  74.0 3.9 %collective-permute-done.4 = f32[17,2048]{1,0:T(8,128)S(1)} collective-permute-done((f32[17,2048]{1,0:T(8,128)S(1)}, f32[17,2048]{1,0:T(8,128)S(1)}, u32[]{:S(2)}, u32[]{:S(2)}) %collective-permute-start.4) | collective-permute-done | bytes 139296 | tf_op jit(solution)/shard_map/ppermute | solution.py:21
  78.0 5.7 %collective-permute-start.5 = (f32[17,2048]{1,0:T(8,128)S(1)}, f32[17,2048]{1,0:T(8,128)S(1)}, u32[]{:S(2)}, u32[]{:S(2)}) collective-permute-start(f32[17,2048]{1,0:T(8,128)S(1)} %pad_maximum_fusion.4), channel_id=1, source_target_pairs={{0,128},{8,136},{16,144},{24,152},{32,160},{40,168},{48,176},{56,1... | collective-permute-start | bytes 417800 | tf_op jit(solution)/shard_map/ppermute | solution.py:21
  83.7 0.2 broadcast_in_dim.89
  83.9 0.9 reshape_reshape.4.refs_3_
  84.8 0.1 reshape.147
  84.9 1.0 scatter_custom_fusion
  85.9 5.5 %gather_fusion = s32[576]{0:T(1024)} fusion(s32[128]{0:T(128)S(1)} %scatter_custom_fusion, s32[1024]{0:T(1024)S(1)} %pad_clamp_fusion), kind=kCustom, calls=%fused_computation | custom fusion | bytes 6912 | tf_op jit(solution)/shard_map/gather | solution.py:46
  91.4 0.0 collective-permute-done.5
  91.4 0.8 fusion.29
  92.1 0.9 copy-done.2
  93.0 2.1 %fusion.15 = f32[256,32,64]{0,2,1:T(8,128)} fusion(f32[32,64,256]{2,1,0:T(8,128)S(1)} %copy-done.2, f32[256,32,64]{0,2,1:T(8,128)S(1)} %bitcast.55, f32[256,32,64]{0,2,1:T(8,128)S(1)} %bitcast.56, f32[32]{0:T(128)S(1)} %copy-done.10, f32[256,32]{0,1:T(8,128)S(1)} %get-tuple-element.4), kind=kLoop, calls=%fused_computation.20 | loop fusion | flops 2097152 | bytes 8421504 | tf_op jit(solution)/shard_map/add | solution.py:154
  95.1 2.0 %copy.40 = f32[256,2048]{1,0:T(8,128)S(1)} copy(f32[256,2048]{0,1:T(8,128)} %bitcast.57) | data formatting | bytes 4194304 | tf_op jit(solution)/shard_map/reshape | solution.py:154
  97.2 0.0 copy-start.9
  97.2 0.7 multiply_reduce_fusion
  97.9 16.1 %psum.7 = f32[256]{0:T(256)S(1)} all-reduce(f32[256]{0:T(256)S(1)} %multiply_reduce_fusion), channel_id=1, replica_groups=mesh['ctx'=32,'tp'=8] {'tp'}, use_global_device_ids=true, to_apply=%region_5.6 | all-reduce | flops 256 | bytes 2048 | tf_op jit(solution)/shard_map/psum | solution.py:157
  114.0 1.7 %multiply_convert_fusion = bf16[256,2048]{1,0:T(8,128)(2,1)} fusion(f32[2048]{0:T(1024)S(1)} %copy-done.9, f32[256]{0:T(256)S(1)} %add_rsqrt_fusion, f32[256,2048]{1,0:T(8,128)S(1)} %copy.40, bf16[256,2048]{1,0:T(8,128)(2,1)S(1)} %copy-done.1), kind=kLoop, calls=%fused_computation.21 | loop fusion | flops 4718592 | bytes 4203520 | tf_op jit(solution)/shard_map/convert_element_type | solution.py:159
  115.7 16.9 %shard_map.149 = bf16[256,1024]{1,0:T(8,128)(2,1)} custom-call(bf16[256,1024]{1,0:T(8,128)(2,1)} %refs_0_.1, bf16[2,8192,128]{2,1,0:T(8,128)(2,1)} %all-gather.2.cloned.1.call-done.refs_1_, s32[576]{0:T(1024)} %gather_fusion, f32[32,1,1152]{2,1,0:T(1,128)} %reshape_reshape.4.refs_3_, f32[64,1152]{1,0:T(8,128)} %fusion.27.refs_4_), custom_call_target="tpu_custom_call" | custom-call | flops 1207959552 | bytes 5242880 | tf_op jit(solution)/shard_map/pallas_call | solution.py:91
  (42 shorter events, 0.4 us)
Async XLA Ops:
  7.2 10.8 %copy-start = (bf16[256,16]{0,1:T(8,128)(2,1)S(1)}, bf16[256,16]{0,1:T(8,128)(2,1)}, u32[]{:S(2)}) copy-start(bf16[256,16]{0,1:T(8,128)(2,1)} %param.23) | copy-start | bytes 24580
  7.2 4.2 %copy-start.3 = (f32[256,32]{0,1:T(8,128)S(1)}, f32[256,32]{0,1:T(8,128)}, u32[]{:S(2)}) copy-start(f32[256,32]{0,1:T(8,128)} %param.24) | copy-start | bytes 98308
  7.2 4.2 %copy-start.7 = (bf16[256,16]{0,1:T(8,128)(2,1)S(1)}, bf16[256,16]{0,1:T(8,128)(2,1)}, u32[]{:S(2)}) copy-start(bf16[256,16]{0,1:T(8,128)(2,1)} %param.22) | copy-start | bytes 24580
  7.2 108.5 %all-gather.2.cloned.1.call-start = ((), (), s32[]{:S(2)}) async-start(), calls=%async_computation | async-start | bytes 4325376 | tf_op jit(solution)/shard_map/all_gather | solution.py:84
  11.4 5.8 %copy-start.4 = (bf16[256,128]{1,0:T(8,128)(2,1)S(1)}, bf16[256,128]{1,0:T(8,128)(2,1)}, u32[]{:S(2)}) copy-start(bf16[256,128]{1,0:T(8,128)(2,1)} %param.16) | copy-start | bytes 196612
  11.4 5.8 %copy-start.5 = (bf16[256,128]{1,0:T(8,128)(2,1)S(1)}, bf16[256,128]{1,0:T(8,128)(2,1)}, u32[]{:S(2)}) copy-start(bf16[256,128]{1,0:T(8,128)(2,1)} %param.15) | copy-start | bytes 196612
  11.4 7.5 %copy-start.11 = (s32[128]{0:T(128)S(1)}, s32[128]{0:T(128)}, u32[]{:S(2)}) copy-start(s32[128]{0:T(128)} %param.19) | copy-start | bytes 1540
  11.5 7.6 %copy-start.8 = (s32[8,8]{1,0:T(8,128)S(1)}, s32[8,8]{1,0:T(8,128)}, u32[]{:S(2)}) copy-start(s32[8,8]{1,0:T(8,128)} %param.18) | copy-start | bytes 772
  12.8 13.2 %collective-permute-start = (f32[17,2048]{1,0:T(8,128)S(1)}, f32[17,2048]{1,0:T(8,128)S(1)}, u32[]{:S(2)}, u32[]{:S(2)}) collective-permute-start(f32[17,2048]{1,0:T(8,128)S(1)} %pad_maximum_fusion), channel_id=1, source_target_pairs={{0,8},{8,16},{16,24},{24,32},{32,40},{40,48},{48,56},{56,64},{64,7... | collective-permute-start | bytes 417800 | tf_op jit(solution)/shard_map/ppermute | solution.py:21
  19.1 6.7 %copy-start.6 = (s32[8,8]{1,0:T(8,128)S(1)}, s32[8,8]{1,0:T(8,128)}, u32[]{:S(2)}) copy-start(s32[8,8]{1,0:T(8,128)} %param.17) | copy-start | bytes 772
  26.0 6.8 %collective-permute-start.1 = (f32[17,2048]{1,0:T(8,128)S(1)}, f32[17,2048]{1,0:T(8,128)S(1)}, u32[]{:S(2)}, u32[]{:S(2)}) collective-permute-start(f32[17,2048]{1,0:T(8,128)S(1)} %collective-permute-done), channel_id=1, source_target_pairs={{0,8},{8,16},{16,24},{24,32},{32,40},{40,48},{48,56},{56,64},{64,7... | collective-permute-start | bytes 417800 | tf_op jit(solution)/shard_map/ppermute | solution.py:21
  32.9 16.5 %collective-permute-start.2 = (f32[17,2048]{1,0:T(8,128)S(1)}, f32[17,2048]{1,0:T(8,128)S(1)}, u32[]{:S(2)}, u32[]{:S(2)}) collective-permute-start(f32[17,2048]{1,0:T(8,128)S(1)} %pad_maximum_fusion.1), channel_id=1, source_target_pairs={{0,16},{8,24},{16,32},{24,40},{32,48},{40,56},{48,64},{56,72},{64,... | collective-permute-start | bytes 417800 | tf_op jit(solution)/shard_map/ppermute | solution.py:21
  49.4 17.6 %collective-permute-start.3 = (f32[17,2048]{1,0:T(8,128)S(1)}, f32[17,2048]{1,0:T(8,128)S(1)}, u32[]{:S(2)}, u32[]{:S(2)}) collective-permute-start(f32[17,2048]{1,0:T(8,128)S(1)} %pad_maximum_fusion.2), channel_id=1, source_target_pairs={{0,32},{8,40},{16,48},{24,56},{32,64},{40,72},{48,80},{56,88},{64,... | collective-permute-start | bytes 417800 | tf_op jit(solution)/shard_map/ppermute | solution.py:21
  67.1 10.8 %collective-permute-start.4 = (f32[17,2048]{1,0:T(8,128)S(1)}, f32[17,2048]{1,0:T(8,128)S(1)}, u32[]{:S(2)}, u32[]{:S(2)}) collective-permute-start(f32[17,2048]{1,0:T(8,128)S(1)} %pad_maximum_fusion.3), channel_id=1, source_target_pairs={{0,64},{8,72},{16,80},{24,88},{32,96},{40,104},{48,112},{56,120},{... | collective-permute-start | bytes 417800 | tf_op jit(solution)/shard_map/ppermute | solution.py:21
  78.0 13.3 %collective-permute-start.5 = (f32[17,2048]{1,0:T(8,128)S(1)}, f32[17,2048]{1,0:T(8,128)S(1)}, u32[]{:S(2)}, u32[]{:S(2)}) collective-permute-start(f32[17,2048]{1,0:T(8,128)S(1)} %pad_maximum_fusion.4), channel_id=1, source_target_pairs={{0,128},{8,136},{16,144},{24,152},{32,160},{40,168},{48,176},{56,1... | collective-permute-start | bytes 417800 | tf_op jit(solution)/shard_map/ppermute | solution.py:21
  91.3 1.7 %copy-start.2 = (f32[32,64,256]{2,1,0:T(8,128)S(1)}, f32[32,64,256]{2,1,0:T(8,128)}, u32[]{:S(2)}) copy-start(f32[32,64,256]{2,1,0:T(8,128)} %fusion) | copy-start | bytes 6291460
  91.4 1.7 %copy-start.10 = (f32[32]{0:T(128)S(1)}, f32[32]{0:T(128)}, u32[]{:S(2)}) copy-start(f32[32]{0:T(128)} %param.26) | copy-start | bytes 388
  95.1 2.1 %copy-start.1 = (bf16[256,2048]{1,0:T(8,128)(2,1)S(1)}, bf16[256,2048]{1,0:T(8,128)(2,1)}, u32[]{:S(2)}) copy-start(bf16[256,2048]{1,0:T(8,128)(2,1)} %param.21) | copy-start | bytes 3145732
  97.2 16.8 %copy-start.9 = (f32[2048]{0:T(1024)S(1)}, f32[2048]{0:T(1024)}, u32[]{:S(2)}) copy-start(f32[2048]{0:T(1024)} %param.27) | copy-start | bytes 24580
Sparse Core Ops, SparseCore 0:
  18.0 89.9 all-gather.1

commit v3 on v2

--- a/solution.py
+++ b/solution.py
@@ -25,9 +25,6 @@
     my_index = lax.axis_index("ctx")
     total_blocks = block_position.shape[0]
     query_seq = lax.dynamic_slice_in_dim(block_position, my_index * blocks_here, blocks_here)
-    storage_of = jnp.zeros((total_blocks,), jnp.int32).at[block_position].set(
-        jnp.arange(total_blocks, dtype=jnp.int32)
-    )
     heads = vertical.shape[0]
     br = query_seq[None, :, None]
     cand_v = jnp.broadcast_to(vertical[:, None, :], (heads, blocks_here, vertical.shape[1]))
@@ -43,7 +40,8 @@
     diag = jnp.broadcast_to(query_seq[None, :, None], (heads, blocks_here, 1))
     cand = jnp.concatenate([diag, cand, jnp.zeros_like(diag)], axis=-1)
     ok = jnp.concatenate([jnp.ones_like(diag, bool), ok, jnp.zeros_like(diag, bool)], axis=-1)
-    index = storage_of[jnp.clip(cand, 0, total_blocks - 1)]
+    match = block_position[None, None, None, :] == cand[..., None]
+    index = jnp.sum(jnp.where(match, jnp.arange(total_blocks, dtype=jnp.int32), 0), axis=-1)
     slots = cand.shape[-1]
     col_bias = jnp.where(ok, 0.0, NEG_FILL).astype(jnp.float32)
     col_bias = jnp.repeat(col_bias, BLOCK, axis=-1).reshape(heads * blocks_here, 1, slots * BLOCK)

time: 140 us -> 139 us (level)
  local copies, waits for them, and re-layouts: 13.1 us -> 6.53 us
  waiting for transfers between devices: 24 us -> 26.3 us
    gather x1 -> x0, local copies, waits for them, and re-layouts: 5.47 us -> none  [key_block_table(): index = storage_of[jnp.clip(cand, 0, total_blocks - 1)]]
    ppermute x6, waiting for transfers between devices: 23.9 us -> 26.3 us  [shifted(): return lax.ppermute(array, axis, pairs)]
  transfers between devices with their start and end apart: 7 -> 7, of which waited for: 4 -> 5; matrix products, arithmetic and copies ran while one was open for 18% -> 15% of each run, Pallas kernels for 0% -> 0%
where the time goes in v3:
time: 139 us
  starting transfers between devices  37.4 us (27%)
  waiting for transfers between devices  26.3 us (19%)
  blocking collectives  17.4 us (13%)
  Pallas kernels  16.9 us (12%)
  between operations  14.4 us (10%)
  other arithmetic  11.2 us (8%)
  matrix products  8.58 us (6%)
  local copies, waits for them, and re-layouts  6.53 us (5%)
    ppermute x6, starting transfers between devices, shifted(): return lax.ppermute(array, axis, pairs)  37.4 us
    ppermute x6, waiting for transfers between devices, shifted(): return lax.ppermute(array, axis, pairs)  26.3 us
    psum x1, blocking collectives, mamba_mix(): squares = lax.psum(jnp.sum(gated * gated, axis=1), 'tp')  17.4 us
    pallas_call x1, Pallas kernels, attend_sparse(): pl.pallas_call(lambda *refs: sparse_attention_kernel(slots, blocks_here,...  16.9 us
    dot_general x1, matrix products, mamba_mix(): jnp.einsum('hts,shp->thp', decay * inner[None], weighted, precision=careful)  6.68 us
  transfers between devices with their start and end apart: 7, of which 5 were waited for; matrix products, arithmetic and copies ran while one was open for 15% of the time, Pallas kernels for 0%

profile of v3, /device:TPU:1, one launch (start us, length us, event | category | flops | bytes accessed | tf_op | source)
XLA Modules:
  0.0 138.7 jit_solution(6267865404269813637)
XLA Ops:
  7.2 0.0 copy-start
  7.2 0.0 copy-start.3
  7.2 0.0 copy-start.6
  7.2 0.0 all-gather.2.cloned.1.call-start
  7.2 0.7 exponential_negate_fusion
  7.9 0.8 copy_bitcast_fusion.1
  8.7 0.6 reduce-window.6
  9.3 0.2 slice_reduce_fusion
  9.5 0.1 fusion.37
  9.6 0.2 slice_reduce_fusion.1
  9.8 0.1 bitcast_exponential_fusion
  9.9 1.5 %copy.45 = f32[256,2048]{0,1:T(8,128)S(1)} copy(bf16[256,2048]{1,0:T(8,128)(2,1)} %param.20) | data formatting | bytes 3145728 | tf_op jit(solution)/shard_map/reshape | solution.py:117
  11.4 0.0 copy-start.4
  11.4 0.0 copy-start.5
  11.4 0.0 copy-start.10
  11.5 0.9 fusion.20
  12.4 0.1 copy.48
  12.5 0.1 reshape.102
  12.6 0.1 broadcast_in_dim.97
  12.7 0.1 broadcast_in_dim_reshape.3
  12.8 4.4 %collective-permute-start = (f32[17,2048]{1,0:T(8,128)S(1)}, f32[17,2048]{1,0:T(8,128)S(1)}, u32[]{:S(2)}, u32[]{:S(2)}) collective-permute-start(f32[17,2048]{1,0:T(8,128)S(1)} %pad_maximum_fusion), channel_id=1, source_target_pairs={{0,8},{8,16},{16,24},{24,32},{32,40},{40,48},{48,56},{56,64},{64,7... | collective-permute-start | bytes 417800 | tf_op jit(solution)/shard_map/ppermute | solution.py:21
  17.2 0.7 pad_maximum_fusion.5
  17.9 0.0 all-gather.2.cloned.1.call-update
  18.0 0.2 fusion.38
  18.2 0.8 fusion.27.refs_4_
  18.9 0.1 dynamic_slice.3
  19.0 6.7 %fusion = f32[32,64,256]{2,1,0:T(8,128)} fusion(f32[256,256]{1,0:T(8,128)S(1)} %fusion.38, f32[32,256]{1,0:T(8,128)S(1)} %get-tuple-element.7, pred[256,256]{1,0:T(8,128)(4,1)S(1)} %iota_compare_fusion.1, f32[256,32,64]{0,2,1:T(8,128)S(1)} %bitcast.50, f32[256,32]{0,1:T(8,128)S(1)} %copy-done.3), kind=kOutput, calls=%fused_computation | convolution fusion | flops 814219264 | bytes 4587520 | tf_op jit(solution)/shard_map/hts,shp->thp/dot_general | solution.py:131
  25.7 0.1 broadcast_subtract_fusion
  25.8 0.1 broadcast_compare_fusion.1
  25.9 0.0 collective-permute-done
  25.9 3.5 %collective-permute-start.1 = (f32[17,2048]{1,0:T(8,128)S(1)}, f32[17,2048]{1,0:T(8,128)S(1)}, u32[]{:S(2)}, u32[]{:S(2)}) collective-permute-start(f32[17,2048]{1,0:T(8,128)S(1)} %collective-permute-done), channel_id=1, source_target_pairs={{0,8},{8,16},{16,24},{24,32},{32,40},{40,48},{48,56},{56,64},{64,7... | collective-permute-start | bytes 417800 | tf_op jit(solution)/shard_map/ppermute | solution.py:21
  29.4 0.1 pad_add_fusion.1
  29.5 0.1 pad_add_fusion
  29.6 3.1 %collective-permute-done.1 = f32[17,2048]{1,0:T(8,128)S(1)} collective-permute-done((f32[17,2048]{1,0:T(8,128)S(1)}, f32[17,2048]{1,0:T(8,128)S(1)}, u32[]{:S(2)}, u32[]{:S(2)}) %collective-permute-start.1) | collective-permute-done | bytes 139296 | tf_op jit(solution)/shard_map/ppermute | solution.py:21
  32.7 6.8 %collective-permute-start.2 = (f32[17,2048]{1,0:T(8,128)S(1)}, f32[17,2048]{1,0:T(8,128)S(1)}, u32[]{:S(2)}, u32[]{:S(2)}) collective-permute-start(f32[17,2048]{1,0:T(8,128)S(1)} %pad_maximum_fusion.1), channel_id=1, source_target_pairs={{0,16},{8,24},{16,32},{24,40},{32,48},{40,56},{48,64},{56,72},{64,... | collective-permute-start | bytes 417800 | tf_op jit(solution)/shard_map/ppermute | solution.py:21
  39.6 0.1 pad.12.clone
  39.6 0.1 pad.20.clone
  39.7 0.8 and_reduce_fusion
  40.5 7.8 %collective-permute-done.2 = f32[17,2048]{1,0:T(8,128)S(1)} collective-permute-done((f32[17,2048]{1,0:T(8,128)S(1)}, f32[17,2048]{1,0:T(8,128)S(1)}, u32[]{:S(2)}, u32[]{:S(2)}) %collective-permute-start.2) | collective-permute-done | bytes 139296 | tf_op jit(solution)/shard_map/ppermute | solution.py:21
  48.3 10.0 %collective-permute-start.3 = (f32[17,2048]{1,0:T(8,128)S(1)}, f32[17,2048]{1,0:T(8,128)S(1)}, u32[]{:S(2)}, u32[]{:S(2)}) collective-permute-start(f32[17,2048]{1,0:T(8,128)S(1)} %pad_maximum_fusion.2), channel_id=1, source_target_pairs={{0,32},{8,40},{16,48},{24,56},{32,64},{40,72},{48,80},{56,88},{64,... | collective-permute-start | bytes 417800 | tf_op jit(solution)/shard_map/ppermute | solution.py:21
  58.4 0.1 not_and_fusion
  58.5 7.0 %collective-permute-done.3 = f32[17,2048]{1,0:T(8,128)S(1)} collective-permute-done((f32[17,2048]{1,0:T(8,128)S(1)}, f32[17,2048]{1,0:T(8,128)S(1)}, u32[]{:S(2)}, u32[]{:S(2)}) %collective-permute-start.3) | collective-permute-done | bytes 139296 | tf_op jit(solution)/shard_map/ppermute | solution.py:21
  65.6 8.0 %collective-permute-start.4 = (f32[17,2048]{1,0:T(8,128)S(1)}, f32[17,2048]{1,0:T(8,128)S(1)}, u32[]{:S(2)}, u32[]{:S(2)}) collective-permute-start(f32[17,2048]{1,0:T(8,128)S(1)} %pad_maximum_fusion.3), channel_id=1, source_target_pairs={{0,64},{8,72},{16,80},{24,88},{32,96},{40,104},{48,112},{56,120},{... | collective-permute-start | bytes 417800 | tf_op jit(solution)/shard_map/ppermute | solution.py:21
  73.6 0.1 add_select_fusion
  73.7 4.4 %collective-permute-done.4 = f32[17,2048]{1,0:T(8,128)S(1)} collective-permute-done((f32[17,2048]{1,0:T(8,128)S(1)}, f32[17,2048]{1,0:T(8,128)S(1)}, u32[]{:S(2)}, u32[]{:S(2)}) %collective-permute-start.4) | collective-permute-done | bytes 139296 | tf_op jit(solution)/shard_map/ppermute | solution.py:21
  78.1 0.0 copy-start.11
  78.1 4.6 %collective-permute-start.5 = (f32[17,2048]{1,0:T(8,128)S(1)}, f32[17,2048]{1,0:T(8,128)S(1)}, u32[]{:S(2)}, u32[]{:S(2)}) collective-permute-start(f32[17,2048]{1,0:T(8,128)S(1)} %pad_maximum_fusion.4), channel_id=1, source_target_pairs={{0,128},{8,136},{16,144},{24,152},{32,160},{40,168},{48,176},{56,1... | collective-permute-start | bytes 417800 | tf_op jit(solution)/shard_map/ppermute | solution.py:21
  82.7 0.1 broadcast_in_dim.48
  82.8 0.1 add_add_fusion
  82.9 0.2 broadcast_in_dim.93
  83.1 0.9 reshape_reshape.4.refs_3_
  83.9 0.1 copy.42
  84.0 1.4 %select_reduce_fusion = s32[8,4,18]{0,2,1:T(8,128)S(1)} fusion(s32[8,4,18]{0,2,1:T(8,128)S(1)} %copy.42, s32[128]{0:T(128)S(1)} %copy-done.10), kind=kLoop, calls=%fused_computation.30 | loop fusion | flops 220608 | bytes 5120 | tf_op jit(solution)/shard_map/reduce_sum | solution.py:44
  85.4 0.1 copy.43
  85.5 0.7 reshape.97.refs_2_
  86.2 4.0 %collective-permute-done.5 = f32[17,2048]{1,0:T(8,128)S(1)} collective-permute-done((f32[17,2048]{1,0:T(8,128)S(1)}, f32[17,2048]{1,0:T(8,128)S(1)}, u32[]{:S(2)}, u32[]{:S(2)}) %collective-permute-start.5) | collective-permute-done | bytes 139296 | tf_op jit(solution)/shard_map/ppermute | solution.py:21
  90.3 0.8 fusion.29
  91.0 2.1 %fusion.15 = f32[256,32,64]{0,2,1:T(8,128)} fusion(f32[32,64,256]{2,1,0:T(8,128)S(1)} %copy-done.2, f32[256,32,64]{0,2,1:T(8,128)S(1)} %bitcast.51, f32[256,32,64]{0,2,1:T(8,128)S(1)} %bitcast.52, f32[32]{0:T(128)S(1)} %copy-done.11, f32[256,32]{0,1:T(8,128)S(1)} %get-tuple-element.4), kind=kLoop, calls=%fused_computation.18 | loop fusion | flops 2097152 | bytes 8421504 | tf_op jit(solution)/shard_map/add | solution.py:152
  93.1 2.0 %copy.49 = f32[256,2048]{1,0:T(8,128)S(1)} copy(f32[256,2048]{0,1:T(8,128)} %bitcast.53) | data formatting | bytes 4194304 | tf_op jit(solution)/shard_map/reshape | solution.py:152
  95.1 0.0 copy-start.9
  95.2 0.7 multiply_reduce_fusion
  95.9 17.4 %psum.7 = f32[256]{0:T(256)S(1)} all-reduce(f32[256]{0:T(256)S(1)} %multiply_reduce_fusion), channel_id=1, replica_groups=mesh['ctx'=32,'tp'=8] {'tp'}, use_global_device_ids=true, to_apply=%region_5.6 | all-reduce | flops 256 | bytes 2048 | tf_op jit(solution)/shard_map/psum | solution.py:155
  113.2 1.7 %multiply_convert_fusion = bf16[256,2048]{1,0:T(8,128)(2,1)} fusion(f32[2048]{0:T(1024)S(1)} %copy-done.9, f32[256]{0:T(256)S(1)} %add_rsqrt_fusion, f32[256,2048]{1,0:T(8,128)S(1)} %copy.49, bf16[256,2048]{1,0:T(8,128)(2,1)S(1)} %copy-done.1), kind=kLoop, calls=%fused_computation.19 | loop fusion | flops 4718592 | bytes 4203520 | tf_op jit(solution)/shard_map/convert_element_type | solution.py:157
  115.0 16.9 %shard_map.149 = bf16[256,1024]{1,0:T(8,128)(2,1)} custom-call(bf16[256,1024]{1,0:T(8,128)(2,1)} %refs_0_.1, bf16[2,8192,128]{2,1,0:T(8,128)(2,1)} %all-gather.2.cloned.1.call-done.refs_1_, s32[576]{0:T(1024)} %reshape.97.refs_2_, f32[32,1,1152]{2,1,0:T(1,128)} %reshape_reshape.4.refs_3_, f32[64,1152]{1,0:T(8,128)} %fusion.27.refs_4_), custom_call_target="tpu_custom_call" | custom-call | flops 1207959552 | bytes 5242880 | tf_op jit(solution)/shard_map/pallas_call | solution.py:89
  (39 shorter events, 0.4 us)
Async XLA Ops:
  7.2 10.8 %copy-start = (bf16[256,16]{0,1:T(8,128)(2,1)S(1)}, bf16[256,16]{0,1:T(8,128)(2,1)}, u32[]{:S(2)}) copy-start(bf16[256,16]{0,1:T(8,128)(2,1)} %param.23) | copy-start | bytes 24580
  7.2 4.2 %copy-start.3 = (f32[256,32]{0,1:T(8,128)S(1)}, f32[256,32]{0,1:T(8,128)}, u32[]{:S(2)}) copy-start(f32[256,32]{0,1:T(8,128)} %param.24) | copy-start | bytes 98308
  7.2 4.2 %copy-start.6 = (bf16[256,16]{0,1:T(8,128)(2,1)S(1)}, bf16[256,16]{0,1:T(8,128)(2,1)}, u32[]{:S(2)}) copy-start(bf16[256,16]{0,1:T(8,128)(2,1)} %param.22) | copy-start | bytes 24580
  7.2 107.8 %all-gather.2.cloned.1.call-start = ((), (), s32[]{:S(2)}) async-start(), calls=%async_computation | async-start | bytes 4325376 | tf_op jit(solution)/shard_map/all_gather | solution.py:82
  11.4 5.8 %copy-start.4 = (bf16[256,128]{1,0:T(8,128)(2,1)S(1)}, bf16[256,128]{1,0:T(8,128)(2,1)}, u32[]{:S(2)}) copy-start(bf16[256,128]{1,0:T(8,128)(2,1)} %param.16) | copy-start | bytes 196612
  11.4 5.8 %copy-start.5 = (bf16[256,128]{1,0:T(8,128)(2,1)S(1)}, bf16[256,128]{1,0:T(8,128)(2,1)}, u32[]{:S(2)}) copy-start(bf16[256,128]{1,0:T(8,128)(2,1)} %param.15) | copy-start | bytes 196612
  11.4 7.5 %copy-start.10 = (s32[128]{0:T(128)S(1)}, s32[128]{0:T(128)}, u32[]{:S(2)}) copy-start(s32[128]{0:T(128)} %param.19) | copy-start | bytes 1540
  12.8 13.1 %collective-permute-start = (f32[17,2048]{1,0:T(8,128)S(1)}, f32[17,2048]{1,0:T(8,128)S(1)}, u32[]{:S(2)}, u32[]{:S(2)}) collective-permute-start(f32[17,2048]{1,0:T(8,128)S(1)} %pad_maximum_fusion), channel_id=1, source_target_pairs={{0,8},{8,16},{16,24},{24,32},{32,40},{40,48},{48,56},{56,64},{64,7... | collective-permute-start | bytes 417800 | tf_op jit(solution)/shard_map/ppermute | solution.py:21
  19.0 6.7 %copy-start.8 = (s32[8,8]{1,0:T(8,128)S(1)}, s32[8,8]{1,0:T(8,128)}, u32[]{:S(2)}) copy-start(s32[8,8]{1,0:T(8,128)} %param.18) | copy-start | bytes 772
  19.0 6.8 %copy-start.7 = (s32[8,8]{1,0:T(8,128)S(1)}, s32[8,8]{1,0:T(8,128)}, u32[]{:S(2)}) copy-start(s32[8,8]{1,0:T(8,128)} %param.17) | copy-start | bytes 772
  25.9 6.8 %collective-permute-start.1 = (f32[17,2048]{1,0:T(8,128)S(1)}, f32[17,2048]{1,0:T(8,128)S(1)}, u32[]{:S(2)}, u32[]{:S(2)}) collective-permute-start(f32[17,2048]{1,0:T(8,128)S(1)} %collective-permute-done), channel_id=1, source_target_pairs={{0,8},{8,16},{16,24},{24,32},{32,40},{40,48},{48,56},{56,64},{64,7... | collective-permute-start | bytes 417800 | tf_op jit(solution)/shard_map/ppermute | solution.py:21
  32.7 15.5 %collective-permute-start.2 = (f32[17,2048]{1,0:T(8,128)S(1)}, f32[17,2048]{1,0:T(8,128)S(1)}, u32[]{:S(2)}, u32[]{:S(2)}) collective-permute-start(f32[17,2048]{1,0:T(8,128)S(1)} %pad_maximum_fusion.1), channel_id=1, source_target_pairs={{0,16},{8,24},{16,32},{24,40},{32,48},{40,56},{48,64},{56,72},{64,... | collective-permute-start | bytes 417800 | tf_op jit(solution)/shard_map/ppermute | solution.py:21
  48.3 17.2 %collective-permute-start.3 = (f32[17,2048]{1,0:T(8,128)S(1)}, f32[17,2048]{1,0:T(8,128)S(1)}, u32[]{:S(2)}, u32[]{:S(2)}) collective-permute-start(f32[17,2048]{1,0:T(8,128)S(1)} %pad_maximum_fusion.2), channel_id=1, source_target_pairs={{0,32},{8,40},{16,48},{24,56},{32,64},{40,72},{48,80},{56,88},{64,... | collective-permute-start | bytes 417800 | tf_op jit(solution)/shard_map/ppermute | solution.py:21
  65.6 12.5 %collective-permute-start.4 = (f32[17,2048]{1,0:T(8,128)S(1)}, f32[17,2048]{1,0:T(8,128)S(1)}, u32[]{:S(2)}, u32[]{:S(2)}) collective-permute-start(f32[17,2048]{1,0:T(8,128)S(1)} %pad_maximum_fusion.3), channel_id=1, source_target_pairs={{0,64},{8,72},{16,80},{24,88},{32,96},{40,104},{48,112},{56,120},{... | collective-permute-start | bytes 417800 | tf_op jit(solution)/shard_map/ppermute | solution.py:21
  78.1 12.9 %copy-start.11 = (f32[32]{0:T(128)S(1)}, f32[32]{0:T(128)}, u32[]{:S(2)}) copy-start(f32[32]{0:T(128)} %param.26) | copy-start | bytes 388
  78.1 12.1 %collective-permute-start.5 = (f32[17,2048]{1,0:T(8,128)S(1)}, f32[17,2048]{1,0:T(8,128)S(1)}, u32[]{:S(2)}, u32[]{:S(2)}) collective-permute-start(f32[17,2048]{1,0:T(8,128)S(1)} %pad_maximum_fusion.4), channel_id=1, source_target_pairs={{0,128},{8,136},{16,144},{24,152},{32,160},{40,168},{48,176},{56,1... | collective-permute-start | bytes 417800 | tf_op jit(solution)/shard_map/ppermute | solution.py:21
  86.2 4.8 %copy-start.2 = (f32[32,64,256]{2,1,0:T(8,128)S(1)}, f32[32,64,256]{2,1,0:T(8,128)}, u32[]{:S(2)}) copy-start(f32[32,64,256]{2,1,0:T(8,128)} %fusion) | copy-start | bytes 6291460
  93.1 2.0 %copy-start.1 = (bf16[256,2048]{1,0:T(8,128)(2,1)S(1)}, bf16[256,2048]{1,0:T(8,128)(2,1)}, u32[]{:S(2)}) copy-start(bf16[256,2048]{1,0:T(8,128)(2,1)} %param.21) | copy-start | bytes 3145732
  95.1 18.1 %copy-start.9 = (f32[2048]{0:T(1024)S(1)}, f32[2048]{0:T(1024)}, u32[]{:S(2)}) copy-start(f32[2048]{0:T(1024)} %param.27) | copy-start | bytes 24580
Sparse Core Ops, SparseCore 0:
  18.0 89.5 all-gather.1

commit v4 on v3

--- a/solution.py
+++ b/solution.py
@@ -109,6 +109,66 @@
     )(queries, kv_all, index, col_bias, causal_bias)
 
 
+SCAN_SHIFTS = (1, 1, 2, 4, 8, 16)
+
+
+def carry_scan_kernel(x_ref, o_ref, cur, got, send_sems, recv_sems):
+    n = lax.axis_size("ctx")
+    me = lax.axis_index("ctx")
+    tp = lax.axis_index("tp")
+    barrier = pltpu.get_barrier_semaphore()
+    partners = sorted({k % n for k in SCAN_SHIFTS} | {(-k) % n for k in SCAN_SHIFTS})
+    for k in partners:
+        pl.semaphore_signal(
+            barrier, inc=1, device_id=(lax.rem(me + k, n), tp), device_id_type=pl.DeviceIdType.MESH
+        )
+    pl.semaphore_wait(barrier, len(partners))
+    rounds = len(SCAN_SHIFTS)
+    for r, k in enumerate(SCAN_SHIFTS):
+        src = x_ref if r == 0 else cur.at[r]
+        copy = pltpu.make_async_remote_copy(
+            src_ref=src,
+            dst_ref=got.at[r],
+            send_sem=send_sems.at[r],
+            recv_sem=recv_sems.at[r],
+            device_id=(lax.rem(me + k, n), tp),
+            device_id_type=pl.DeviceIdType.MESH,
+        )
+        copy.start()
+        copy.wait()
+        keep = ((me - k + n) // n).astype(jnp.float32)
+        incoming = got[r]
+        if r == 0:
+            new = incoming * keep
+        else:
+            prev = cur[r]
+            decay = prev[0:8]
+            new_decay = decay * (incoming[0:8] * keep + (1.0 - keep))
+            new_state = prev[8:] + prev[0:1] * (incoming[8:] * keep)
+            new = jnp.concatenate([new_decay, new_state], axis=0)
+        if r + 1 < rounds:
+            cur[r + 1] = new
+        else:
+            o_ref[...] = new
+
+
+def carry_scan(packed):
+    rounds = len(SCAN_SHIFTS)
+    return pl.pallas_call(
+        carry_scan_kernel,
+        out_shape=jax.ShapeDtypeStruct(packed.shape, packed.dtype),
+        in_specs=[pl.BlockSpec(memory_space=pltpu.VMEM)],
+        out_specs=pl.BlockSpec(memory_space=pltpu.VMEM),
+        scratch_shapes=[
+            pltpu.VMEM((rounds,) + packed.shape, packed.dtype),
+            pltpu.VMEM((rounds,) + packed.shape, packed.dtype),
+            pltpu.SemaphoreType.DMA((rounds,)),
+            pltpu.SemaphoreType.DMA((rounds,)),
+        ],
+        compiler_params=pltpu.CompilerParams(collective_id=0, has_side_effects=True),
+    )(packed)
+
+
 def mamba_mix(ssm_input, gate, state_in, state_out, step_size, decay_log, skip_gain, norm_gain):
     careful = lax.Precision.HIGH
     row_count = ssm_input.shape[0]
@@ -135,15 +195,8 @@
     ).reshape(D_STATE, inner_width)
     carry_decay = jnp.repeat(jnp.exp(cumulative[-1]), SSM_HEAD_DIM)[None, :]
 
-    packed = shifted(jnp.concatenate([carry_decay, local_state], axis=0), "ctx", 1)
-    size = lax.axis_size("ctx")
-    step = 1
-    while step < size:
-        got = shifted(packed, "ctx", step)
-        factor = packed[0:1]
-        packed = jnp.concatenate([factor * got[0:1], factor * got[1:] + packed[1:]], axis=0)
-        step *= 2
-    incoming = packed[1:]
+    packed = jnp.concatenate([jnp.broadcast_to(carry_decay, (8, inner_width)), local_state], axis=0)
+    incoming = carry_scan(packed)[8:]
 
     from_past = jnp.dot(
         out_map, incoming, precision=careful, preferred_element_type=jnp.float32

time: 139 us -> 137 us (0.986)
  the two profiles are of different devices: /device:TPU:1 before, /device:TPU:33 now
where the time goes in v4:
time: 137 us
  Pallas kernels  70.3 us (51%)
  blocking collectives  23.5 us (17%)
  between operations  14.3 us (10%)
  other arithmetic  11.8 us (9%)
  matrix products  9.64 us (7%)
  local copies, waits for them, and re-layouts  7.43 us (5%)
    pallas_call x1, Pallas kernels, carry_scan(): pl.pallas_call(carry_scan_kernel, out_shape=jax.ShapeDtypeStruct(packed.s...  53.4 us
    psum x1, blocking collectives, mamba_mix(): squares = lax.psum(jnp.sum(gated * gated, axis=1), 'tp')  23.5 us
    pallas_call x1, Pallas kernels, attend_sparse(): pl.pallas_call(lambda *refs: sparse_attention_kernel(slots, blocks_here,...  16.9 us
    dot_general x1, matrix products, mamba_mix(): jnp.einsum('hts,shp->thp', decay * inner[None], weighted, precision=careful)  6.76 us
  transfers between devices with their start and end apart: 1, of which 0 were waited for; matrix products, arithmetic and copies ran while one was open for 20% of the time, Pallas kernels for 39%

profile of v4, /device:TPU:33, one launch (start us, length us, event | category | flops | bytes accessed | tf_op | source)
XLA Modules:
  0.0 137.0 jit_solution(7658764403431066706)
XLA Ops:
  7.2 0.0 copy-start
  7.2 0.0 copy-start.4
  7.2 0.0 copy-start.5
  7.2 0.0 all-gather.2.cloned.1.call-start
  7.2 1.5 %pad_maximum_fusion.1 = bf16[2,256,128]{2,1,0:T(8,128)(2,1)} fusion(bf16[1,256,128]{2,1,0:T(8,128)(2,1)} %bitcast.48, bf16[1,256,128]{2,1,0:T(8,128)(2,1)} %bitcast.49), kind=kLoop, calls=%fused_computation.36 | loop fusion | flops 65536 | bytes 262144 | tf_op jit(solution)/shard_map/stack | solution.py:82
  8.8 0.0 all-gather.2.cloned.1.call-update
  8.8 0.7 exponential_negate_fusion
  9.5 0.8 copy_bitcast_fusion.1
  10.3 0.6 reduce-window.6
  10.9 0.2 slice_reduce_fusion
  11.1 1.5 %copy.46 = f32[256,2048]{0,1:T(8,128)S(1)} copy(bf16[256,2048]{1,0:T(8,128)(2,1)} %param.20) | data formatting | bytes 3145728 | tf_op jit(solution)/shard_map/reshape | solution.py:177
  12.6 0.1 copy_bitcast_fusion
  12.7 0.2 slice_reduce_fusion.1
  12.8 0.1 bitcast_exponential_fusion
  12.9 0.0 copy-done.4
  13.0 0.0 copy-done.5
  13.0 0.9 fusion.24
  13.9 0.0 copy-start.11
  13.9 0.1 copy.49
  14.0 0.1 reshape.103
  14.1 0.1 broadcast_in_dim.104
  14.2 0.1 broadcast_in_dim.105
  14.3 0.7 pad_maximum_fusion.x_ref
  15.0 53.4 %shard_map.150 = f32[24,2048]{1,0:T(8,128)} custom-call(f32[24,2048]{1,0:T(8,128)} %pad_maximum_fusion.x_ref), custom_call_target="tpu_custom_call" | custom-call | tf_op jit(solution)/shard_map/pallas_call | solution.py:157
  68.4 0.0 copy-done
  68.4 0.2 fusion.37
  68.6 1.7 %fusion.32 = f32[2048,256]{1,0:T(8,128)S(1)} fusion(bf16[256,16]{0,1:T(8,128)(2,1)S(1)} %copy-done, f32[24,2048]{1,0:T(8,128)} %shard_map.150), kind=kOutput, calls=%fused_computation.37 | convolution fusion | flops 50331648 | bytes 2236416 | tf_op jit(solution)/shard_map/dot_general | solution.py:201
  70.3 0.0 copy-done.11
  70.4 6.8 %fusion.15 = f32[256,32,64]{0,2,1:T(8,128)} fusion(f32[256,32,64]{0,2,1:T(8,128)S(1)} %bitcast.45, f32[256,32,64]{0,2,1:T(8,128)S(1)} %bitcast.46, f32[256,256]{1,0:T(8,128)S(1)} %fusion.37, f32[32,256]{1,0:T(8,128)S(1)} %get-tuple-element.4, pred[256,256]{1,0:T(8,128)(4,1)S(1)} %iota_compare_fusion.1, f32[32]{0:T(128)S(1)} %copy-done.11, ...), kind=kOutput, calls=%fused_computation.18 | convolution fusion | flops 816316416 | bytes 6717568 | tf_op jit(solution)/shard_map/hts,shp->thp/dot_general | solution.py:191
  77.1 0.0 copy-start.10
  77.1 2.0 %copy.50 = f32[256,2048]{1,0:T(8,128)S(1)} copy(f32[256,2048]{0,1:T(8,128)} %bitcast.47) | data formatting | bytes 4194304 | tf_op jit(solution)/shard_map/reshape | solution.py:205
  79.2 0.1 pad.4.clone
  79.2 0.0 copy-done.10
  79.2 0.1 dynamic_slice.3
  79.3 0.0 copy-done.6
  79.3 0.0 copy-done.7
  79.3 0.1 broadcast_compare_fusion.1
  79.4 0.1 pad_add_fusion.1
  79.5 0.3 copy-done.9
  79.8 0.1 broadcast_subtract_fusion
  79.9 0.0 copy-start.2
  79.9 0.1 pad_add_fusion
  80.0 0.8 and_reduce_fusion
  80.8 0.1 not_and_fusion
  80.9 0.0 copy-done.2
  80.9 0.1 add_select_fusion
  81.0 0.0 copy-done.3
  81.0 0.2 broadcast_in_dim.100
  81.1 0.0 copy-start.8
  81.1 0.9 reshape_reshape.4.refs_3_
  82.0 0.1 pad.12.clone
  82.1 0.7 broadcast_in_dim.52
  82.7 0.8 add_add_fusion
  83.6 0.1 copy.43
  83.7 2.0 %select_reduce_fusion = s32[8,4,18]{0,2,1:T(8,128)S(1)} fusion(s32[8,4,18]{0,2,1:T(8,128)S(1)} %copy.43, s32[128]{0:T(128)} %param.19), kind=kLoop, calls=%fused_computation.30 | loop fusion | flops 220608 | bytes 5120 | tf_op jit(solution)/shard_map/reduce_sum | solution.py:44
  85.7 0.1 copy.44
  85.8 0.7 reshape.98.refs_2_
  86.5 0.0 copy-done.1
  86.5 0.7 multiply_reduce_fusion
  87.2 23.5 %psum.7 = f32[256]{0:T(256)S(1)} all-reduce(f32[256]{0:T(256)S(1)} %multiply_reduce_fusion), channel_id=1, replica_groups=mesh['ctx'=32,'tp'=8] {'tp'}, use_global_device_ids=true, to_apply=%region_5.6 | all-reduce | flops 256 | bytes 2048 | tf_op jit(solution)/shard_map/psum | solution.py:208
  110.8 0.7 fusion.31.refs_4_
  111.5 0.0 copy-done.8
  111.5 1.7 %multiply_convert_fusion = bf16[256,2048]{1,0:T(8,128)(2,1)} fusion(f32[2048]{0:T(1024)S(1)} %copy-done.8, f32[256]{0:T(256)S(1)} %add_rsqrt_fusion, f32[256,2048]{1,0:T(8,128)S(1)} %copy.50, bf16[256,2048]{1,0:T(8,128)(2,1)S(1)} %copy-done.1), kind=kLoop, calls=%fused_computation.19 | loop fusion | flops 4718592 | bytes 4203520 | tf_op jit(solution)/shard_map/convert_element_type | solution.py:210
  113.2 16.9 %shard_map.149 = bf16[256,1024]{1,0:T(8,128)(2,1)} custom-call(bf16[256,1024]{1,0:T(8,128)(2,1)} %refs_0_.1, bf16[2,8192,128]{2,1,0:T(8,128)(2,1)} %all-gather.2.cloned.1.call-done.refs_1_, s32[576]{0:T(1024)} %reshape.98.refs_2_, f32[32,1,1152]{2,1,0:T(1,128)} %reshape_reshape.4.refs_3_, f32[64,1152]{1,0:T(8,128)} %fusion.31.refs_4_), custom_call_target="tpu_custom_call" | custom-call | flops 1207959552 | bytes 5242880 | tf_op jit(solution)/shard_map/pallas_call | solution.py:89
  (16 shorter events, 0.1 us)
Async XLA Ops:
  7.2 61.2 %copy-start = (bf16[256,16]{0,1:T(8,128)(2,1)S(1)}, bf16[256,16]{0,1:T(8,128)(2,1)}, u32[]{:S(2)}) copy-start(bf16[256,16]{0,1:T(8,128)(2,1)} %param.23) | copy-start | bytes 24580
  7.2 5.8 %copy-start.4 = (f32[256,32]{0,1:T(8,128)S(1)}, f32[256,32]{0,1:T(8,128)}, u32[]{:S(2)}) copy-start(f32[256,32]{0,1:T(8,128)} %param.24) | copy-start | bytes 98308
  7.2 5.8 %copy-start.5 = (bf16[256,16]{0,1:T(8,128)(2,1)S(1)}, bf16[256,16]{0,1:T(8,128)(2,1)}, u32[]{:S(2)}) copy-start(bf16[256,16]{0,1:T(8,128)(2,1)} %param.22) | copy-start | bytes 24580
  7.2 106.0 %all-gather.2.cloned.1.call-start = ((), (), s32[]{:S(2)}) async-start(), calls=%async_computation | async-start | bytes 4325376 | tf_op jit(solution)/shard_map/all_gather | solution.py:82
  13.9 56.4 %copy-start.11 = (f32[32]{0:T(128)S(1)}, f32[32]{0:T(128)}, u32[]{:S(2)}) copy-start(f32[32]{0:T(128)} %param.26) | copy-start | bytes 388
  77.1 2.1 %copy-start.10 = (s32[128]{0:T(128)S(1)}, s32[128]{0:T(128)}, u32[]{:S(2)}) copy-start(s32[128]{0:T(128)} %param.19) | copy-start | bytes 1540
  77.1 2.2 %copy-start.6 = (s32[8,8]{1,0:T(8,128)S(1)}, s32[8,8]{1,0:T(8,128)}, u32[]{:S(2)}) copy-start(s32[8,8]{1,0:T(8,128)} %param.17) | copy-start | bytes 772
  77.1 2.2 %copy-start.7 = (s32[8,8]{1,0:T(8,128)S(1)}, s32[8,8]{1,0:T(8,128)}, u32[]{:S(2)}) copy-start(s32[8,8]{1,0:T(8,128)} %param.18) | copy-start | bytes 772
  77.1 9.4 %copy-start.1 = (bf16[256,2048]{1,0:T(8,128)(2,1)S(1)}, bf16[256,2048]{1,0:T(8,128)(2,1)}, u32[]{:S(2)}) copy-start(bf16[256,2048]{1,0:T(8,128)(2,1)} %param.21) | copy-start | bytes 3145732
  79.3 0.5 copy-start.9
  79.9 1.0 copy-start.3
  79.9 0.9 copy-start.2
  81.1 30.4 %copy-start.8 = (f32[2048]{0:T(1024)S(1)}, f32[2048]{0:T(1024)}, u32[]{:S(2)}) copy-start(f32[2048]{0:T(1024)} %param.27) | copy-start | bytes 24580
Sparse Core Ops, SparseCore 0:
  10.6 87.4 all-gather.1

commit v5 on v3

--- a/solution.py
+++ b/solution.py
@@ -109,6 +109,80 @@
     )(queries, kv_all, index, col_bias, causal_bias)
 
 
+SCAN_SHIFTS = (2, 4, 8, 16)
+
+
+def carry_scan_kernel(s_ref, a_ref, o_ref, cur_s, cur_a, got_s, got_a, sems):
+    n = lax.axis_size("ctx")
+    me = lax.axis_index("ctx")
+    tp = lax.axis_index("tp")
+    shifts = (1,) + SCAN_SHIFTS
+    barrier = pltpu.get_barrier_semaphore()
+    partners = sorted({k % n for k in shifts} | {(-k) % n for k in shifts})
+    for k in partners:
+        pl.semaphore_signal(
+            barrier, inc=1, device_id=(lax.rem(me + k, n), tp), device_id_type=pl.DeviceIdType.MESH
+        )
+    pl.semaphore_wait(barrier, len(partners))
+
+    def send(slot, k, src_s, src_a):
+        target = (lax.rem(me + k, n), tp)
+        copies = [
+            pltpu.make_async_remote_copy(
+                src_ref=src,
+                dst_ref=dst.at[slot],
+                send_sem=sems.at[part, 0, slot],
+                recv_sem=sems.at[part, 1, slot],
+                device_id=target,
+                device_id_type=pl.DeviceIdType.MESH,
+            )
+            for part, (src, dst) in enumerate(((src_s, got_s), (src_a, got_a)))
+        ]
+        for copy in copies:
+            copy.start()
+        return copies
+
+    def keep_of(k):
+        return ((me - k + n) // n).astype(jnp.float32)
+
+    first = send(0, 1, s_ref, a_ref) + send(1, 2, s_ref, a_ref)
+    for copy in first:
+        copy.wait()
+    keep1, keep2 = keep_of(1), keep_of(2)
+    a1, a2 = got_a[0], got_a[1]
+    state = keep1 * (got_s[0] + a1 * (keep2 * got_s[1]))
+    decay = (keep1 * a1 + (1.0 - keep1)) * (keep2 * a2 + (1.0 - keep2))
+    for j, k in enumerate(SCAN_SHIFTS):
+        cur_s[j] = state
+        cur_a[j] = decay
+        slot = j + 2
+        for copy in send(slot, k, cur_s.at[j], cur_a.at[j]):
+            copy.wait()
+        keep = keep_of(k)
+        state = cur_s[j] + cur_a[j] * (keep * got_s[slot])
+        decay = cur_a[j] * (keep * got_a[slot] + (1.0 - keep))
+    o_ref[...] = state
+
+
+def carry_scan(local_state, carry_decay):
+    rounds = len(SCAN_SHIFTS)
+    slots = rounds + 2
+    return pl.pallas_call(
+        carry_scan_kernel,
+        out_shape=jax.ShapeDtypeStruct(local_state.shape, local_state.dtype),
+        in_specs=[pl.BlockSpec(memory_space=pltpu.VMEM)] * 2,
+        out_specs=pl.BlockSpec(memory_space=pltpu.VMEM),
+        scratch_shapes=[
+            pltpu.VMEM((rounds,) + local_state.shape, jnp.float32),
+            pltpu.VMEM((rounds,) + carry_decay.shape, jnp.float32),
+            pltpu.VMEM((slots,) + local_state.shape, jnp.float32),
+            pltpu.VMEM((slots,) + carry_decay.shape, jnp.float32),
+            pltpu.SemaphoreType.DMA((2, 2, slots)),
+        ],
+        compiler_params=pltpu.CompilerParams(collective_id=0, has_side_effects=True),
+    )(local_state, carry_decay)
+
+
 def mamba_mix(ssm_input, gate, state_in, state_out, step_size, decay_log, skip_gain, norm_gain):
     careful = lax.Precision.HIGH
     row_count = ssm_input.shape[0]
@@ -135,15 +209,7 @@
     ).reshape(D_STATE, inner_width)
     carry_decay = jnp.repeat(jnp.exp(cumulative[-1]), SSM_HEAD_DIM)[None, :]
 
-    packed = shifted(jnp.concatenate([carry_decay, local_state], axis=0), "ctx", 1)
-    size = lax.axis_size("ctx")
-    step = 1
-    while step < size:
-        got = shifted(packed, "ctx", step)
-        factor = packed[0:1]
-        packed = jnp.concatenate([factor * got[0:1], factor * got[1:] + packed[1:]], axis=0)
-        step *= 2
-    incoming = packed[1:]
+    incoming = carry_scan(local_state, carry_decay)
 
     from_past = jnp.dot(
         out_map, incoming, precision=careful, preferred_element_type=jnp.float32

time: 139 us -> 125 us (0.90)
  Pallas kernels: 16.9 us -> 63.6 us
  starting transfers between devices: 37.4 us -> 0.04 us
  waiting for transfers between devices: 26.3 us -> 0.02 us
  local copies, waits for them, and re-layouts: 6.53 us -> 8.72 us
    pallas_call x0 -> x1, Pallas kernels: none -> 46.7 us  [carry_scan(): pl.pallas_call(carry_scan_kernel, out_shape=jax.ShapeDtypeStruct(local_st...]
    ppermute x6 -> x0, starting transfers between devices: 37.4 us -> none  [shifted(): return lax.ppermute(array, axis, pairs)]
    ppermute x6 -> x0, waiting for transfers between devices: 26.3 us -> none  [shifted(): return lax.ppermute(array, axis, pairs)]
    add x5 -> x0, other arithmetic: 2.2 us -> none  [the longest x1 2.06 us: mamba_mix(): within + from_past + skip_gain[None, :, None] * inputs]
  transfers between devices with their start and end apart: 7 -> 1, of which waited for: 5 -> 0; matrix products, arithmetic and copies ran while one was open for 15% -> 22% of each run, Pallas kernels for 0% -> 38%
where the time goes in v5:
time: 125 us; the launch traced here: 124 us
  Pallas kernels  63.6 us (51%)
  blocking collectives  16.7 us (13%)
  between operations  14.3 us (11%)
  other arithmetic  11.1 us (9%)
  matrix products  9.59 us (8%)
  local copies, waits for them, and re-layouts  8.72 us (7%)
    pallas_call x1, Pallas kernels, carry_scan(): pl.pallas_call(carry_scan_kernel, out_shape=jax.ShapeDtypeStruct(local_st...  46.7 us
    pallas_call x1, Pallas kernels, attend_sparse(): pl.pallas_call(lambda *refs: sparse_attention_kernel(slots, blocks_here,...  16.9 us
    psum x1, blocking collectives, mamba_mix(): squares = lax.psum(jnp.sum(gated * gated, axis=1), 'tp')  16.7 us
    dot_general x1, matrix products, mamba_mix(): jnp.einsum('hts,shp->thp', decay * inner[None], weighted, precision=careful)  6.76 us
  transfers between devices with their start and end apart: 1, of which 0 were waited for; matrix products, arithmetic and copies ran while one was open for 22% of the time, Pallas kernels for 38%

profile of v5, /device:TPU:1, one launch (start us, length us, event | category | flops | bytes accessed | tf_op | source)
XLA Modules:
  0.0 124.0 jit_solution(502922624874131223)
XLA Ops:
  7.2 0.0 copy-start
  7.2 0.0 copy-start.4
  7.2 0.0 copy-start.5
  7.2 0.0 all-gather.2.cloned.1.call-start
  7.2 1.5 %pad_maximum_fusion = bf16[2,256,128]{2,1,0:T(8,128)(2,1)} fusion(bf16[1,256,128]{2,1,0:T(8,128)(2,1)} %bitcast.49, bf16[1,256,128]{2,1,0:T(8,128)(2,1)} %bitcast.50), kind=kLoop, calls=%fused_computation.35 | loop fusion | flops 65536 | bytes 262144 | tf_op jit(solution)/shard_map/stack | solution.py:82
  8.8 0.0 all-gather.2.cloned.1.call-update
  8.8 0.7 exponential_negate_fusion
  9.5 0.8 copy_bitcast_fusion.1
  10.3 0.6 reduce-window.6
  10.9 0.2 slice_reduce_fusion
  11.1 1.5 %copy.46 = f32[256,2048]{0,1:T(8,128)S(1)} copy(bf16[256,2048]{1,0:T(8,128)(2,1)} %param.20) | data formatting | bytes 3145728 | tf_op jit(solution)/shard_map/reshape | solution.py:191
  12.6 0.1 copy_bitcast_fusion
  12.7 0.2 slice_reduce_fusion.1
  12.9 0.1 bitcast_exponential_fusion
  13.0 0.0 copy-done.4
  13.0 0.0 copy-done.5
  13.0 0.9 fusion.24
  13.9 0.0 copy-start.11
  13.9 0.1 copy.49
  14.0 0.8 reshape.102.s_ref
  14.8 0.1 broadcast_in_dim.97
  14.9 0.7 broadcast_in_dim_reshape.3.a_ref
  15.5 46.7 %shard_map.150 = f32[16,2048]{1,0:T(8,128)} custom-call(f32[16,2048]{1,0:T(8,128)} %reshape.102.s_ref, f32[1,2048]{1,0:T(1,128)} %broadcast_in_dim_reshape.3.a_ref), custom_call_target="tpu_custom_call" | custom-call | tf_op jit(solution)/shard_map/pallas_call | solution.py:170
  62.3 0.0 copy-done
  62.3 0.2 fusion.35
  62.5 1.7 %fusion.36 = f32[2048,256]{1,0:T(8,128)S(1)} fusion(f32[16,2048]{1,0:T(8,128)} %shard_map.150, bf16[256,16]{0,1:T(8,128)(2,1)S(1)} %copy-done), kind=kOutput, calls=%fused_computation.60 | convolution fusion | flops 50331648 | bytes 2236416 | tf_op jit(solution)/shard_map/dot_general | solution.py:214
  64.2 0.0 copy-done.11
  64.2 6.8 %fusion.15 = f32[256,32,64]{0,2,1:T(8,128)} fusion(f32[256,32,64]{0,2,1:T(8,128)S(1)} %bitcast.46, f32[256,32,64]{0,2,1:T(8,128)S(1)} %bitcast.47, f32[256,256]{1,0:T(8,128)S(1)} %fusion.35, f32[32,256]{1,0:T(8,128)S(1)} %get-tuple-element.4, pred[256,256]{1,0:T(8,128)(4,1)S(1)} %iota_compare_fusion.1, f32[32]{0:T(128)S(1)} %copy-done.11, ...), kind=kOutput, calls=%fused_computation.18 | convolution fusion | flops 816316416 | bytes 6717568 | tf_op jit(solution)/shard_map/hts,shp->thp/dot_general | solution.py:205
  71.0 0.0 copy-start.10
  71.0 0.0 copy-start.6
  71.0 2.0 %copy.50 = f32[256,2048]{1,0:T(8,128)S(1)} copy(f32[256,2048]{0,1:T(8,128)} %bitcast.48) | data formatting | bytes 4194304 | tf_op jit(solution)/shard_map/reshape | solution.py:218
  73.0 0.1 pad.2.clone
  73.1 0.0 copy-done.10
  73.1 0.1 dynamic_slice.3
  73.2 0.0 copy-done.6
  73.2 0.0 copy-done.7
  73.2 0.1 broadcast_compare_fusion.1
  73.3 0.1 pad_add_fusion.1
  73.4 0.3 copy-done.9
  73.7 0.1 broadcast_subtract_fusion
  73.8 0.0 copy-start.2
  73.8 0.1 pad_add_fusion
  73.9 0.8 and_reduce_fusion
  74.6 0.1 not_and_fusion
  74.7 0.0 copy-done.2
  74.7 0.1 add_select_fusion
  74.8 0.0 copy-done.3
  74.8 0.2 broadcast_in_dim.93
  75.0 0.0 copy-start.8
  75.0 0.9 reshape_reshape.4.refs_3_
  75.8 0.1 pad.10.clone
  75.9 0.7 broadcast_in_dim.48
  76.6 0.8 add_add_fusion
  77.5 0.1 copy.43
  77.6 2.1 %select_reduce_fusion = s32[8,4,18]{0,2,1:T(8,128)S(1)} fusion(s32[8,4,18]{0,2,1:T(8,128)S(1)} %copy.43, s32[128]{0:T(128)} %param.19), kind=kLoop, calls=%fused_computation.30 | loop fusion | flops 220608 | bytes 5120 | tf_op jit(solution)/shard_map/reduce_sum | solution.py:44
  79.6 0.1 copy.44
  79.7 0.7 reshape.97.refs_2_
  80.4 0.0 copy-done.1
  80.4 0.7 multiply_reduce_fusion
  81.1 16.7 %psum.7 = f32[256]{0:T(256)S(1)} all-reduce(f32[256]{0:T(256)S(1)} %multiply_reduce_fusion), channel_id=1, replica_groups=mesh['ctx'=32,'tp'=8] {'tp'}, use_global_device_ids=true, to_apply=%region_5.6 | all-reduce | flops 256 | bytes 2048 | tf_op jit(solution)/shard_map/psum | solution.py:221
  97.8 0.7 fusion.31.refs_4_
  98.5 0.0 copy-done.8
  98.5 1.7 %multiply_convert_fusion = bf16[256,2048]{1,0:T(8,128)(2,1)} fusion(f32[2048]{0:T(1024)S(1)} %copy-done.8, f32[256]{0:T(256)S(1)} %add_rsqrt_fusion, f32[256,2048]{1,0:T(8,128)S(1)} %copy.50, bf16[256,2048]{1,0:T(8,128)(2,1)S(1)} %copy-done.1), kind=kLoop, calls=%fused_computation.19 | loop fusion | flops 4718592 | bytes 4203520 | tf_op jit(solution)/shard_map/convert_element_type | solution.py:223
  100.3 16.9 %shard_map.149 = bf16[256,1024]{1,0:T(8,128)(2,1)} custom-call(bf16[256,1024]{1,0:T(8,128)(2,1)} %refs_0_.1, bf16[2,8192,128]{2,1,0:T(8,128)(2,1)} %all-gather.2.cloned.1.call-done.refs_1_, s32[576]{0:T(1024)} %reshape.97.refs_2_, f32[32,1,1152]{2,1,0:T(1,128)} %reshape_reshape.4.refs_3_, f32[64,1152]{1,0:T(8,128)} %fusion.31.refs_4_), custom_call_target="tpu_custom_call" | custom-call | flops 1207959552 | bytes 5242880 | tf_op jit(solution)/shard_map/pallas_call | solution.py:89
  (14 shorter events, 0.1 us)
Async XLA Ops:
  7.2 55.1 %copy-start = (bf16[256,16]{0,1:T(8,128)(2,1)S(1)}, bf16[256,16]{0,1:T(8,128)(2,1)}, u32[]{:S(2)}) copy-start(bf16[256,16]{0,1:T(8,128)(2,1)} %param.23) | copy-start | bytes 24580
  7.2 5.8 %copy-start.4 = (f32[256,32]{0,1:T(8,128)S(1)}, f32[256,32]{0,1:T(8,128)}, u32[]{:S(2)}) copy-start(f32[256,32]{0,1:T(8,128)} %param.24) | copy-start | bytes 98308
  7.2 5.8 %copy-start.5 = (bf16[256,16]{0,1:T(8,128)(2,1)S(1)}, bf16[256,16]{0,1:T(8,128)(2,1)}, u32[]{:S(2)}) copy-start(bf16[256,16]{0,1:T(8,128)(2,1)} %param.22) | copy-start | bytes 24580
  7.2 93.1 %all-gather.2.cloned.1.call-start = ((), (), s32[]{:S(2)}) async-start(), calls=%async_computation | async-start | bytes 4325376 | tf_op jit(solution)/shard_map/all_gather | solution.py:82
  13.9 50.3 %copy-start.11 = (f32[32]{0:T(128)S(1)}, f32[32]{0:T(128)}, u32[]{:S(2)}) copy-start(f32[32]{0:T(128)} %param.26) | copy-start | bytes 388
  71.0 2.1 %copy-start.10 = (s32[128]{0:T(128)S(1)}, s32[128]{0:T(128)}, u32[]{:S(2)}) copy-start(s32[128]{0:T(128)} %param.19) | copy-start | bytes 1540
  71.0 2.2 %copy-start.6 = (s32[8,8]{1,0:T(8,128)S(1)}, s32[8,8]{1,0:T(8,128)}, u32[]{:S(2)}) copy-start(s32[8,8]{1,0:T(8,128)} %param.17) | copy-start | bytes 772
  71.0 2.2 %copy-start.7 = (s32[8,8]{1,0:T(8,128)S(1)}, s32[8,8]{1,0:T(8,128)}, u32[]{:S(2)}) copy-start(s32[8,8]{1,0:T(8,128)} %param.18) | copy-start | bytes 772
  71.0 9.5 %copy-start.1 = (bf16[256,2048]{1,0:T(8,128)(2,1)S(1)}, bf16[256,2048]{1,0:T(8,128)(2,1)}, u32[]{:S(2)}) copy-start(bf16[256,2048]{1,0:T(8,128)(2,1)} %param.21) | copy-start | bytes 3145732
  73.2 0.5 copy-start.9
  73.8 1.0 copy-start.3
  73.8 0.9 copy-start.2
  75.0 23.6 %copy-start.8 = (f32[2048]{0:T(1024)S(1)}, f32[2048]{0:T(1024)}, u32[]{:S(2)}) copy-start(f32[2048]{0:T(1024)} %param.27) | copy-start | bytes 24580
Sparse Core Ops, SparseCore 0:
  11.2 86.1 all-gather.1

commit v6 on v5

--- a/solution.py
+++ b/solution.py
@@ -73,7 +73,7 @@
         o_ref[rows, cols] = (out / denom).astype(o_ref.dtype)
         return carry
 
-    lax.fori_loop(0, units, unit, 0, unroll=4)
+    lax.fori_loop(0, units, unit, 0, unroll=units)
 
 
 def attend_sparse(queries, keys, values, vertical, slash, block_position):

time: 125 us -> 124 us (level)
  Pallas kernels: 63.6 us -> 62.2 us
    pallas_call x1, Pallas kernels: 16.9 us -> 15.5 us  [attend_sparse(): pl.pallas_call(lambda *refs: sparse_attention_kernel(slots, blocks_here,...]
where the time goes in v6:
time: 124 us; the launch traced here: 123 us
  Pallas kernels  62.2 us (50%)
  blocking collectives  16.7 us (13%)
  between operations  14.3 us (12%)
  other arithmetic  11.1 us (9%)
  matrix products  9.58 us (8%)
  local copies, waits for them, and re-layouts  8.72 us (7%)
    pallas_call x1, Pallas kernels, carry_scan(): pl.pallas_call(carry_scan_kernel, out_shape=jax.ShapeDtypeStruct(local_st...  46.7 us
    psum x1, blocking collectives, mamba_mix(): squares = lax.psum(jnp.sum(gated * gated, axis=1), 'tp')  16.7 us
    pallas_call x1, Pallas kernels, attend_sparse(): pl.pallas_call(lambda *refs: sparse_attention_kernel(slots, blocks_here,...  15.5 us
    dot_general x1, matrix products, mamba_mix(): jnp.einsum('hts,shp->thp', decay * inner[None], weighted, precision=careful)  6.76 us
  transfers between devices with their start and end apart: 1, of which 0 were waited for; matrix products, arithmetic and copies ran while one was open for 22% of the time, Pallas kernels for 38%

profile of v6, /device:TPU:1, one launch (start us, length us, event | category | flops | bytes accessed | tf_op | source)
XLA Modules:
  0.0 122.6 jit_solution(13758956718425314920)
XLA Ops:
  7.2 0.0 copy-start
  7.2 0.0 copy-start.4
  7.2 0.0 copy-start.5
  7.2 0.0 all-gather.2.cloned.1.call-start
  7.2 1.5 %pad_maximum_fusion = bf16[2,256,128]{2,1,0:T(8,128)(2,1)} fusion(bf16[1,256,128]{2,1,0:T(8,128)(2,1)} %bitcast.49, bf16[1,256,128]{2,1,0:T(8,128)(2,1)} %bitcast.50), kind=kLoop, calls=%fused_computation.35 | loop fusion | flops 65536 | bytes 262144 | tf_op jit(solution)/shard_map/stack | solution.py:82
  8.8 0.0 all-gather.2.cloned.1.call-update
  8.8 0.7 exponential_negate_fusion
  9.5 0.8 copy_bitcast_fusion.1
  10.3 0.6 reduce-window.6
  10.9 0.2 slice_reduce_fusion
  11.1 1.5 %copy.46 = f32[256,2048]{0,1:T(8,128)S(1)} copy(bf16[256,2048]{1,0:T(8,128)(2,1)} %param.20) | data formatting | bytes 3145728 | tf_op jit(solution)/shard_map/reshape | solution.py:191
  12.6 0.1 copy_bitcast_fusion
  12.7 0.2 slice_reduce_fusion.1
  12.9 0.1 bitcast_exponential_fusion
  13.0 0.0 copy-done.4
  13.0 0.0 copy-done.5
  13.0 0.9 fusion.24
  13.9 0.0 copy-start.11
  13.9 0.1 copy.49
  14.0 0.8 reshape.102.s_ref
  14.8 0.1 broadcast_in_dim.97
  14.9 0.7 broadcast_in_dim_reshape.3.a_ref
  15.5 46.7 %shard_map.150 = f32[16,2048]{1,0:T(8,128)} custom-call(f32[16,2048]{1,0:T(8,128)} %reshape.102.s_ref, f32[1,2048]{1,0:T(1,128)} %broadcast_in_dim_reshape.3.a_ref), custom_call_target="tpu_custom_call" | custom-call | tf_op jit(solution)/shard_map/pallas_call | solution.py:170
  62.3 0.0 copy-done
  62.3 0.2 fusion.35
  62.5 1.7 %fusion.36 = f32[2048,256]{1,0:T(8,128)S(1)} fusion(f32[16,2048]{1,0:T(8,128)} %shard_map.150, bf16[256,16]{0,1:T(8,128)(2,1)S(1)} %copy-done), kind=kOutput, calls=%fused_computation.60 | convolution fusion | flops 50331648 | bytes 2236416 | tf_op jit(solution)/shard_map/dot_general | solution.py:214
  64.2 0.0 copy-done.11
  64.2 6.8 %fusion.15 = f32[256,32,64]{0,2,1:T(8,128)} fusion(f32[256,32,64]{0,2,1:T(8,128)S(1)} %bitcast.46, f32[256,32,64]{0,2,1:T(8,128)S(1)} %bitcast.47, f32[256,256]{1,0:T(8,128)S(1)} %fusion.35, f32[32,256]{1,0:T(8,128)S(1)} %get-tuple-element.4, pred[256,256]{1,0:T(8,128)(4,1)S(1)} %iota_compare_fusion.1, f32[32]{0:T(128)S(1)} %copy-done.11, ...), kind=kOutput, calls=%fused_computation.18 | convolution fusion | flops 816316416 | bytes 6717568 | tf_op jit(solution)/shard_map/hts,shp->thp/dot_general | solution.py:205
  71.0 0.0 copy-start.10
  71.0 0.0 copy-start.6
  71.0 2.0 %copy.50 = f32[256,2048]{1,0:T(8,128)S(1)} copy(f32[256,2048]{0,1:T(8,128)} %bitcast.48) | data formatting | bytes 4194304 | tf_op jit(solution)/shard_map/reshape | solution.py:218
  73.0 0.1 pad.2.clone
  73.1 0.0 copy-done.10
  73.1 0.1 dynamic_slice.3
  73.2 0.0 copy-done.6
  73.2 0.0 copy-done.7
  73.2 0.1 broadcast_compare_fusion.1
  73.3 0.1 pad_add_fusion.1
  73.3 0.3 copy-done.9
  73.7 0.1 broadcast_subtract_fusion
  73.8 0.0 copy-start.2
  73.8 0.1 pad_add_fusion
  73.9 0.8 and_reduce_fusion
  74.6 0.1 not_and_fusion
  74.7 0.0 copy-done.2
  74.7 0.1 add_select_fusion
  74.8 0.0 copy-done.3
  74.8 0.2 broadcast_in_dim.93
  75.0 0.0 copy-start.8
  75.0 0.9 reshape_reshape.4.refs_3_
  75.8 0.1 pad.10.clone
  75.9 0.7 broadcast_in_dim.48
  76.6 0.8 add_add_fusion
  77.4 0.1 copy.43
  77.6 2.1 %select_reduce_fusion = s32[8,4,18]{0,2,1:T(8,128)S(1)} fusion(s32[8,4,18]{0,2,1:T(8,128)S(1)} %copy.43, s32[128]{0:T(128)} %param.19), kind=kLoop, calls=%fused_computation.30 | loop fusion | flops 220608 | bytes 5120 | tf_op jit(solution)/shard_map/reduce_sum | solution.py:44
  79.6 0.1 copy.44
  79.7 0.7 reshape.97.refs_2_
  80.4 0.0 copy-done.1
  80.4 0.7 multiply_reduce_fusion
  81.1 16.7 %psum.7 = f32[256]{0:T(256)S(1)} all-reduce(f32[256]{0:T(256)S(1)} %multiply_reduce_fusion), channel_id=1, replica_groups=mesh['ctx'=32,'tp'=8] {'tp'}, use_global_device_ids=true, to_apply=%region_5.6 | all-reduce | flops 256 | bytes 2048 | tf_op jit(solution)/shard_map/psum | solution.py:221
  97.8 0.7 fusion.31.refs_4_
  98.5 0.0 copy-done.8
  98.5 1.7 %multiply_convert_fusion = bf16[256,2048]{1,0:T(8,128)(2,1)} fusion(f32[2048]{0:T(1024)S(1)} %copy-done.8, f32[256]{0:T(256)S(1)} %add_rsqrt_fusion, f32[256,2048]{1,0:T(8,128)S(1)} %copy.50, bf16[256,2048]{1,0:T(8,128)(2,1)S(1)} %copy-done.1), kind=kLoop, calls=%fused_computation.19 | loop fusion | flops 4718592 | bytes 4203520 | tf_op jit(solution)/shard_map/convert_element_type | solution.py:223
  100.3 15.5 %shard_map.149 = bf16[256,1024]{1,0:T(8,128)(2,1)} custom-call(bf16[256,1024]{1,0:T(8,128)(2,1)} %refs_0_.1, bf16[2,8192,128]{2,1,0:T(8,128)(2,1)} %all-gather.2.cloned.1.call-done.refs_1_, s32[576]{0:T(1024)} %reshape.97.refs_2_, f32[32,1,1152]{2,1,0:T(1,128)} %reshape_reshape.4.refs_3_, f32[64,1152]{1,0:T(8,128)} %fusion.31.refs_4_), custom_call_target="tpu_custom_call" | custom-call | flops 1207959552 | bytes 5242880 | tf_op jit(solution)/shard_map/pallas_call | solution.py:89
  (14 shorter events, 0.1 us)
Async XLA Ops:
  7.2 55.1 %copy-start = (bf16[256,16]{0,1:T(8,128)(2,1)S(1)}, bf16[256,16]{0,1:T(8,128)(2,1)}, u32[]{:S(2)}) copy-start(bf16[256,16]{0,1:T(8,128)(2,1)} %param.23) | copy-start | bytes 24580
  7.2 5.8 %copy-start.4 = (f32[256,32]{0,1:T(8,128)S(1)}, f32[256,32]{0,1:T(8,128)}, u32[]{:S(2)}) copy-start(f32[256,32]{0,1:T(8,128)} %param.24) | copy-start | bytes 98308
  7.2 5.8 %copy-start.5 = (bf16[256,16]{0,1:T(8,128)(2,1)S(1)}, bf16[256,16]{0,1:T(8,128)(2,1)}, u32[]{:S(2)}) copy-start(bf16[256,16]{0,1:T(8,128)(2,1)} %param.22) | copy-start | bytes 24580
  7.2 93.0 %all-gather.2.cloned.1.call-start = ((), (), s32[]{:S(2)}) async-start(), calls=%async_computation | async-start | bytes 4325376 | tf_op jit(solution)/shard_map/all_gather | solution.py:82
  13.9 50.3 %copy-start.11 = (f32[32]{0:T(128)S(1)}, f32[32]{0:T(128)}, u32[]{:S(2)}) copy-start(f32[32]{0:T(128)} %param.26) | copy-start | bytes 388
  71.0 2.1 %copy-start.10 = (s32[128]{0:T(128)S(1)}, s32[128]{0:T(128)}, u32[]{:S(2)}) copy-start(s32[128]{0:T(128)} %param.19) | copy-start | bytes 1540
  71.0 2.2 %copy-start.6 = (s32[8,8]{1,0:T(8,128)S(1)}, s32[8,8]{1,0:T(8,128)}, u32[]{:S(2)}) copy-start(s32[8,8]{1,0:T(8,128)} %param.17) | copy-start | bytes 772
  71.0 2.2 %copy-start.7 = (s32[8,8]{1,0:T(8,128)S(1)}, s32[8,8]{1,0:T(8,128)}, u32[]{:S(2)}) copy-start(s32[8,8]{1,0:T(8,128)} %param.18) | copy-start | bytes 772
  71.0 9.4 %copy-start.1 = (bf16[256,2048]{1,0:T(8,128)(2,1)S(1)}, bf16[256,2048]{1,0:T(8,128)(2,1)}, u32[]{:S(2)}) copy-start(bf16[256,2048]{1,0:T(8,128)(2,1)} %param.21) | copy-start | bytes 3145732
  73.2 0.5 copy-start.9
  73.8 1.0 copy-start.3
  73.8 0.9 copy-start.2
  75.0 23.6 %copy-start.8 = (f32[2048]{0:T(1024)S(1)}, f32[2048]{0:T(1024)}, u32[]{:S(2)}) copy-start(f32[2048]{0:T(1024)} %param.27) | copy-start | bytes 24580
Sparse Core Ops, SparseCore 0:
  11.2 86.1 all-gather.1

commit v7 on v6

--- a/solution.py
+++ b/solution.py
@@ -76,10 +76,10 @@
     lax.fori_loop(0, units, unit, 0, unroll=units)
 
 
-def attend_sparse(queries, keys, values, vertical, slash, block_position):
+def attend_sparse(queries, kv_local, vertical, slash, block_position):
     row_count = queries.shape[0]
     blocks_here = row_count // BLOCK
-    kv_all = lax.all_gather(jnp.stack((keys, values)), "ctx", axis=1, tiled=True)
+    kv_all = lax.all_gather(kv_local, "ctx", axis=1, tiled=True)
     index, col_bias, slots = key_block_table(vertical, slash, block_position, blocks_here)
     units = col_bias.shape[0]
     r = lax.broadcasted_iota(jnp.int32, (BLOCK, slots * BLOCK), 0)
@@ -183,6 +183,64 @@
     )(local_state, carry_decay)
 
 
+def tp_sum_kernel(x_ref, o_ref, got, sems):
+    n = lax.axis_size("tp")
+    me = lax.axis_index("tp")
+    row = lax.axis_index("ctx")
+    barrier = pltpu.get_barrier_semaphore()
+    for k in range(1, n):
+        pl.semaphore_signal(
+            barrier, inc=1, device_id=(row, lax.rem(me + k, n)), device_id_type=pl.DeviceIdType.MESH
+        )
+    pl.semaphore_wait(barrier, n - 1)
+    copies = []
+    for k in range(1, n):
+        copy = pltpu.make_async_remote_copy(
+            src_ref=x_ref,
+            dst_ref=got.at[me],
+            send_sem=sems.at[0, k],
+            recv_sem=sems.at[1, k],
+            device_id=(row, lax.rem(me + k, n)),
+            device_id_type=pl.DeviceIdType.MESH,
+        )
+        copy.start()
+        copies.append(copy)
+    got[me] = x_ref[...]
+    for k in range(1, n):
+        copies[k - 1].wait_send()
+        arriving = pltpu.make_async_remote_copy(
+            src_ref=x_ref,
+            dst_ref=got.at[lax.rem(me - k + n, n)],
+            send_sem=sems.at[0, k],
+            recv_sem=sems.at[1, k],
+            device_id=(row, lax.rem(me + k, n)),
+            device_id_type=pl.DeviceIdType.MESH,
+        )
+        arriving.wait_recv()
+    total = got[0]
+    for j in range(1, n):
+        total = total + got[j]
+    o_ref[...] = total
+
+
+def tp_sum(values):
+    n = lax.axis_size("tp")
+    rows = values.size // 128
+    shaped = jnp.pad(values.reshape(rows, 128), ((0, (-rows) % 8), (0, 0)))
+    out = pl.pallas_call(
+        tp_sum_kernel,
+        out_shape=jax.ShapeDtypeStruct(shaped.shape, shaped.dtype),
+        in_specs=[pl.BlockSpec(memory_space=pltpu.VMEM)],
+        out_specs=pl.BlockSpec(memory_space=pltpu.VMEM),
+        scratch_shapes=[
+            pltpu.VMEM((n,) + shaped.shape, shaped.dtype),
+            pltpu.SemaphoreType.DMA((2, n)),
+        ],
+        compiler_params=pltpu.CompilerParams(collective_id=1, has_side_effects=True),
+    )(shaped)
+    return out.reshape(-1)[: values.size]
+
+
 def mamba_mix(ssm_input, gate, state_in, state_out, step_size, decay_log, skip_gain, norm_gain):
     careful = lax.Precision.HIGH
     row_count = ssm_input.shape[0]
@@ -218,7 +276,7 @@
     mixed = (within + from_past + skip_gain[None, :, None] * inputs).reshape(row_count, inner_width)
     gate_full = gate.astype(jnp.float32)
     gated = mixed * gate_full * jax.nn.sigmoid(gate_full)
-    squares = lax.psum(jnp.sum(gated * gated, axis=1), "tp")
+    squares = tp_sum(jnp.sum(gated * gated, axis=1))
     scaled = gated * lax.rsqrt(squares / INNER + 1e-05)[:, None] * norm_gain[None, :]
     return scaled.astype(jnp.bfloat16)
 
@@ -239,7 +297,11 @@
     skip_gain,
     norm_gain,
 ):
-    attention_out = attend_sparse(queries, keys, values, vertical, slash, block_position)
+    kv_local = jnp.stack((keys, values))
+    kv_local, ssm_input, step_size, decay_log, state_in = lax.optimization_barrier(
+        (kv_local, ssm_input, step_size, decay_log, state_in)
+    )
+    attention_out = attend_sparse(queries, kv_local, vertical, slash, block_position)
     recurrent_mixer_result = mamba_mix(
         ssm_input, gate, state_in, state_out, step_size, decay_log, skip_gain, norm_gain
     )

time: 124 us -> 122 us (0.984)
  blocking collectives: 16.7 us -> 0 us
  Pallas kernels: 62.2 us -> 74.4 us
    psum x1 -> x0, blocking collectives: 16.7 us -> none  [mamba_mix(): squares = lax.psum(jnp.sum(gated * gated, axis=1), 'tp')]
    pallas_call x0 -> x1, Pallas kernels: none -> 12.2 us  [tp_sum(): pl.pallas_call(tp_sum_kernel, out_shape=jax.ShapeDtypeStruct(shaped.shape...]
  transfers between devices with their start and end apart: 1 -> 1, of which waited for: 0 -> 1; matrix products, arithmetic and copies ran while one was open for 22% -> 24% of each run, Pallas kernels for 38% -> 49%
where the time goes in v7:
time: 122 us; the launch traced here: 120 us
  Pallas kernels  74.4 us (61%)
  between operations  14.3 us (12%)
  other arithmetic  12.1 us (10%)
  matrix products  9.91 us (8%)
  local copies, waits for them, and re-layouts  8.88 us (7%)
    pallas_call x1, Pallas kernels, carry_scan(): pl.pallas_call(carry_scan_kernel, out_shape=jax.ShapeDtypeStruct(local_st...  46.8 us
    pallas_call x1, Pallas kernels, attend_sparse(): pl.pallas_call(lambda *refs: sparse_attention_kernel(slots, blocks_here,...  15.5 us
    pallas_call x1, Pallas kernels, tp_sum(): pl.pallas_call(tp_sum_kernel, out_shape=jax.ShapeDtypeStruct(shaped.shape...  12.2 us
    dot_general x1, matrix products, mamba_mix(): jnp.einsum('hts,shp->thp', decay * inner[None], weighted, precision=careful)  6.72 us
  transfers between devices with their start and end apart: 1, of which 1 were waited for; matrix products, arithmetic and copies ran while one was open for 24% of the time, Pallas kernels for 49%

profile of v7, /device:TPU:1, one launch (start us, length us, event | category | flops | bytes accessed | tf_op | source)
XLA Modules:
  0.0 120.0 jit_solution(15518234252408432647)
XLA Ops:
  7.2 0.0 copy-start
  7.2 0.0 copy-start.5
  7.2 0.0 all-gather.2.cloned.1.call-start
  7.2 1.5 %pad_maximum_fusion = bf16[2,256,128]{2,1,0:T(8,128)(2,1)} fusion(bf16[1,256,128]{2,1,0:T(8,128)(2,1)} %bitcast.55, bf16[1,256,128]{2,1,0:T(8,128)(2,1)} %bitcast.56), kind=kLoop, calls=%fused_computation.31 | loop fusion | flops 65536 | bytes 262144 | tf_op jit(solution)/shard_map/stack | solution.py:300
  8.8 0.0 all-gather.2.cloned.1.call-update
  8.8 0.7 exponential_negate_fusion
  9.5 0.8 copy_bitcast_fusion.1
  10.3 0.6 reduce-window.6
  10.9 0.2 slice_reduce_fusion
  11.1 1.5 %copy.44 = f32[256,2048]{0,1:T(8,128)S(1)} copy(bf16[256,2048]{1,0:T(8,128)(2,1)} %param.20) | data formatting | bytes 3145728 | tf_op jit(solution)/shard_map/reshape | solution.py:249
  12.6 0.1 copy_bitcast_fusion
  12.7 0.2 slice_reduce_fusion.1
  12.9 0.1 broadcast_in_dim.97
  12.9 0.7 broadcast_in_dim_reshape.3.a_ref
  13.6 0.0 copy-done
  13.6 0.0 copy-done.5
  13.6 0.2 convolution_bitcast_fusion
  13.8 0.1 copy.47
  14.0 0.1 bitcast_exponential_fusion
  14.1 0.0 copy-done.4
  14.1 0.3 multiply_multiply_fusion
  14.4 0.0 copy-start.11
  14.4 1.3 %fusion.26.s_ref = f32[16,2048]{1,0:T(8,128)} fusion(bf16[256,16]{0,1:T(8,128)(2,1)S(1)} %copy-done.5, f32[2048,256]{1,0:T(8,128)S(1)} %bitcast.52), kind=kOutput, calls=%fused_computation.54 | convolution fusion | flops 50331648 | bytes 2236416 | tf_op jit(solution)/shard_map/sn,shp->nhp/dot_general | solution.py:265
  15.7 46.8 %shard_map.150 = f32[16,2048]{1,0:T(8,128)} custom-call(f32[16,2048]{1,0:T(8,128)} %fusion.26.s_ref, f32[1,2048]{1,0:T(1,128)} %broadcast_in_dim_reshape.3.a_ref), custom_call_target="tpu_custom_call" | custom-call | tf_op jit(solution)/shard_map/pallas_call | solution.py:170
  62.6 1.7 %fusion.27 = f32[2048,256]{1,0:T(8,128)S(1)} fusion(f32[16,2048]{1,0:T(8,128)} %shard_map.150, bf16[256,16]{0,1:T(8,128)(2,1)S(1)} %copy-done), kind=kOutput, calls=%fused_computation.55 | convolution fusion | flops 50331648 | bytes 2236416 | tf_op jit(solution)/shard_map/dot_general | solution.py:272
  64.2 0.0 copy-done.11
  64.2 6.7 %fusion.15 = f32[256,32,64]{0,2,1:T(8,128)} fusion(f32[256,32,64]{0,2,1:T(8,128)S(1)} %bitcast.51, f32[256,32,64]{0,2,1:T(8,128)S(1)} %bitcast.53, f32[256,256]{1,0:T(8,128)S(1)} %copy.47, f32[32,256]{1,0:T(8,128)S(1)} %get-tuple-element.14, pred[256,256]{1,0:T(8,128)(4,1)S(1)} %iota_compare_fusion.1, f32[32]{0:T(128)S(1)} %copy-done.11, ...), kind=kOutput, calls=%fused_computation.18 | convolution fusion | flops 816316416 | bytes 6717568 | tf_op jit(solution)/shard_map/hts,shp->thp/dot_general | solution.py:263
  71.0 2.2 %copy.48 = f32[256,2048]{1,0:T(8,128)S(1)} copy(f32[256,2048]{0,1:T(8,128)} %bitcast.54) | data formatting | bytes 4194304 | tf_op jit(solution)/shard_map/reshape | solution.py:276
  73.2 0.0 copy-done.1
  73.2 0.0 copy-start.10
  73.2 0.0 copy-start.6
  73.2 0.0 copy-start.7
  73.2 0.0 copy-start.8
  73.2 0.7 multiply_reduce_fusion
  73.9 0.6 pad.4.x_ref
  74.5 12.2 %shard_map.151 = f32[8,128]{1,0:T(8,128)} custom-call(f32[8,128]{1,0:T(8,128)} %pad.4.x_ref), custom_call_target="tpu_custom_call" | custom-call | tf_op jit(solution)/shard_map/pallas_call | solution.py:230
  86.7 0.1 pad.7.clone
  86.8 0.0 copy-done.10
  86.8 0.1 dynamic_slice.3
  86.9 0.0 copy-done.6
  86.9 0.1 broadcast_compare_fusion.1
  87.0 0.1 pad_add_fusion.1
  87.1 0.4 copy-done.9
  87.5 0.1 broadcast_subtract_fusion
  87.5 0.0 copy-start.2
  87.5 0.1 pad_add_fusion
  87.6 0.8 and_reduce_fusion
  88.4 0.1 not_and_fusion
  88.5 0.0 copy-done.2
  88.5 0.1 add_select_fusion
  88.6 0.2 broadcast_in_dim.93
  88.7 0.9 reshape_reshape.4.refs_3_
  89.6 0.1 pad.15.clone
  89.7 0.7 broadcast_in_dim.48
  90.4 0.8 add_add_fusion
  91.2 0.1 copy.41
  91.4 2.0 %select_reduce_fusion = s32[8,4,18]{0,2,1:T(8,128)S(1)} fusion(s32[8,4,18]{0,2,1:T(8,128)S(1)} %copy.41, s32[128]{0:T(128)} %param.19), kind=kLoop, calls=%fused_computation.26 | loop fusion | flops 220608 | bytes 5120 | tf_op jit(solution)/shard_map/reduce_sum | solution.py:44
  93.4 0.1 copy.42
  93.5 0.7 reshape.112.refs_2_
  94.2 0.7 rsqrt_bitcast_fusion
  94.9 0.7 fusion.23.refs_4_
  95.6 1.7 %multiply_convert_fusion = bf16[256,2048]{1,0:T(8,128)(2,1)} fusion(f32[2048]{0:T(1024)S(1)} %copy-done.8, f32[256]{0:T(256)S(1)} %rsqrt_bitcast_fusion, f32[256,2048]{1,0:T(8,128)S(1)} %copy.48, bf16[256,2048]{1,0:T(8,128)(2,1)S(1)} %copy-done.1), kind=kLoop, calls=%fused_computation.19 | loop fusion | flops 4718592 | bytes 4203520 | tf_op jit(solution)/shard_map/convert_element_type | solution.py:281
  97.3 0.4 all-gather.2.cloned.1.call-done.refs_1_
  97.7 15.5 %shard_map.149 = bf16[256,1024]{1,0:T(8,128)(2,1)} custom-call(bf16[256,1024]{1,0:T(8,128)(2,1)} %refs_0_.1, bf16[2,8192,128]{2,1,0:T(8,128)(2,1)} %all-gather.2.cloned.1.call-done.refs_1_, s32[576]{0:T(1024)} %reshape.112.refs_2_, f32[32,1,1152]{2,1,0:T(1,128)} %reshape_reshape.4.refs_3_, f32[64,1152]{1,0:T(8,128)} %fusion.23.refs_4_), custom_call_target="tpu_custom_call" | custom-call | flops 1207959552 | bytes 5242880 | tf_op jit(solution)/shard_map/pallas_call | solution.py:89
  (15 shorter events, 0.1 us)
Async XLA Ops:
  7.2 6.4 %copy-start = (bf16[256,16]{0,1:T(8,128)(2,1)S(1)}, bf16[256,16]{0,1:T(8,128)(2,1)}, u32[]{:S(2)}) copy-start(bf16[256,16]{0,1:T(8,128)(2,1)} %param.23) | copy-start | bytes 24580
  7.2 6.4 %copy-start.5 = (bf16[256,16]{0,1:T(8,128)(2,1)S(1)}, bf16[256,16]{0,1:T(8,128)(2,1)}, u32[]{:S(2)}) copy-start(bf16[256,16]{0,1:T(8,128)(2,1)} %param.22) | copy-start | bytes 24580
  7.2 90.5 %all-gather.2.cloned.1.call-start = ((), (), s32[]{:S(2)}) async-start(), calls=%async_computation | async-start | bytes 4325376 | tf_op jit(solution)/shard_map/all_gather | solution.py:82
  11.1 3.0 %copy-start.4 = (f32[256,32]{0,1:T(8,128)S(1)}, f32[256,32]{0,1:T(8,128)}, u32[]{:S(2)}) copy-start(f32[256,32]{0,1:T(8,128)} %param.24) | copy-start | bytes 98308
  14.4 49.8 %copy-start.11 = (f32[32]{0:T(128)S(1)}, f32[32]{0:T(128)}, u32[]{:S(2)}) copy-start(f32[32]{0:T(128)} %param.26) | copy-start | bytes 388
  71.0 2.2 %copy-start.1 = (bf16[256,2048]{1,0:T(8,128)(2,1)S(1)}, bf16[256,2048]{1,0:T(8,128)(2,1)}, u32[]{:S(2)}) copy-start(bf16[256,2048]{1,0:T(8,128)(2,1)} %param.21) | copy-start | bytes 3145732
  73.2 13.6 %copy-start.10 = (s32[128]{0:T(128)S(1)}, s32[128]{0:T(128)}, u32[]{:S(2)}) copy-start(s32[128]{0:T(128)} %param.19) | copy-start | bytes 1540
  73.2 13.7 %copy-start.6 = (s32[8,8]{1,0:T(8,128)S(1)}, s32[8,8]{1,0:T(8,128)}, u32[]{:S(2)}) copy-start(s32[8,8]{1,0:T(8,128)} %param.17) | copy-start | bytes 772
  73.2 13.7 %copy-start.7 = (s32[8,8]{1,0:T(8,128)S(1)}, s32[8,8]{1,0:T(8,128)}, u32[]{:S(2)}) copy-start(s32[8,8]{1,0:T(8,128)} %param.18) | copy-start | bytes 772
  73.2 22.4 %copy-start.8 = (f32[2048]{0:T(1024)S(1)}, f32[2048]{0:T(1024)}, u32[]{:S(2)}) copy-start(f32[2048]{0:T(1024)} %param.27) | copy-start | bytes 24580
  86.9 0.6 copy-start.9
  87.5 1.0 copy-start.3
  87.5 0.9 copy-start.2
Sparse Core Ops, SparseCore 0:
  11.2 86.4 all-gather.1

commit v8 on v7

--- a/solution.py
+++ b/solution.py
@@ -109,14 +109,14 @@
     )(queries, kv_all, index, col_bias, causal_bias)
 
 
-SCAN_SHIFTS = (2, 4, 8, 16)
+SCAN_ROUNDS = ((1, 2, 3, 4), (4, 8, 12), (16,))
 
 
 def carry_scan_kernel(s_ref, a_ref, o_ref, cur_s, cur_a, got_s, got_a, sems):
     n = lax.axis_size("ctx")
     me = lax.axis_index("ctx")
     tp = lax.axis_index("tp")
-    shifts = (1,) + SCAN_SHIFTS
+    shifts = [k for ks in SCAN_ROUNDS for k in ks]
     barrier = pltpu.get_barrier_semaphore()
     partners = sorted({k % n for k in shifts} | {(-k) % n for k in shifts})
     for k in partners:
@@ -142,31 +142,41 @@
             copy.start()
         return copies
 
-    def keep_of(k):
-        return ((me - k + n) // n).astype(jnp.float32)
-
-    first = send(0, 1, s_ref, a_ref) + send(1, 2, s_ref, a_ref)
-    for copy in first:
-        copy.wait()
-    keep1, keep2 = keep_of(1), keep_of(2)
-    a1, a2 = got_a[0], got_a[1]
-    state = keep1 * (got_s[0] + a1 * (keep2 * got_s[1]))
-    decay = (keep1 * a1 + (1.0 - keep1)) * (keep2 * a2 + (1.0 - keep2))
-    for j, k in enumerate(SCAN_SHIFTS):
-        cur_s[j] = state
-        cur_a[j] = decay
-        slot = j + 2
-        for copy in send(slot, k, cur_s.at[j], cur_a.at[j]):
+    def arrived(slot, k):
+        keep = ((me - k + n) // n).astype(jnp.float32)
+        return keep * got_a[slot] + (1.0 - keep), keep * got_s[slot]
+
+    slot = 0
+    decay = state = None
+    for r, ks in enumerate(SCAN_ROUNDS):
+        first = slot
+        copies = []
+        for k in ks:
+            if r == 0:
+                copies += send(slot, k, s_ref, a_ref)
+            else:
+                copies += send(slot, k, cur_s.at[r - 1], cur_a.at[r - 1])
+            slot += 1
+        for copy in copies:
             copy.wait()
-        keep = keep_of(k)
-        state = cur_s[j] + cur_a[j] * (keep * got_s[slot])
-        decay = cur_a[j] * (keep * got_a[slot] + (1.0 - keep))
-    o_ref[...] = state
+        acc_a, acc_s = arrived(first + len(ks) - 1, ks[-1])
+        for j in range(len(ks) - 2, -1, -1):
+            part_a, part_s = arrived(first + j, ks[j])
+            acc_s = part_a * acc_s + part_s
+            acc_a = part_a * acc_a
+        if r > 0:
+            acc_s = cur_a[r - 1] * acc_s + cur_s[r - 1]
+            acc_a = cur_a[r - 1] * acc_a
+        if r + 1 < len(SCAN_ROUNDS):
+            cur_s[r] = acc_s
+            cur_a[r] = acc_a
+        else:
+            o_ref[...] = acc_s
 
 
 def carry_scan(local_state, carry_decay):
-    rounds = len(SCAN_SHIFTS)
-    slots = rounds + 2
+    rounds = len(SCAN_ROUNDS) - 1
+    slots = sum(len(ks) for ks in SCAN_ROUNDS)
     return pl.pallas_call(
         carry_scan_kernel,
         out_shape=jax.ShapeDtypeStruct(local_state.shape, local_state.dtype),

time: 122 us -> 132 us (1.082)
  Pallas kernels: 74.4 us -> 82.2 us
  waiting for transfers between devices: 0.41 us -> 1.82 us
    pallas_call x1, Pallas kernels: 46.8 us -> 56 us  [carry_scan(): pl.pallas_call(carry_scan_kernel, out_shape=jax.ShapeDtypeStruct(local_st...]
    all_gather x1, waiting for transfers between devices: 0.39 us -> 1.81 us  [attend_sparse(): kv_all = lax.all_gather(kv_local, 'ctx', axis=1, tiled=True)]
    pallas_call x1, Pallas kernels: 12.2 us -> 10.8 us  [tp_sum(): pl.pallas_call(tp_sum_kernel, out_shape=jax.ShapeDtypeStruct(shaped.shape...]
  transfers between devices with their start and end apart: 1 -> 1, of which waited for: 1 -> 1; matrix products, arithmetic and copies ran while one was open for 24% -> 22% of each run, Pallas kernels for 49% -> 52%
where the time goes in v8:
time: 132 us; the launch traced here: 129 us
  Pallas kernels  82.2 us (62%)
  between operations  14.3 us (11%)
  other arithmetic  12.1 us (9%)
  matrix products  9.91 us (8%)
  local copies, waits for them, and re-layouts  8.88 us (7%)
  waiting for transfers between devices  1.82 us (1%)
    pallas_call x1, Pallas kernels, carry_scan(): pl.pallas_call(carry_scan_kernel, out_shape=jax.ShapeDtypeStruct(local_st...  56 us
    pallas_call x1, Pallas kernels, attend_sparse(): pl.pallas_call(lambda *refs: sparse_attention_kernel(slots, blocks_here,...  15.5 us
    pallas_call x1, Pallas kernels, tp_sum(): pl.pallas_call(tp_sum_kernel, out_shape=jax.ShapeDtypeStruct(shaped.shape...  10.8 us
    dot_general x1, matrix products, mamba_mix(): jnp.einsum('hts,shp->thp', decay * inner[None], weighted, precision=careful)  6.72 us
  transfers between devices with their start and end apart: 1, of which 1 were waited for; matrix products, arithmetic and copies ran while one was open for 22% of the time, Pallas kernels for 52%

profile of v8, /device:TPU:1, one launch (start us, length us, event | category | flops | bytes accessed | tf_op | source)
XLA Modules:
  0.0 129.3 jit_solution(1914589215113844731)
XLA Ops:
  7.2 0.0 copy-start
  7.2 0.0 copy-start.5
  7.2 0.0 all-gather.2.cloned.1.call-start
  7.2 1.5 %pad_maximum_fusion = bf16[2,256,128]{2,1,0:T(8,128)(2,1)} fusion(bf16[1,256,128]{2,1,0:T(8,128)(2,1)} %bitcast.55, bf16[1,256,128]{2,1,0:T(8,128)(2,1)} %bitcast.56), kind=kLoop, calls=%fused_computation.31 | loop fusion | flops 65536 | bytes 262144 | tf_op jit(solution)/shard_map/stack | solution.py:310
  8.8 0.0 all-gather.2.cloned.1.call-update
  8.8 0.7 exponential_negate_fusion
  9.5 0.8 copy_bitcast_fusion.1
  10.3 0.6 reduce-window.6
  10.9 0.2 slice_reduce_fusion
  11.1 1.5 %copy.44 = f32[256,2048]{0,1:T(8,128)S(1)} copy(bf16[256,2048]{1,0:T(8,128)(2,1)} %param.20) | data formatting | bytes 3145728 | tf_op jit(solution)/shard_map/reshape | solution.py:259
  12.6 0.1 copy_bitcast_fusion
  12.7 0.2 slice_reduce_fusion.1
  12.9 0.1 broadcast_in_dim.97
  12.9 0.7 broadcast_in_dim_reshape.3.a_ref
  13.6 0.0 copy-done
  13.6 0.0 copy-done.5
  13.6 0.2 convolution_bitcast_fusion
  13.8 0.1 copy.47
  14.0 0.1 bitcast_exponential_fusion
  14.1 0.0 copy-done.4
  14.1 0.3 multiply_multiply_fusion
  14.4 0.0 copy-start.11
  14.4 1.3 %fusion.26.s_ref = f32[16,2048]{1,0:T(8,128)} fusion(bf16[256,16]{0,1:T(8,128)(2,1)S(1)} %copy-done.5, f32[2048,256]{1,0:T(8,128)S(1)} %bitcast.52), kind=kOutput, calls=%fused_computation.54 | convolution fusion | flops 50331648 | bytes 2236416 | tf_op jit(solution)/shard_map/sn,shp->nhp/dot_general | solution.py:275
  15.7 56.0 %shard_map.150 = f32[16,2048]{1,0:T(8,128)} custom-call(f32[16,2048]{1,0:T(8,128)} %fusion.26.s_ref, f32[1,2048]{1,0:T(1,128)} %broadcast_in_dim_reshape.3.a_ref), custom_call_target="tpu_custom_call" | custom-call | tf_op jit(solution)/shard_map/pallas_call | solution.py:180
  71.8 1.7 %fusion.27 = f32[2048,256]{1,0:T(8,128)S(1)} fusion(f32[16,2048]{1,0:T(8,128)} %shard_map.150, bf16[256,16]{0,1:T(8,128)(2,1)S(1)} %copy-done), kind=kOutput, calls=%fused_computation.55 | convolution fusion | flops 50331648 | bytes 2236416 | tf_op jit(solution)/shard_map/dot_general | solution.py:282
  73.4 0.0 copy-done.11
  73.4 6.7 %fusion.15 = f32[256,32,64]{0,2,1:T(8,128)} fusion(f32[256,32,64]{0,2,1:T(8,128)S(1)} %bitcast.51, f32[256,32,64]{0,2,1:T(8,128)S(1)} %bitcast.53, f32[256,256]{1,0:T(8,128)S(1)} %copy.47, f32[32,256]{1,0:T(8,128)S(1)} %get-tuple-element.14, pred[256,256]{1,0:T(8,128)(4,1)S(1)} %iota_compare_fusion.1, f32[32]{0:T(128)S(1)} %copy-done.11, ...), kind=kOutput, calls=%fused_computation.18 | convolution fusion | flops 816316416 | bytes 6717568 | tf_op jit(solution)/shard_map/hts,shp->thp/dot_general | solution.py:273
  80.2 2.2 %copy.48 = f32[256,2048]{1,0:T(8,128)S(1)} copy(f32[256,2048]{0,1:T(8,128)} %bitcast.54) | data formatting | bytes 4194304 | tf_op jit(solution)/shard_map/reshape | solution.py:286
  82.4 0.0 copy-done.1
  82.4 0.0 copy-start.10
  82.4 0.0 copy-start.6
  82.4 0.0 copy-start.7
  82.4 0.0 copy-start.8
  82.4 0.7 multiply_reduce_fusion
  83.1 0.6 pad.4.x_ref
  83.7 10.8 %shard_map.151 = f32[8,128]{1,0:T(8,128)} custom-call(f32[8,128]{1,0:T(8,128)} %pad.4.x_ref), custom_call_target="tpu_custom_call" | custom-call | tf_op jit(solution)/shard_map/pallas_call | solution.py:240
  94.5 0.1 pad.7.clone
  94.6 0.0 copy-done.10
  94.6 0.1 dynamic_slice.3
  94.7 0.0 copy-done.6
  94.7 0.0 copy-done.7
  94.7 0.1 broadcast_compare_fusion.1
  94.8 0.1 pad_add_fusion.1
  94.9 0.4 copy-done.9
  95.3 0.1 broadcast_subtract_fusion
  95.4 0.0 copy-start.2
  95.4 0.1 pad_add_fusion
  95.4 0.8 and_reduce_fusion
  96.2 0.1 not_and_fusion
  96.3 0.1 add_select_fusion
  96.4 0.2 broadcast_in_dim.93
  96.6 0.9 reshape_reshape.4.refs_3_
  97.4 0.1 pad.15.clone
  97.5 0.7 broadcast_in_dim.48
  98.2 0.8 add_add_fusion
  99.1 0.1 copy.41
  99.2 2.0 %select_reduce_fusion = s32[8,4,18]{0,2,1:T(8,128)S(1)} fusion(s32[8,4,18]{0,2,1:T(8,128)S(1)} %copy.41, s32[128]{0:T(128)} %param.19), kind=kLoop, calls=%fused_computation.26 | loop fusion | flops 220608 | bytes 5120 | tf_op jit(solution)/shard_map/reduce_sum | solution.py:44
  101.2 0.1 copy.42
  101.3 0.7 reshape.112.refs_2_
  102.0 0.7 rsqrt_bitcast_fusion
  102.7 0.7 fusion.23.refs_4_
  103.4 1.7 %multiply_convert_fusion = bf16[256,2048]{1,0:T(8,128)(2,1)} fusion(f32[2048]{0:T(1024)S(1)} %copy-done.8, f32[256]{0:T(256)S(1)} %rsqrt_bitcast_fusion, f32[256,2048]{1,0:T(8,128)S(1)} %copy.48, bf16[256,2048]{1,0:T(8,128)(2,1)S(1)} %copy-done.1), kind=kLoop, calls=%fused_computation.19 | loop fusion | flops 4718592 | bytes 4203520 | tf_op jit(solution)/shard_map/convert_element_type | solution.py:291
  105.2 1.8 %all-gather.2.cloned.1.call-done.refs_1_ = bf16[2,8192,128]{2,1,0:T(8,128)(2,1)} async-done(((bf16[2,256,128]{2,1,0:T(8,128)(2,1)}), bf16[2,8192,128]{2,1,0:T(8,128)(2,1)}) %all-gather.2.cloned.1.call-update) | async-done | bytes 4194320 | tf_op jit(solution)/shard_map/all_gather | solution.py:82
  107.0 15.5 %shard_map.149 = bf16[256,1024]{1,0:T(8,128)(2,1)} custom-call(bf16[256,1024]{1,0:T(8,128)(2,1)} %refs_0_.1, bf16[2,8192,128]{2,1,0:T(8,128)(2,1)} %all-gather.2.cloned.1.call-done.refs_1_, s32[576]{0:T(1024)} %reshape.112.refs_2_, f32[32,1,1152]{2,1,0:T(1,128)} %reshape_reshape.4.refs_3_, f32[64,1152]{1,0:T(8,128)} %fusion.23.refs_4_), custom_call_target="tpu_custom_call" | custom-call | flops 1207959552 | bytes 5242880 | tf_op jit(solution)/shard_map/pallas_call | solution.py:89
  (15 shorter events, 0.1 us)
Async XLA Ops:
  7.2 6.4 %copy-start = (bf16[256,16]{0,1:T(8,128)(2,1)S(1)}, bf16[256,16]{0,1:T(8,128)(2,1)}, u32[]{:S(2)}) copy-start(bf16[256,16]{0,1:T(8,128)(2,1)} %param.23) | copy-start | bytes 24580
  7.2 6.4 %copy-start.5 = (bf16[256,16]{0,1:T(8,128)(2,1)S(1)}, bf16[256,16]{0,1:T(8,128)(2,1)}, u32[]{:S(2)}) copy-start(bf16[256,16]{0,1:T(8,128)(2,1)} %param.22) | copy-start | bytes 24580
  7.2 99.8 %all-gather.2.cloned.1.call-start = ((), (), s32[]{:S(2)}) async-start(), calls=%async_computation | async-start | bytes 4325376 | tf_op jit(solution)/shard_map/all_gather | solution.py:82
  11.1 3.0 %copy-start.4 = (f32[256,32]{0,1:T(8,128)S(1)}, f32[256,32]{0,1:T(8,128)}, u32[]{:S(2)}) copy-start(f32[256,32]{0,1:T(8,128)} %param.24) | copy-start | bytes 98308
  14.4 59.0 %copy-start.11 = (f32[32]{0:T(128)S(1)}, f32[32]{0:T(128)}, u32[]{:S(2)}) copy-start(f32[32]{0:T(128)} %param.26) | copy-start | bytes 388
  80.2 2.2 %copy-start.1 = (bf16[256,2048]{1,0:T(8,128)(2,1)S(1)}, bf16[256,2048]{1,0:T(8,128)(2,1)}, u32[]{:S(2)}) copy-start(bf16[256,2048]{1,0:T(8,128)(2,1)} %param.21) | copy-start | bytes 3145732
  82.4 12.2 %copy-start.10 = (s32[128]{0:T(128)S(1)}, s32[128]{0:T(128)}, u32[]{:S(2)}) copy-start(s32[128]{0:T(128)} %param.19) | copy-start | bytes 1540
  82.4 12.3 %copy-start.6 = (s32[8,8]{1,0:T(8,128)S(1)}, s32[8,8]{1,0:T(8,128)}, u32[]{:S(2)}) copy-start(s32[8,8]{1,0:T(8,128)} %param.17) | copy-start | bytes 772
  82.4 12.3 %copy-start.7 = (s32[8,8]{1,0:T(8,128)S(1)}, s32[8,8]{1,0:T(8,128)}, u32[]{:S(2)}) copy-start(s32[8,8]{1,0:T(8,128)} %param.18) | copy-start | bytes 772
  82.4 21.0 %copy-start.8 = (f32[2048]{0:T(1024)S(1)}, f32[2048]{0:T(1024)}, u32[]{:S(2)}) copy-start(f32[2048]{0:T(1024)} %param.27) | copy-start | bytes 24580
  94.7 0.6 copy-start.9
  95.3 1.0 copy-start.3
  95.4 0.9 copy-start.2
Sparse Core Ops, SparseCore 0:
  11.2 95.7 all-gather.1

commit v9 on v7

--- a/solution.py
+++ b/solution.py
@@ -43,9 +43,10 @@
     match = block_position[None, None, None, :] == cand[..., None]
     index = jnp.sum(jnp.where(match, jnp.arange(total_blocks, dtype=jnp.int32), 0), axis=-1)
     slots = cand.shape[-1]
-    col_bias = jnp.where(ok, 0.0, NEG_FILL).astype(jnp.float32)
-    col_bias = jnp.repeat(col_bias, BLOCK, axis=-1).reshape(heads * blocks_here, 1, slots * BLOCK)
-    return index.reshape(-1).astype(jnp.int32), col_bias, slots
+    units = heads * blocks_here
+    col_bias = jnp.where(ok.reshape(units, slots), 0.0, NEG_FILL).astype(jnp.float32)
+    col_bias = jnp.repeat(col_bias, BLOCK, axis=-1)
+    return index.reshape(units, slots).astype(jnp.int32), col_bias, slots
 
 
 def sparse_attention_kernel(slots, blocks_here, q_ref, kv_ref, idx_ref, bias_ref, causal_ref, o_ref, kbuf, vbuf):
@@ -56,7 +57,7 @@
         head = i // blocks_here
         qblock = i % blocks_here
         for j in range(slots):
-            src = pl.multiple_of(idx_ref[i * slots + j] * BLOCK, BLOCK)
+            src = pl.multiple_of(idx_ref[i, j] * BLOCK, BLOCK)
             kbuf[pl.ds(j * BLOCK, BLOCK), :] = kv_ref[0, pl.ds(src, BLOCK), :]
             vbuf[pl.ds(j * BLOCK, BLOCK), :] = kv_ref[1, pl.ds(src, BLOCK), :]
         rows = pl.ds(pl.multiple_of(qblock * BLOCK, BLOCK), BLOCK)
@@ -65,7 +66,7 @@
         scores = lax.dot_general(
             q, kbuf[...], (((1,), (1,)), ((), ())), preferred_element_type=jnp.float32
         ) * score_scale
-        masked = scores + causal_ref[...] + bias_ref[i]
+        masked = scores + causal_ref[...] + bias_ref[pl.ds(i, 1), :]
         top = jnp.max(masked, axis=1, keepdims=True)
         expo = jnp.exp(masked - top)
         denom = jnp.sum(expo, axis=1, keepdims=True)

time: 122 us -> 122 us (level)
  no operation moved by 1% of the time
where the time goes in v9:
time: 122 us; the launch traced here: 120 us
  Pallas kernels  74.4 us (61%)
  between operations  14.3 us (12%)
  other arithmetic  12.2 us (10%)
  matrix products  9.91 us (8%)
  local copies, waits for them, and re-layouts  8.4 us (7%)
    pallas_call x1, Pallas kernels, carry_scan(): pl.pallas_call(carry_scan_kernel, out_shape=jax.ShapeDtypeStruct(local_st...  46.8 us
    pallas_call x1, Pallas kernels, attend_sparse(): pl.pallas_call(lambda *refs: sparse_attention_kernel(slots, blocks_here,...  15.5 us
    pallas_call x1, Pallas kernels, tp_sum(): pl.pallas_call(tp_sum_kernel, out_shape=jax.ShapeDtypeStruct(shaped.shape...  12.2 us
    dot_general x1, matrix products, mamba_mix(): jnp.einsum('hts,shp->thp', decay * inner[None], weighted, precision=careful)  6.72 us
  transfers between devices with their start and end apart: 1, of which 1 were waited for; matrix products, arithmetic and copies ran while one was open for 24% of the time, Pallas kernels for 49%

profile of v9, /device:TPU:1, one launch (start us, length us, event | category | flops | bytes accessed | tf_op | source)
XLA Modules:
  0.0 120.1 jit_solution(5623804505337661868)
XLA Ops:
  7.2 0.0 copy-start
  7.2 0.0 copy-start.6
  7.2 0.0 all-gather.2.cloned.1.call-start
  7.2 1.5 %pad_maximum_fusion = bf16[2,256,128]{2,1,0:T(8,128)(2,1)} fusion(bf16[1,256,128]{2,1,0:T(8,128)(2,1)} %bitcast.62, bf16[1,256,128]{2,1,0:T(8,128)(2,1)} %bitcast.63), kind=kLoop, calls=%fused_computation.31 | loop fusion | flops 65536 | bytes 262144 | tf_op jit(solution)/shard_map/stack | solution.py:301
  8.8 0.0 all-gather.2.cloned.1.call-update
  8.8 0.7 exponential_negate_fusion
  9.5 0.8 copy_bitcast_fusion.1
  10.3 0.6 reduce-window.6
  10.9 0.2 slice_reduce_fusion
  11.1 1.5 %copy.34 = f32[256,2048]{0,1:T(8,128)S(1)} copy(bf16[256,2048]{1,0:T(8,128)(2,1)} %param.20) | data formatting | bytes 3145728 | tf_op jit(solution)/shard_map/reshape | solution.py:250
  12.6 0.1 copy_bitcast_fusion
  12.7 0.2 slice_reduce_fusion.1
  12.9 0.1 broadcast_in_dim.100
  12.9 0.7 broadcast_in_dim_reshape.3.a_ref
  13.6 0.0 copy-done
  13.6 0.0 copy-done.6
  13.6 0.2 convolution_bitcast_fusion
  13.8 0.1 copy.37
  14.0 0.1 bitcast_exponential_fusion
  14.1 0.0 copy-done.4
  14.1 0.3 multiply_multiply_fusion
  14.4 0.0 copy-start.11
  14.4 1.3 %fusion.26.s_ref = f32[16,2048]{1,0:T(8,128)} fusion(bf16[256,16]{0,1:T(8,128)(2,1)S(1)} %copy-done.6, f32[2048,256]{1,0:T(8,128)S(1)} %bitcast.56), kind=kOutput, calls=%fused_computation.56 | convolution fusion | flops 50331648 | bytes 2236416 | tf_op jit(solution)/shard_map/sn,shp->nhp/dot_general | solution.py:266
  15.7 46.8 %shard_map.150 = f32[16,2048]{1,0:T(8,128)} custom-call(f32[16,2048]{1,0:T(8,128)} %fusion.26.s_ref, f32[1,2048]{1,0:T(1,128)} %broadcast_in_dim_reshape.3.a_ref), custom_call_target="tpu_custom_call" | custom-call | tf_op jit(solution)/shard_map/pallas_call | solution.py:171
  62.6 1.7 %fusion.27 = f32[2048,256]{1,0:T(8,128)S(1)} fusion(f32[16,2048]{1,0:T(8,128)} %shard_map.150, bf16[256,16]{0,1:T(8,128)(2,1)S(1)} %copy-done), kind=kOutput, calls=%fused_computation.57 | convolution fusion | flops 50331648 | bytes 2236416 | tf_op jit(solution)/shard_map/dot_general | solution.py:273
  64.2 0.0 copy-done.11
  64.2 6.7 %fusion.15 = f32[256,32,64]{0,2,1:T(8,128)} fusion(f32[256,32,64]{0,2,1:T(8,128)S(1)} %bitcast.55, f32[256,32,64]{0,2,1:T(8,128)S(1)} %bitcast.57, f32[256,256]{1,0:T(8,128)S(1)} %copy.37, f32[32,256]{1,0:T(8,128)S(1)} %get-tuple-element.14, pred[256,256]{1,0:T(8,128)(4,1)S(1)} %iota_compare_fusion.1, f32[32]{0:T(128)S(1)} %copy-done.11, ...), kind=kOutput, calls=%fused_computation.18 | convolution fusion | flops 816316416 | bytes 6717568 | tf_op jit(solution)/shard_map/hts,shp->thp/dot_general | solution.py:264
  71.0 2.2 %copy.38 = f32[256,2048]{1,0:T(8,128)S(1)} copy(f32[256,2048]{0,1:T(8,128)} %bitcast.58) | data formatting | bytes 4194304 | tf_op jit(solution)/shard_map/reshape | solution.py:277
  73.2 0.0 copy-start.10
  73.2 0.0 copy-start.5
  73.2 0.0 copy-start.7
  73.2 0.0 copy-start.8
  73.2 0.7 multiply_reduce_fusion
  73.9 0.6 pad.4.x_ref
  74.5 12.2 %shard_map.151 = f32[8,128]{1,0:T(8,128)} custom-call(f32[8,128]{1,0:T(8,128)} %pad.4.x_ref), custom_call_target="tpu_custom_call" | custom-call | tf_op jit(solution)/shard_map/pallas_call | solution.py:231
  86.7 0.0 copy-done.10
  86.7 0.1 dynamic_slice.3
  86.8 0.1 broadcast_compare_fusion.2
  86.9 0.1 pad_add_fusion.1
  87.0 0.1 broadcast_subtract_fusion
  87.1 0.0 copy-start.2
  87.1 0.1 pad_add_fusion
  87.2 0.8 and_reduce_fusion
  87.9 0.0 copy-done.9
  88.0 0.1 sub.51
  88.0 0.1 pad.7.clone
  88.1 0.1 broadcast_compare_fusion.1
  88.2 0.1 add_and_fusion
  88.3 0.0 copy-done.2
  88.3 0.1 add_select_fusion
  88.4 0.2 broadcast_in_dim.96
  88.5 0.8 reshape.128.refs_3_
  89.3 0.1 pad.17.clone
  89.4 0.7 broadcast_in_dim.50
  90.1 0.8 add_add_fusion
  91.0 0.1 copy.32
  91.1 2.0 %select_reduce_fusion = s32[8,4,18]{0,2,1:T(8,128)S(1)} fusion(s32[8,4,18]{0,2,1:T(8,128)S(1)} %copy.32, s32[128]{0:T(128)} %param.19), kind=kLoop, calls=%fused_computation.26 | loop fusion | flops 220608 | bytes 5120 | tf_op jit(solution)/shard_map/reduce_sum | solution.py:44
  93.1 0.7 copy.33
  93.8 0.7 rsqrt_bitcast_fusion
  94.5 0.7 fusion.23.refs_4_
  95.2 0.0 copy-done.8
  95.2 1.7 %multiply_convert_fusion = bf16[256,2048]{1,0:T(8,128)(2,1)} fusion(f32[2048]{0:T(1024)S(1)} %copy-done.8, f32[256]{0:T(256)S(1)} %rsqrt_bitcast_fusion, f32[256,2048]{1,0:T(8,128)S(1)} %copy.38, bf16[256,2048]{1,0:T(8,128)(2,1)S(1)} %copy-done.1), kind=kLoop, calls=%fused_computation.19 | loop fusion | flops 4718592 | bytes 4203520 | tf_op jit(solution)/shard_map/convert_element_type | solution.py:282
  97.0 0.8 all-gather.2.cloned.1.call-done.refs_1_
  97.8 15.5 %shard_map.149 = bf16[256,1024]{1,0:T(8,128)(2,1)} custom-call(bf16[256,1024]{1,0:T(8,128)(2,1)} %refs_0_.1, bf16[2,8192,128]{2,1,0:T(8,128)(2,1)} %all-gather.2.cloned.1.call-done.refs_1_, s32[32,18]{1,0:T(8,128)} %bitcast.60, f32[32,1152]{1,0:T(8,128)} %reshape.128.refs_3_, f32[64,1152]{1,0:T(8,128)} %fusion.23.refs_4_), custom_call_target="tpu_custom_call" | custom-call | flops 1207959552 | bytes 5242880 | tf_op jit(solution)/shard_map/pallas_call | solution.py:90
  (19 shorter events, 0.1 us)
Async XLA Ops:
  7.2 6.4 %copy-start = (bf16[256,16]{0,1:T(8,128)(2,1)S(1)}, bf16[256,16]{0,1:T(8,128)(2,1)}, u32[]{:S(2)}) copy-start(bf16[256,16]{0,1:T(8,128)(2,1)} %param.23) | copy-start | bytes 24580
  7.2 6.4 %copy-start.6 = (bf16[256,16]{0,1:T(8,128)(2,1)S(1)}, bf16[256,16]{0,1:T(8,128)(2,1)}, u32[]{:S(2)}) copy-start(bf16[256,16]{0,1:T(8,128)(2,1)} %param.22) | copy-start | bytes 24580
  7.2 90.6 %all-gather.2.cloned.1.call-start = ((), (), s32[]{:S(2)}) async-start(), calls=%async_computation | async-start | bytes 4325376 | tf_op jit(solution)/shard_map/all_gather | solution.py:83
  11.1 3.0 %copy-start.4 = (f32[256,32]{0,1:T(8,128)S(1)}, f32[256,32]{0,1:T(8,128)}, u32[]{:S(2)}) copy-start(f32[256,32]{0,1:T(8,128)} %param.24) | copy-start | bytes 98308
  14.4 49.8 %copy-start.11 = (f32[32]{0:T(128)S(1)}, f32[32]{0:T(128)}, u32[]{:S(2)}) copy-start(f32[32]{0:T(128)} %param.26) | copy-start | bytes 388
  71.0 2.2 %copy-start.1 = (bf16[256,2048]{1,0:T(8,128)(2,1)S(1)}, bf16[256,2048]{1,0:T(8,128)(2,1)}, u32[]{:S(2)}) copy-start(bf16[256,2048]{1,0:T(8,128)(2,1)} %param.21) | copy-start | bytes 3145732
  73.2 13.5 %copy-start.10 = (s32[128]{0:T(128)S(1)}, s32[128]{0:T(128)}, u32[]{:S(2)}) copy-start(s32[128]{0:T(128)} %param.19) | copy-start | bytes 1540
  73.2 13.6 %copy-start.5 = (s32[8,8]{1,0:T(8,128)S(1)}, s32[8,8]{1,0:T(8,128)}, u32[]{:S(2)}) copy-start(s32[8,8]{1,0:T(8,128)} %param.18) | copy-start | bytes 772
  73.2 13.6 %copy-start.7 = (s32[8,8]{1,0:T(8,128)S(1)}, s32[8,8]{1,0:T(8,128)}, u32[]{:S(2)}) copy-start(s32[8,8]{1,0:T(8,128)} %param.17) | copy-start | bytes 772
  73.2 22.0 %copy-start.8 = (f32[2048]{0:T(1024)S(1)}, f32[2048]{0:T(1024)}, u32[]{:S(2)}) copy-start(f32[2048]{0:T(1024)} %param.27) | copy-start | bytes 24580
  86.8 1.1 copy-start.9
  87.1 0.9 copy-start.3
  87.1 1.2 %copy-start.2 = (s32[8,4,8]{2,1,0:T(4,128)}, s32[8,4,8]{2,1,0:T(4,128)S(1)}, u32[]{:S(2)}) copy-start(s32[8,4,8]{2,1,0:T(4,128)S(1)} %broadcast_in_dim.51) | copy-start | bytes 3076
Sparse Core Ops, SparseCore 0:
  11.2 86.5 all-gather.1

commit v10 on v9

--- a/solution.py
+++ b/solution.py
@@ -113,10 +113,11 @@
 SCAN_SHIFTS = (2, 4, 8, 16)
 
 
-def carry_scan_kernel(s_ref, a_ref, o_ref, cur_s, cur_a, got_s, got_a, sems):
+def carry_scan_kernel(x_ref, o_ref, cur, got, sems):
     n = lax.axis_size("ctx")
     me = lax.axis_index("ctx")
     tp = lax.axis_index("tp")
+    rows = D_STATE
     shifts = (1,) + SCAN_SHIFTS
     barrier = pltpu.get_barrier_semaphore()
     partners = sorted({k % n for k in shifts} | {(-k) % n for k in shifts})
@@ -126,62 +127,56 @@
         )
     pl.semaphore_wait(barrier, len(partners))
 
-    def send(slot, k, src_s, src_a):
-        target = (lax.rem(me + k, n), tp)
-        copies = [
-            pltpu.make_async_remote_copy(
-                src_ref=src,
-                dst_ref=dst.at[slot],
-                send_sem=sems.at[part, 0, slot],
-                recv_sem=sems.at[part, 1, slot],
-                device_id=target,
-                device_id_type=pl.DeviceIdType.MESH,
-            )
-            for part, (src, dst) in enumerate(((src_s, got_s), (src_a, got_a)))
-        ]
-        for copy in copies:
-            copy.start()
-        return copies
+    def send(slot, k, src):
+        copy = pltpu.make_async_remote_copy(
+            src_ref=src,
+            dst_ref=got.at[slot],
+            send_sem=sems.at[0, slot],
+            recv_sem=sems.at[1, slot],
+            device_id=(lax.rem(me + k, n), tp),
+            device_id_type=pl.DeviceIdType.MESH,
+        )
+        copy.start()
+        return copy
 
     def keep_of(k):
         return ((me - k + n) // n).astype(jnp.float32)
 
-    first = send(0, 1, s_ref, a_ref) + send(1, 2, s_ref, a_ref)
+    first = [send(0, 1, x_ref), send(1, 2, x_ref)]
     for copy in first:
         copy.wait()
     keep1, keep2 = keep_of(1), keep_of(2)
-    a1, a2 = got_a[0], got_a[1]
-    state = keep1 * (got_s[0] + a1 * (keep2 * got_s[1]))
+    g0, g1 = got[0], got[1]
+    a1, a2 = g0[rows:], g1[rows:]
+    state = keep1 * (g0[:rows] + a1 * (keep2 * g1[:rows]))
     decay = (keep1 * a1 + (1.0 - keep1)) * (keep2 * a2 + (1.0 - keep2))
     for j, k in enumerate(SCAN_SHIFTS):
-        cur_s[j] = state
-        cur_a[j] = decay
+        cur[j] = jnp.concatenate([state, decay], axis=0)
         slot = j + 2
-        for copy in send(slot, k, cur_s.at[j], cur_a.at[j]):
-            copy.wait()
+        send(slot, k, cur.at[j]).wait()
         keep = keep_of(k)
-        state = cur_s[j] + cur_a[j] * (keep * got_s[slot])
-        decay = cur_a[j] * (keep * got_a[slot] + (1.0 - keep))
+        mine, arrived = cur[j], got[slot]
+        state = mine[:rows] + mine[rows:] * (keep * arrived[:rows])
+        decay = mine[rows:] * (keep * arrived[rows:] + (1.0 - keep))
     o_ref[...] = state
 
 
 def carry_scan(local_state, carry_decay):
     rounds = len(SCAN_SHIFTS)
     slots = rounds + 2
+    packed = jnp.concatenate([local_state, carry_decay], axis=0)
     return pl.pallas_call(
         carry_scan_kernel,
         out_shape=jax.ShapeDtypeStruct(local_state.shape, local_state.dtype),
-        in_specs=[pl.BlockSpec(memory_space=pltpu.VMEM)] * 2,
+        in_specs=[pl.BlockSpec(memory_space=pltpu.VMEM)],
         out_specs=pl.BlockSpec(memory_space=pltpu.VMEM),
         scratch_shapes=[
-            pltpu.VMEM((rounds,) + local_state.shape, jnp.float32),
-            pltpu.VMEM((rounds,) + carry_decay.shape, jnp.float32),
-            pltpu.VMEM((slots,) + local_state.shape, jnp.float32),
-            pltpu.VMEM((slots,) + carry_decay.shape, jnp.float32),
-            pltpu.SemaphoreType.DMA((2, 2, slots)),
+            pltpu.VMEM((rounds,) + packed.shape, jnp.float32),
+            pltpu.VMEM((slots,) + packed.shape, jnp.float32),
+            pltpu.SemaphoreType.DMA((2, slots)),
         ],
         compiler_params=pltpu.CompilerParams(collective_id=0, has_side_effects=True),
-    )(local_state, carry_decay)
+    )(packed)
 
 
 def tp_sum_kernel(x_ref, o_ref, got, sems):

time: 122 us -> 138 us (1.13); the launches traced: 120 us -> 138 us
  Pallas kernels: 74.4 us -> 93.3 us
    pallas_call x1, Pallas kernels: 46.8 us -> 66.2 us  [carry_scan(): pl.pallas_call(carry_scan_kernel, out_shape=jax.ShapeDtypeStruct(local_st...]
  transfers between devices with their start and end apart: 1 -> 1, of which waited for: 1 -> 0; matrix products, arithmetic and copies ran while one was open for 24% -> 21% of each run, Pallas kernels for 49% -> 56%
where the time goes in v10:
time: 138 us
  Pallas kernels  93.3 us (68%)
  between operations  14.3 us (10%)
  other arithmetic  12.9 us (9%)
  matrix products  9.32 us (7%)
  local copies, waits for them, and re-layouts  8.13 us (6%)
    pallas_call x1, Pallas kernels, carry_scan(): pl.pallas_call(carry_scan_kernel, out_shape=jax.ShapeDtypeStruct(local_st...  66.2 us
    pallas_call x1, Pallas kernels, attend_sparse(): pl.pallas_call(lambda *refs: sparse_attention_kernel(slots, blocks_here,...  15.5 us
    pallas_call x1, Pallas kernels, tp_sum(): pl.pallas_call(tp_sum_kernel, out_shape=jax.ShapeDtypeStruct(shaped.shape...  11.6 us
    dot_general x1, matrix products, mamba_mix(): jnp.einsum('hts,shp->thp', decay * inner[None], weighted, precision=careful)  6.79 us
  transfers between devices with their start and end apart: 1, of which 0 were waited for; matrix products, arithmetic and copies ran while one was open for 21% of the time, Pallas kernels for 56%

profile of v10, /device:TPU:1, one launch (start us, length us, event | category | flops | bytes accessed | tf_op | source)
XLA Modules:
  0.0 138.0 jit_solution(9450426517820268817)
XLA Ops:
  7.2 0.0 copy-start
  7.2 0.0 copy-start.4
  7.2 0.0 all-gather.2.cloned.1.call-start
  7.2 1.5 %pad_maximum_fusion.1 = bf16[2,256,128]{2,1,0:T(8,128)(2,1)} fusion(bf16[1,256,128]{2,1,0:T(8,128)(2,1)} %bitcast.62, bf16[1,256,128]{2,1,0:T(8,128)(2,1)} %bitcast.63), kind=kLoop, calls=%fused_computation.32 | loop fusion | flops 65536 | bytes 262144 | tf_op jit(solution)/shard_map/stack | solution.py:296
  8.8 0.0 all-gather.2.cloned.1.call-update
  8.8 0.7 exponential_negate_fusion
  9.5 0.8 copy_bitcast_fusion.1
  10.3 0.6 reduce-window.6
  10.9 0.2 slice_reduce_fusion
  11.1 1.5 %copy.34 = f32[256,2048]{0,1:T(8,128)S(1)} copy(bf16[256,2048]{1,0:T(8,128)(2,1)} %param.20) | data formatting | bytes 3145728 | tf_op jit(solution)/shard_map/reshape | solution.py:245
  12.6 0.1 copy_bitcast_fusion
  12.6 0.2 slice_reduce_fusion.1
  12.8 0.1 broadcast_in_dim.100
  12.9 0.1 broadcast_in_dim_reshape.3
  13.0 0.1 bitcast_exponential_fusion
  13.1 0.0 copy-done.4
  13.1 0.0 copy-start.6
  13.1 0.3 multiply_multiply_fusion
  13.4 0.4 copy-done.6
  13.8 0.6 fusion.26
  14.5 0.7 pad_maximum_fusion.x_ref
  15.2 66.2 %shard_map.150 = f32[16,2048]{1,0:T(8,128)} custom-call(f32[17,2048]{1,0:T(8,128)} %pad_maximum_fusion.x_ref), custom_call_target="tpu_custom_call" | custom-call | tf_op jit(solution)/shard_map/pallas_call | solution.py:168
  81.4 0.0 copy-done
  81.4 0.2 convolution_bitcast_fusion
  81.6 0.1 copy.37
  81.8 1.7 %fusion.27 = f32[2048,256]{1,0:T(8,128)S(1)} fusion(f32[16,2048]{1,0:T(8,128)} %shard_map.150, bf16[256,16]{0,1:T(8,128)(2,1)S(1)} %copy-done), kind=kOutput, calls=%fused_computation.58 | convolution fusion | flops 50331648 | bytes 2236416 | tf_op jit(solution)/shard_map/dot_general | solution.py:268
  83.5 0.0 copy-done.11
  83.5 6.8 %fusion.15 = f32[256,32,64]{0,2,1:T(8,128)} fusion(f32[256,32,64]{0,2,1:T(8,128)S(1)} %bitcast.55, f32[256,32,64]{0,2,1:T(8,128)S(1)} %bitcast.57, f32[256,256]{1,0:T(8,128)S(1)} %copy.37, f32[32,256]{1,0:T(8,128)S(1)} %get-tuple-element.14, pred[256,256]{1,0:T(8,128)(4,1)S(1)} %iota_compare_fusion.1, f32[32]{0:T(128)S(1)} %copy-done.11, ...), kind=kOutput, calls=%fused_computation.18 | convolution fusion | flops 816316416 | bytes 6717568 | tf_op jit(solution)/shard_map/hts,shp->thp/dot_general | solution.py:259
  90.3 2.2 %copy.38 = f32[256,2048]{1,0:T(8,128)S(1)} copy(f32[256,2048]{0,1:T(8,128)} %bitcast.58) | data formatting | bytes 4194304 | tf_op jit(solution)/shard_map/reshape | solution.py:272
  92.5 0.0 copy-done.1
  92.5 0.0 copy-start.10
  92.5 0.0 copy-start.5
  92.5 0.0 copy-start.7
  92.5 0.0 copy-start.8
  92.5 0.7 multiply_reduce_fusion
  93.2 0.6 pad.4.x_ref
  93.8 11.6 %shard_map.151 = f32[8,128]{1,0:T(8,128)} custom-call(f32[8,128]{1,0:T(8,128)} %pad.4.x_ref), custom_call_target="tpu_custom_call" | custom-call | tf_op jit(solution)/shard_map/pallas_call | solution.py:226
  105.5 0.0 copy-done.10
  105.5 0.1 dynamic_slice.3
  105.6 0.0 copy-done.5
  105.6 0.0 copy-done.7
  105.6 0.1 broadcast_compare_fusion.2
  105.7 0.1 pad_add_fusion.1
  105.7 0.1 broadcast_subtract_fusion
  105.8 0.0 copy-start.2
  105.8 0.1 pad_add_fusion
  105.9 0.8 and_reduce_fusion
  106.7 0.1 sub.51
  106.8 0.1 pad.9.clone
  106.9 0.1 broadcast_compare_fusion.1
  107.0 0.1 add_and_fusion
  107.0 0.1 add_select_fusion
  107.1 0.2 broadcast_in_dim.96
  107.3 0.8 reshape.128.refs_3_
  108.1 0.1 pad.19.clone
  108.2 0.7 broadcast_in_dim.50
  108.9 0.8 add_add_fusion
  109.7 0.1 copy.32
  109.8 2.0 %select_reduce_fusion = s32[8,4,18]{0,2,1:T(8,128)S(1)} fusion(s32[8,4,18]{0,2,1:T(8,128)S(1)} %copy.32, s32[128]{0:T(128)} %param.19), kind=kLoop, calls=%fused_computation.26 | loop fusion | flops 220608 | bytes 5120 | tf_op jit(solution)/shard_map/reduce_sum | solution.py:44
  111.8 0.7 copy.33
  112.5 0.7 rsqrt_bitcast_fusion
  113.2 0.7 fusion.23.refs_4_
  114.0 1.7 %multiply_convert_fusion = bf16[256,2048]{1,0:T(8,128)(2,1)} fusion(f32[2048]{0:T(1024)S(1)} %copy-done.8, f32[256]{0:T(256)S(1)} %rsqrt_bitcast_fusion, f32[256,2048]{1,0:T(8,128)S(1)} %copy.38, bf16[256,2048]{1,0:T(8,128)(2,1)S(1)} %copy-done.1), kind=kLoop, calls=%fused_computation.19 | loop fusion | flops 4718592 | bytes 4203520 | tf_op jit(solution)/shard_map/convert_element_type | solution.py:277
  115.7 15.5 %shard_map.149 = bf16[256,1024]{1,0:T(8,128)(2,1)} custom-call(bf16[256,1024]{1,0:T(8,128)(2,1)} %refs_0_.1, bf16[2,8192,128]{2,1,0:T(8,128)(2,1)} %all-gather.2.cloned.1.call-done.refs_1_, s32[32,18]{1,0:T(8,128)} %bitcast.60, f32[32,1152]{1,0:T(8,128)} %reshape.128.refs_3_, f32[64,1152]{1,0:T(8,128)} %fusion.23.refs_4_), custom_call_target="tpu_custom_call" | custom-call | flops 1207959552 | bytes 5242880 | tf_op jit(solution)/shard_map/pallas_call | solution.py:90
  (20 shorter events, 0.1 us)
Async XLA Ops:
  7.2 74.2 %copy-start = (bf16[256,16]{0,1:T(8,128)(2,1)S(1)}, bf16[256,16]{0,1:T(8,128)(2,1)}, u32[]{:S(2)}) copy-start(bf16[256,16]{0,1:T(8,128)(2,1)} %param.23) | copy-start | bytes 24580
  7.2 5.9 %copy-start.4 = (f32[256,32]{0,1:T(8,128)S(1)}, f32[256,32]{0,1:T(8,128)}, u32[]{:S(2)}) copy-start(f32[256,32]{0,1:T(8,128)} %param.24) | copy-start | bytes 98308
  7.2 108.5 %all-gather.2.cloned.1.call-start = ((), (), s32[]{:S(2)}) async-start(), calls=%async_computation | async-start | bytes 4325376 | tf_op jit(solution)/shard_map/all_gather | solution.py:83
  13.1 0.7 copy-start.6
  14.5 69.0 %copy-start.11 = (f32[32]{0:T(128)S(1)}, f32[32]{0:T(128)}, u32[]{:S(2)}) copy-start(f32[32]{0:T(128)} %param.26) | copy-start | bytes 388
  90.3 2.2 %copy-start.1 = (bf16[256,2048]{1,0:T(8,128)(2,1)S(1)}, bf16[256,2048]{1,0:T(8,128)(2,1)}, u32[]{:S(2)}) copy-start(bf16[256,2048]{1,0:T(8,128)(2,1)} %param.21) | copy-start | bytes 3145732
  92.5 13.0 %copy-start.10 = (s32[128]{0:T(128)S(1)}, s32[128]{0:T(128)}, u32[]{:S(2)}) copy-start(s32[128]{0:T(128)} %param.19) | copy-start | bytes 1540
  92.5 13.1 %copy-start.5 = (s32[8,8]{1,0:T(8,128)S(1)}, s32[8,8]{1,0:T(8,128)}, u32[]{:S(2)}) copy-start(s32[8,8]{1,0:T(8,128)} %param.18) | copy-start | bytes 772
  92.5 13.1 %copy-start.7 = (s32[8,8]{1,0:T(8,128)S(1)}, s32[8,8]{1,0:T(8,128)}, u32[]{:S(2)}) copy-start(s32[8,8]{1,0:T(8,128)} %param.17) | copy-start | bytes 772
  92.5 21.5 %copy-start.8 = (f32[2048]{0:T(1024)S(1)}, f32[2048]{0:T(1024)}, u32[]{:S(2)}) copy-start(f32[2048]{0:T(1024)} %param.27) | copy-start | bytes 24580
  105.5 1.1 copy-start.9
  105.8 0.9 copy-start.3
  105.8 1.2 copy-start.2
Sparse Core Ops, SparseCore 0:
  10.6 92.3 all-gather.1

commit v11 on v9

--- a/solution.py
+++ b/solution.py
@@ -128,16 +128,22 @@
 
     def send(slot, k, src_s, src_a):
         target = (lax.rem(me + k, n), tp)
+        half = src_s.shape[0] // 2
+        pieces = (
+            (src_s.at[pl.ds(0, half)], got_s.at[slot, pl.ds(0, half)]),
+            (src_s.at[pl.ds(half, half)], got_s.at[slot, pl.ds(half, half)]),
+            (src_a, got_a.at[slot]),
+        )
         copies = [
             pltpu.make_async_remote_copy(
                 src_ref=src,
-                dst_ref=dst.at[slot],
+                dst_ref=dst,
                 send_sem=sems.at[part, 0, slot],
                 recv_sem=sems.at[part, 1, slot],
                 device_id=target,
                 device_id_type=pl.DeviceIdType.MESH,
             )
-            for part, (src, dst) in enumerate(((src_s, got_s), (src_a, got_a)))
+            for part, (src, dst) in enumerate(pieces)
         ]
         for copy in copies:
             copy.start()
@@ -178,7 +184,7 @@
             pltpu.VMEM((rounds,) + carry_decay.shape, jnp.float32),
             pltpu.VMEM((slots,) + local_state.shape, jnp.float32),
             pltpu.VMEM((slots,) + carry_decay.shape, jnp.float32),
-            pltpu.SemaphoreType.DMA((2, 2, slots)),
+            pltpu.SemaphoreType.DMA((3, 2, slots)),
         ],
         compiler_params=pltpu.CompilerParams(collective_id=0, has_side_effects=True),
     )(local_state, carry_decay)

time: 122 us -> 122 us (level)
  no operation moved by 1% of the time
where the time goes in v11:
time: 122 us; the launch traced here: 120 us
  Pallas kernels  74.5 us (61%)
  between operations  14.3 us (12%)
  other arithmetic  12.2 us (10%)
  matrix products  9.9 us (8%)
  local copies, waits for them, and re-layouts  8.41 us (7%)
    pallas_call x1, Pallas kernels, carry_scan(): pl.pallas_call(carry_scan_kernel, out_shape=jax.ShapeDtypeStruct(local_st...  47.1 us
    pallas_call x1, Pallas kernels, attend_sparse(): pl.pallas_call(lambda *refs: sparse_attention_kernel(slots, blocks_here,...  15.5 us
    pallas_call x1, Pallas kernels, tp_sum(): pl.pallas_call(tp_sum_kernel, out_shape=jax.ShapeDtypeStruct(shaped.shape...  12 us
    dot_general x1, matrix products, mamba_mix(): jnp.einsum('hts,shp->thp', decay * inner[None], weighted, precision=careful)  6.72 us
  transfers between devices with their start and end apart: 1, of which 1 were waited for; matrix products, arithmetic and copies ran while one was open for 24% of the time, Pallas kernels for 49%

profile of v11, /device:TPU:1, one launch (start us, length us, event | category | flops | bytes accessed | tf_op | source)
XLA Modules:
  0.0 120.0 jit_solution(6228863460051772940)
XLA Ops:
  7.2 0.0 copy-start
  7.2 0.0 copy-start.6
  7.2 0.0 all-gather.2.cloned.1.call-start
  7.2 1.5 %pad_maximum_fusion = bf16[2,256,128]{2,1,0:T(8,128)(2,1)} fusion(bf16[1,256,128]{2,1,0:T(8,128)(2,1)} %bitcast.62, bf16[1,256,128]{2,1,0:T(8,128)(2,1)} %bitcast.63), kind=kLoop, calls=%fused_computation.31 | loop fusion | flops 65536 | bytes 262144 | tf_op jit(solution)/shard_map/stack | solution.py:307
  8.8 0.0 all-gather.2.cloned.1.call-update
  8.8 0.7 exponential_negate_fusion
  9.5 0.8 copy_bitcast_fusion.1
  10.3 0.6 reduce-window.6
  10.9 0.2 slice_reduce_fusion
  11.1 1.5 %copy.34 = f32[256,2048]{0,1:T(8,128)S(1)} copy(bf16[256,2048]{1,0:T(8,128)(2,1)} %param.20) | data formatting | bytes 3145728 | tf_op jit(solution)/shard_map/reshape | solution.py:256
  12.6 0.1 copy_bitcast_fusion
  12.7 0.2 slice_reduce_fusion.1
  12.9 0.1 broadcast_in_dim.100
  12.9 0.7 broadcast_in_dim_reshape.3.a_ref
  13.6 0.0 copy-done
  13.6 0.0 copy-done.6
  13.6 0.2 convolution_bitcast_fusion
  13.8 0.1 copy.37
  14.0 0.1 bitcast_exponential_fusion
  14.1 0.0 copy-done.4
  14.1 0.3 multiply_multiply_fusion
  14.4 0.0 copy-start.11
  14.4 1.3 %fusion.26.s_ref = f32[16,2048]{1,0:T(8,128)} fusion(bf16[256,16]{0,1:T(8,128)(2,1)S(1)} %copy-done.6, f32[2048,256]{1,0:T(8,128)S(1)} %bitcast.56), kind=kOutput, calls=%fused_computation.56 | convolution fusion | flops 50331648 | bytes 2236416 | tf_op jit(solution)/shard_map/sn,shp->nhp/dot_general | solution.py:272
  15.7 47.1 %shard_map.150 = f32[16,2048]{1,0:T(8,128)} custom-call(f32[16,2048]{1,0:T(8,128)} %fusion.26.s_ref, f32[1,2048]{1,0:T(1,128)} %broadcast_in_dim_reshape.3.a_ref), custom_call_target="tpu_custom_call" | custom-call | tf_op jit(solution)/shard_map/pallas_call | solution.py:177
  62.9 1.7 %fusion.27 = f32[2048,256]{1,0:T(8,128)S(1)} fusion(f32[16,2048]{1,0:T(8,128)} %shard_map.150, bf16[256,16]{0,1:T(8,128)(2,1)S(1)} %copy-done), kind=kOutput, calls=%fused_computation.57 | convolution fusion | flops 50331648 | bytes 2236416 | tf_op jit(solution)/shard_map/dot_general | solution.py:279
  64.5 0.0 copy-done.11
  64.5 6.7 %fusion.15 = f32[256,32,64]{0,2,1:T(8,128)} fusion(f32[256,32,64]{0,2,1:T(8,128)S(1)} %bitcast.55, f32[256,32,64]{0,2,1:T(8,128)S(1)} %bitcast.57, f32[256,256]{1,0:T(8,128)S(1)} %copy.37, f32[32,256]{1,0:T(8,128)S(1)} %get-tuple-element.14, pred[256,256]{1,0:T(8,128)(4,1)S(1)} %iota_compare_fusion.1, f32[32]{0:T(128)S(1)} %copy-done.11, ...), kind=kOutput, calls=%fused_computation.18 | convolution fusion | flops 816316416 | bytes 6717568 | tf_op jit(solution)/shard_map/hts,shp->thp/dot_general | solution.py:270
  71.3 2.2 %copy.38 = f32[256,2048]{1,0:T(8,128)S(1)} copy(f32[256,2048]{0,1:T(8,128)} %bitcast.58) | data formatting | bytes 4194304 | tf_op jit(solution)/shard_map/reshape | solution.py:283
  73.5 0.0 copy-done.1
  73.5 0.0 copy-start.10
  73.5 0.0 copy-start.5
  73.5 0.0 copy-start.7
  73.5 0.0 copy-start.8
  73.5 0.7 multiply_reduce_fusion
  74.2 0.6 pad.4.x_ref
  74.8 12.0 %shard_map.151 = f32[8,128]{1,0:T(8,128)} custom-call(f32[8,128]{1,0:T(8,128)} %pad.4.x_ref), custom_call_target="tpu_custom_call" | custom-call | tf_op jit(solution)/shard_map/pallas_call | solution.py:237
  86.8 0.0 copy-done.10
  86.8 0.1 dynamic_slice.3
  86.9 0.0 copy-done.5
  86.9 0.0 copy-done.7
  86.9 0.1 broadcast_compare_fusion.2
  87.0 0.1 pad_add_fusion.1
  87.1 0.1 broadcast_subtract_fusion
  87.2 0.0 copy-start.2
  87.2 0.1 pad_add_fusion
  87.3 0.8 and_reduce_fusion
  88.1 0.1 sub.51
  88.2 0.1 pad.7.clone
  88.2 0.1 broadcast_compare_fusion.1
  88.3 0.1 add_and_fusion
  88.4 0.1 add_select_fusion
  88.5 0.2 broadcast_in_dim.96
  88.7 0.8 reshape.128.refs_3_
  89.4 0.1 pad.17.clone
  89.5 0.7 broadcast_in_dim.50
  90.3 0.8 add_add_fusion
  91.1 0.1 copy.32
  91.2 2.0 %select_reduce_fusion = s32[8,4,18]{0,2,1:T(8,128)S(1)} fusion(s32[8,4,18]{0,2,1:T(8,128)S(1)} %copy.32, s32[128]{0:T(128)} %param.19), kind=kLoop, calls=%fused_computation.26 | loop fusion | flops 220608 | bytes 5120 | tf_op jit(solution)/shard_map/reduce_sum | solution.py:44
  93.2 0.7 copy.33
  93.9 0.7 rsqrt_bitcast_fusion
  94.6 0.7 fusion.23.refs_4_
  95.4 1.7 %multiply_convert_fusion = bf16[256,2048]{1,0:T(8,128)(2,1)} fusion(f32[2048]{0:T(1024)S(1)} %copy-done.8, f32[256]{0:T(256)S(1)} %rsqrt_bitcast_fusion, f32[256,2048]{1,0:T(8,128)S(1)} %copy.38, bf16[256,2048]{1,0:T(8,128)(2,1)S(1)} %copy-done.1), kind=kLoop, calls=%fused_computation.19 | loop fusion | flops 4718592 | bytes 4203520 | tf_op jit(solution)/shard_map/convert_element_type | solution.py:288
  97.1 0.6 all-gather.2.cloned.1.call-done.refs_1_
  97.7 15.5 %shard_map.149 = bf16[256,1024]{1,0:T(8,128)(2,1)} custom-call(bf16[256,1024]{1,0:T(8,128)(2,1)} %refs_0_.1, bf16[2,8192,128]{2,1,0:T(8,128)(2,1)} %all-gather.2.cloned.1.call-done.refs_1_, s32[32,18]{1,0:T(8,128)} %bitcast.60, f32[32,1152]{1,0:T(8,128)} %reshape.128.refs_3_, f32[64,1152]{1,0:T(8,128)} %fusion.23.refs_4_), custom_call_target="tpu_custom_call" | custom-call | flops 1207959552 | bytes 5242880 | tf_op jit(solution)/shard_map/pallas_call | solution.py:90
  (19 shorter events, 0.1 us)
Async XLA Ops:
  7.2 6.4 %copy-start = (bf16[256,16]{0,1:T(8,128)(2,1)S(1)}, bf16[256,16]{0,1:T(8,128)(2,1)}, u32[]{:S(2)}) copy-start(bf16[256,16]{0,1:T(8,128)(2,1)} %param.23) | copy-start | bytes 24580
  7.2 6.4 %copy-start.6 = (bf16[256,16]{0,1:T(8,128)(2,1)S(1)}, bf16[256,16]{0,1:T(8,128)(2,1)}, u32[]{:S(2)}) copy-start(bf16[256,16]{0,1:T(8,128)(2,1)} %param.22) | copy-start | bytes 24580
  7.2 90.5 %all-gather.2.cloned.1.call-start = ((), (), s32[]{:S(2)}) async-start(), calls=%async_computation | async-start | bytes 4325376 | tf_op jit(solution)/shard_map/all_gather | solution.py:83
  11.1 3.0 %copy-start.4 = (f32[256,32]{0,1:T(8,128)S(1)}, f32[256,32]{0,1:T(8,128)}, u32[]{:S(2)}) copy-start(f32[256,32]{0,1:T(8,128)} %param.24) | copy-start | bytes 98308
  14.4 50.1 %copy-start.11 = (f32[32]{0:T(128)S(1)}, f32[32]{0:T(128)}, u32[]{:S(2)}) copy-start(f32[32]{0:T(128)} %param.26) | copy-start | bytes 388
  71.3 2.2 %copy-start.1 = (bf16[256,2048]{1,0:T(8,128)(2,1)S(1)}, bf16[256,2048]{1,0:T(8,128)(2,1)}, u32[]{:S(2)}) copy-start(bf16[256,2048]{1,0:T(8,128)(2,1)} %param.21) | copy-start | bytes 3145732
  73.5 13.4 %copy-start.10 = (s32[128]{0:T(128)S(1)}, s32[128]{0:T(128)}, u32[]{:S(2)}) copy-start(s32[128]{0:T(128)} %param.19) | copy-start | bytes 1540
  73.5 13.4 %copy-start.5 = (s32[8,8]{1,0:T(8,128)S(1)}, s32[8,8]{1,0:T(8,128)}, u32[]{:S(2)}) copy-start(s32[8,8]{1,0:T(8,128)} %param.18) | copy-start | bytes 772
  73.5 13.4 %copy-start.7 = (s32[8,8]{1,0:T(8,128)S(1)}, s32[8,8]{1,0:T(8,128)}, u32[]{:S(2)}) copy-start(s32[8,8]{1,0:T(8,128)} %param.17) | copy-start | bytes 772
  73.5 21.9 %copy-start.8 = (f32[2048]{0:T(1024)S(1)}, f32[2048]{0:T(1024)}, u32[]{:S(2)}) copy-start(f32[2048]{0:T(1024)} %param.27) | copy-start | bytes 24580
  86.9 1.1 copy-start.9
  87.2 0.9 copy-start.3
  87.2 1.2 %copy-start.2 = (s32[8,4,8]{2,1,0:T(4,128)}, s32[8,4,8]{2,1,0:T(4,128)S(1)}, u32[]{:S(2)}) copy-start(s32[8,4,8]{2,1,0:T(4,128)S(1)} %broadcast_in_dim.51) | copy-start | bytes 3076
Sparse Core Ops, SparseCore 0:
  11.2 86.4 all-gather.1

commit v12 on v9

--- a/solution.py
+++ b/solution.py
@@ -1,6 +1,7 @@
 import math
 
 import jax
+import numpy as np
 import jax.numpy as jnp
 from jax import lax
 from jax.experimental import pallas as pl
@@ -83,9 +84,9 @@
     kv_all = lax.all_gather(kv_local, "ctx", axis=1, tiled=True)
     index, col_bias, slots = key_block_table(vertical, slash, block_position, blocks_here)
     units = col_bias.shape[0]
-    r = lax.broadcasted_iota(jnp.int32, (BLOCK, slots * BLOCK), 0)
-    c = lax.broadcasted_iota(jnp.int32, (BLOCK, slots * BLOCK), 1)
-    causal_bias = jnp.where((c < BLOCK) & (c > r), NEG_FILL, 0.0).astype(jnp.float32)
+    r = np.arange(BLOCK)[:, None]
+    c = np.arange(slots * BLOCK)[None, :]
+    causal_bias = jnp.asarray(np.where((c < BLOCK) & (c > r), NEG_FILL, 0.0).astype(np.float32))
     flops = units * 4 * BLOCK * slots * BLOCK * HEAD_DIM
     return pl.pallas_call(
         lambda *refs: sparse_attention_kernel(slots, blocks_here, *refs),

time: 122 us -> 122 us (level)
  transfers between devices with their start and end apart: 1 -> 1, of which waited for: 1 -> 1; matrix products, arithmetic and copies ran while one was open for 24% -> 23% of each run, Pallas kernels for 49% -> 49%
where the time goes in v12:
time: 122 us; the launch traced here: 120 us
  Pallas kernels  74.4 us (61%)
  between operations  14.3 us (12%)
  other arithmetic  11.4 us (9%)
  matrix products  9.91 us (8%)
  local copies, waits for them, and re-layouts  8.38 us (7%)
  waiting for transfers between devices  1.59 us (1%)
    pallas_call x1, Pallas kernels, carry_scan(): pl.pallas_call(carry_scan_kernel, out_shape=jax.ShapeDtypeStruct(local_st...  46.8 us
    pallas_call x1, Pallas kernels, attend_sparse(): pl.pallas_call(lambda *refs: sparse_attention_kernel(slots, blocks_here,...  15.5 us
    pallas_call x1, Pallas kernels, tp_sum(): pl.pallas_call(tp_sum_kernel, out_shape=jax.ShapeDtypeStruct(shaped.shape...  12.2 us
    dot_general x1, matrix products, mamba_mix(): jnp.einsum('hts,shp->thp', decay * inner[None], weighted, precision=careful)  6.72 us
  transfers between devices with their start and end apart: 1, of which 1 were waited for; matrix products, arithmetic and copies ran while one was open for 23% of the time, Pallas kernels for 49%

profile of v12, /device:TPU:1, one launch (start us, length us, event | category | flops | bytes accessed | tf_op | source)
XLA Modules:
  0.0 120.1 jit_solution(202189270498506917)
XLA Ops:
  7.2 0.0 copy-start
  7.2 0.0 copy-start.6
  7.2 0.0 all-gather.2.cloned.1.call-start
  7.2 1.5 %pad_maximum_fusion = bf16[2,256,128]{2,1,0:T(8,128)(2,1)} fusion(bf16[1,256,128]{2,1,0:T(8,128)(2,1)} %bitcast.62, bf16[1,256,128]{2,1,0:T(8,128)(2,1)} %bitcast.63), kind=kLoop, calls=%fused_computation.28 | loop fusion | flops 65536 | bytes 262144 | tf_op jit(solution)/shard_map/stack | solution.py:302
  8.8 0.0 all-gather.2.cloned.1.call-update
  8.8 0.7 exponential_negate_fusion
  9.5 0.8 copy_bitcast_fusion.1
  10.3 0.6 reduce-window.6
  10.9 0.2 slice_reduce_fusion
  11.1 1.5 %copy.35 = f32[256,2048]{0,1:T(8,128)S(1)} copy(bf16[256,2048]{1,0:T(8,128)(2,1)} %param.21) | data formatting | bytes 3145728 | tf_op jit(solution)/shard_map/reshape | solution.py:251
  12.6 0.1 copy_bitcast_fusion
  12.7 0.2 slice_reduce_fusion.1
  12.9 0.1 broadcast_in_dim.90
  12.9 0.7 broadcast_in_dim_reshape.3.a_ref
  13.6 0.0 copy-done
  13.6 0.0 copy-done.6
  13.6 0.2 convolution_bitcast_fusion
  13.8 0.1 copy.38
  14.0 0.1 bitcast_exponential_fusion
  14.1 0.0 copy-done.4
  14.1 0.3 multiply_multiply_fusion
  14.4 0.0 copy-start.11
  14.4 1.3 %fusion.24.s_ref = f32[16,2048]{1,0:T(8,128)} fusion(bf16[256,16]{0,1:T(8,128)(2,1)S(1)} %copy-done.6, f32[2048,256]{1,0:T(8,128)S(1)} %bitcast.56), kind=kOutput, calls=%fused_computation.52 | convolution fusion | flops 50331648 | bytes 2236416 | tf_op jit(solution)/shard_map/sn,shp->nhp/dot_general | solution.py:267
  15.7 46.8 %shard_map.159 = f32[16,2048]{1,0:T(8,128)} custom-call(f32[16,2048]{1,0:T(8,128)} %fusion.24.s_ref, f32[1,2048]{1,0:T(1,128)} %broadcast_in_dim_reshape.3.a_ref), custom_call_target="tpu_custom_call" | custom-call | tf_op jit(solution)/shard_map/pallas_call | solution.py:172
  62.6 1.7 %fusion.25 = f32[2048,256]{1,0:T(8,128)S(1)} fusion(f32[16,2048]{1,0:T(8,128)} %shard_map.159, bf16[256,16]{0,1:T(8,128)(2,1)S(1)} %copy-done), kind=kOutput, calls=%fused_computation.53 | convolution fusion | flops 50331648 | bytes 2236416 | tf_op jit(solution)/shard_map/dot_general | solution.py:274
  64.2 0.0 copy-done.11
  64.2 6.7 %fusion.15 = f32[256,32,64]{0,2,1:T(8,128)} fusion(f32[256,32,64]{0,2,1:T(8,128)S(1)} %bitcast.55, f32[256,32,64]{0,2,1:T(8,128)S(1)} %bitcast.57, f32[256,256]{1,0:T(8,128)S(1)} %copy.38, f32[32,256]{1,0:T(8,128)S(1)} %get-tuple-element.14, pred[256,256]{1,0:T(8,128)(4,1)S(1)} %iota_compare_fusion, f32[32]{0:T(128)S(1)} %copy-done.11, ...), kind=kOutput, calls=%fused_computation.18 | convolution fusion | flops 816316416 | bytes 6717568 | tf_op jit(solution)/shard_map/hts,shp->thp/dot_general | solution.py:265
  71.0 2.2 %copy.39 = f32[256,2048]{1,0:T(8,128)S(1)} copy(f32[256,2048]{0,1:T(8,128)} %bitcast.58) | data formatting | bytes 4194304 | tf_op jit(solution)/shard_map/reshape | solution.py:278
  73.2 0.0 copy-done.1
  73.2 0.0 copy-start.10
  73.2 0.0 copy-start.5
  73.2 0.0 copy-start.7
  73.2 0.0 copy-start.8
  73.2 0.7 multiply_reduce_fusion
  73.9 0.6 pad.4.x_ref
  74.5 12.2 %shard_map.160 = f32[8,128]{1,0:T(8,128)} custom-call(f32[8,128]{1,0:T(8,128)} %pad.4.x_ref), custom_call_target="tpu_custom_call" | custom-call | tf_op jit(solution)/shard_map/pallas_call | solution.py:232
  86.7 0.0 copy-done.10
  86.7 0.1 dynamic_slice.3
  86.8 0.0 copy-done.5
  86.8 0.0 copy-done.7
  86.8 0.1 broadcast_compare_fusion.2
  86.9 0.1 pad_add_fusion.1
  87.0 0.1 broadcast_subtract_fusion
  87.1 0.0 copy-start.2
  87.1 0.1 pad_add_fusion
  87.2 0.8 and_reduce_fusion
  87.9 0.0 copy-done.3
  88.0 0.1 sub.51
  88.0 0.1 pad.7.clone
  88.1 0.1 broadcast_compare_fusion.1
  88.2 0.1 add_and_fusion
  88.3 0.1 add_select_fusion
  88.4 0.2 broadcast_in_dim.88
  88.5 0.8 reshape.128.refs_3_
  89.3 0.1 pad.17.clone
  89.4 0.7 broadcast_in_dim.38
  90.1 0.8 add_add_fusion
  91.0 0.1 copy.33
  91.1 2.0 %select_reduce_fusion = s32[8,4,18]{0,2,1:T(8,128)S(1)} fusion(s32[8,4,18]{0,2,1:T(8,128)S(1)} %copy.33, s32[128]{0:T(128)} %param.20), kind=kLoop, calls=%fused_computation.25 | loop fusion | flops 220608 | bytes 5120 | tf_op jit(solution)/shard_map/reduce_sum | solution.py:45
  93.1 0.7 copy.34
  93.8 0.7 rsqrt_bitcast_fusion
  94.5 1.7 %multiply_convert_fusion = bf16[256,2048]{1,0:T(8,128)(2,1)} fusion(f32[2048]{0:T(1024)S(1)} %copy-done.8, f32[256]{0:T(256)S(1)} %rsqrt_bitcast_fusion, f32[256,2048]{1,0:T(8,128)S(1)} %copy.39, bf16[256,2048]{1,0:T(8,128)(2,1)S(1)} %copy-done.1), kind=kLoop, calls=%fused_computation.19 | loop fusion | flops 4718592 | bytes 4203520 | tf_op jit(solution)/shard_map/convert_element_type | solution.py:283
  96.2 1.6 %all-gather.2.cloned.1.call-done.refs_1_ = bf16[2,8192,128]{2,1,0:T(8,128)(2,1)} async-done(((bf16[2,256,128]{2,1,0:T(8,128)(2,1)}), bf16[2,8192,128]{2,1,0:T(8,128)(2,1)}) %all-gather.2.cloned.1.call-update) | async-done | bytes 4194320 | tf_op jit(solution)/shard_map/all_gather | solution.py:84
  97.8 15.5 %shard_map.158 = bf16[256,1024]{1,0:T(8,128)(2,1)} custom-call(bf16[256,1024]{1,0:T(8,128)(2,1)} %refs_0_.1, bf16[2,8192,128]{2,1,0:T(8,128)(2,1)} %all-gather.2.cloned.1.call-done.refs_1_, s32[32,18]{1,0:T(8,128)} %bitcast.60, f32[32,1152]{1,0:T(8,128)} %reshape.128.refs_3_, f32[64,1152]{1,0:T(8,128)} %constant.37.clone.refs_4_), custom_call_target="tpu_custom_call" | custom-call | flops 1207959552 | bytes 5242880 | tf_op jit(solution)/shard_map/pallas_call | solution.py:91
  (17 shorter events, 0.1 us)
Async XLA Ops:
  7.2 6.4 %copy-start = (bf16[256,16]{0,1:T(8,128)(2,1)S(1)}, bf16[256,16]{0,1:T(8,128)(2,1)}, u32[]{:S(2)}) copy-start(bf16[256,16]{0,1:T(8,128)(2,1)} %param.24) | copy-start | bytes 24580
  7.2 6.4 %copy-start.6 = (bf16[256,16]{0,1:T(8,128)(2,1)S(1)}, bf16[256,16]{0,1:T(8,128)(2,1)}, u32[]{:S(2)}) copy-start(bf16[256,16]{0,1:T(8,128)(2,1)} %param.23) | copy-start | bytes 24580
  7.2 90.6 %all-gather.2.cloned.1.call-start = ((), (), s32[]{:S(2)}) async-start(), calls=%async_computation | async-start | bytes 4325376 | tf_op jit(solution)/shard_map/all_gather | solution.py:84
  11.1 3.0 %copy-start.4 = (f32[256,32]{0,1:T(8,128)S(1)}, f32[256,32]{0,1:T(8,128)}, u32[]{:S(2)}) copy-start(f32[256,32]{0,1:T(8,128)} %param.25) | copy-start | bytes 98308
  14.4 49.8 %copy-start.11 = (f32[32]{0:T(128)S(1)}, f32[32]{0:T(128)}, u32[]{:S(2)}) copy-start(f32[32]{0:T(128)} %param.27) | copy-start | bytes 388
  71.0 2.2 %copy-start.1 = (bf16[256,2048]{1,0:T(8,128)(2,1)S(1)}, bf16[256,2048]{1,0:T(8,128)(2,1)}, u32[]{:S(2)}) copy-start(bf16[256,2048]{1,0:T(8,128)(2,1)} %param.22) | copy-start | bytes 3145732
  73.2 13.5 %copy-start.10 = (s32[128]{0:T(128)S(1)}, s32[128]{0:T(128)}, u32[]{:S(2)}) copy-start(s32[128]{0:T(128)} %param.20) | copy-start | bytes 1540
  73.2 13.6 %copy-start.5 = (s32[8,8]{1,0:T(8,128)S(1)}, s32[8,8]{1,0:T(8,128)}, u32[]{:S(2)}) copy-start(s32[8,8]{1,0:T(8,128)} %param.19) | copy-start | bytes 772
  73.2 13.6 %copy-start.7 = (s32[8,8]{1,0:T(8,128)S(1)}, s32[8,8]{1,0:T(8,128)}, u32[]{:S(2)}) copy-start(s32[8,8]{1,0:T(8,128)} %param.18) | copy-start | bytes 772
  73.2 21.3 %copy-start.8 = (f32[2048]{0:T(1024)S(1)}, f32[2048]{0:T(1024)}, u32[]{:S(2)}) copy-start(f32[2048]{0:T(1024)} %param.28) | copy-start | bytes 24580
  86.8 1.1 copy-start.9
  87.1 0.9 copy-start.3
  87.1 1.2 %copy-start.2 = (s32[8,4,8]{2,1,0:T(4,128)}, s32[8,4,8]{2,1,0:T(4,128)S(1)}, u32[]{:S(2)}) copy-start(s32[8,4,8]{2,1,0:T(4,128)S(1)} %broadcast_in_dim.39) | copy-start | bytes 3076
Sparse Core Ops, SparseCore 0:
  11.2 86.5 all-gather.1
